TPU v7x, 512 devices: a whole 4x4x16 slice. The times are simulated.
512 devices in a mesh: row: 16 (over x, y), col: 32 (over z, core).
Axes of the slice: x: 4, y: 4, z: 16, core: 2. Of those that a mesh axis runs over, the one named last changes fastest.
Arguments:
- kron_inverse: float32 [9216, 9216], P('row', 'col'), may hold values from -1 to 13, as said below
- activations: float32 [2, 128, 9216], P(None, None, 'col'), may hold values from -0.125 to 0.125
Outputs:
- updated: float32 [9216, 9216], P('row', 'col')
- gain_blocks: float32 [2, 9216, 128], P(None, ('row', 'col'))
Inputs may be any that keep to these rules, and one draw needn't show every extreme that they name: `kron_inverse`: symmetric positive definite, with smallest eigenvalue at least 0.5.
All inputs are finite; a program needn't handle non-finite values.
Results may differ from a plain program's by a relative error of at most 0.0001.
Values sent between devices are 32-bit elements; how exact they have to be, the bound alone decides.
No kernel may reach another device: no remote copies, remote signals or barrier semaphores. Data moves between devices by JAX's collectives and lax.ppermute only.
A program may use at most 64 MiB of HBM per device.

v0:
```python
import jax
import jax.numpy as jnp
from jax import lax
from jax.sharding import PartitionSpec as P

highest = lax.Precision.HIGHEST


def rows_for(lines, size):
    spare = -lines.shape[0] % size
    if not spare:
        return lines
    return jnp.concatenate([lines, jnp.zeros((spare, *lines.shape[1:]), lines.dtype)])


def laid_out(blocks, dim):
    blocks = jnp.moveaxis(blocks, 0, dim)
    lengths = blocks.shape
    return blocks.reshape(*lengths[:dim], lengths[dim] * lengths[dim + 1], *lengths[dim + 2 :])


def copy_for_each(value, axis):
    size = lax.axis_size(axis)
    return lax.all_to_all(
        jnp.broadcast_to(value[None], (size, *value.shape)), axis, 0, 0, tiled=True
    )


def gather_directly(value, axis, dim):
    return laid_out(copy_for_each(value, axis), dim)


def in_blocks(value, dim, size):
    before, after = (value.shape[:dim], value.shape[dim + 1 :])
    return jnp.moveaxis(value.reshape(*before, size, -1, *after), dim, 0)


def sum_at_owner(value, axis, dim):
    size = lax.axis_size(axis)
    blocks = lax.all_to_all(in_blocks(value, dim, size), axis, 0, 0, tiled=True)
    return jnp.sum(blocks, axis=0)


def total_of(value, axes):
    lines = value.reshape(-1, value.shape[-1])
    padded = rows_for(lines, lax.axis_size(axes))
    whole = gather_directly(sum_at_owner(padded, axes, 0), axes, 0)
    return lax.slice_in_dim(whole, 0, len(lines)).reshape(value.shape)


def broadcast(value, axis, root):
    return lax.dynamic_index_in_dim(lax.all_gather(value, axis), root, 0, keepdims=False)


def shards(kron_inverse, activations):
    row_count, col_count = kron_inverse.shape
    blocks, width = (activations.shape[0], activations.shape[1])
    col_devices = lax.axis_size("col")
    col_index = lax.axis_index("col")
    first_row = col_index * col_count
    owner = first_row // row_count
    offset = first_row % row_count
    share = row_count // col_devices
    pieces = []
    stacked = activations.reshape(blocks * width, col_count)
    partial_value = jnp.dot(kron_inverse, stacked.T, precision=highest)
    row_terms = total_of(partial_value, "col")
    chosen = lax.dynamic_slice_in_dim(row_terms, offset, col_count, 0)
    col_terms = broadcast(chosen, "row", owner)
    small_term = jnp.dot(stacked, col_terms, precision=highest)
    system = jnp.eye(blocks * width, dtype=jnp.float32) + total_of(small_term, "col")
    factor = jnp.linalg.cholesky(system)
    row_scaled = jax.scipy.linalg.solve_triangular(factor, row_terms.T, lower=True).T
    col_scaled = jax.scipy.linalg.solve_triangular(factor, col_terms.T, lower=True).T
    updated = kron_inverse - jnp.dot(row_scaled, col_scaled.T, precision=highest)
    for number in range(blocks):
        lowest = number * width
        diag_block = factor[lowest : lowest + width, lowest : lowest + width]
        gain = jax.scipy.linalg.solve_triangular(
            diag_block, row_scaled[:, lowest : lowest + width].T, lower=True, trans="T"
        ).T
        pieces.append(lax.dynamic_slice_in_dim(gain, col_index * share, share, 0))
    return (updated, jnp.stack(pieces))


def solution(mesh):
    placed = (P("row", "col"), P(None, None, "col"))
    return jax.shard_map(
        shards,
        mesh=mesh,
        in_specs=placed,
        out_specs=(P("row", "col"), P(None, ("row", "col"), None)),
        check_vma=False,
    )
```

profile of v0, /device:TPU:1, one launch (start us, length us, event | category | flops | bytes accessed | tf_op | source)
XLA Modules:
  0.0 339.7 jit_solution(14047837843097152522)
XLA Ops:
  7.2 1.2 copy.14
  8.6 1.4 copy.13
  10.2 1.4 fusion.30
  11.5 61.2 %all_to_all.20 = f32[32,18,256]{2,1,0:T(8,128)S(1)} all-to-all(f32[32,18,256]{2,1,0:T(8,128)S(1)} %fusion.30), channel_id=1, replica_groups=mesh['row'=16,'col'=32] {'col'}, dimensions={0} | all-to-all | bytes 1179648 | tf_op jit(solution)/shard_map/all_to_all | solution.py:40
  72.8 0.9 broadcast_in_dim.5
  73.7 4.1 %all-to-all-start.1 = ((f32[32,18,256]{2,1,0:T(8,128)}), f32[32,18,256]{2,1,0:T(8,128)S(1)}, u32[]{:S(2)}, u32[]{:S(2)}) async-start(f32[32,18,256]{2,1,0:T(8,128)} %broadcast_in_dim.5), calls=%async_computation.1 | async-start | bytes 1572864 | tf_op jit(solution)/shard_map/all_to_all | solution.py:24
  77.9 44.6 %all-to-all-done.1 = f32[32,18,256]{2,1,0:T(8,128)S(1)} async-done(((f32[32,18,256]{2,1,0:T(8,128)}), f32[32,18,256]{2,1,0:T(8,128)S(1)}, u32[]{:S(2)}, u32[]{:S(2)}) %all-to-all-start.1) | async-done | bytes 589856 | tf_op jit(solution)/shard_map/all_to_all | solution.py:24
  122.5 0.7 constant_dynamic-slice_fusion.1
  123.3 60.5 %all-gather.3.cloned.1.call-done = f32[4608,256]{1,0:T(8,128)} async-done(((f32[288,256]{1,0:T(8,128)}), f32[4608,256]{1,0:T(8,128)}) %all-gather.3.cloned.1.call-update) | async-done | bytes 4718608 | tf_op jit(solution)/shard_map/all_gather | solution.py:52
  183.9 1.8 convolution_bitcast_fusion
  185.7 35.2 %all_to_all.21 = f32[32,8,256]{2,1,0:T(8,128)S(1)} all-to-all(f32[32,8,256]{2,1,0:T(8,128)S(1)} %convolution_bitcast_fusion), channel_id=1, replica_groups=mesh['row'=16,'col'=32] {'col'}, dimensions={0} | all-to-all | bytes 524288 | tf_op jit(solution)/shard_map/all_to_all | solution.py:40
  221.7 4.4 %all-to-all-start.3 = ((f32[32,8,256]{2,1,0:T(8,128)}), f32[32,8,256]{2,1,0:T(8,128)S(1)}, u32[]{:S(2)}, u32[]{:S(2)}) async-start(f32[32,8,256]{2,1,0:T(8,128)} %broadcast_in_dim.6), calls=%async_computation.3 | async-start | bytes 524288 | tf_op jit(solution)/shard_map/all_to_all | solution.py:24
  226.0 1.0 dynamic-slice_bitcast_fusion
  227.0 20.4 %all-to-all-done.3 = f32[32,8,256]{2,1,0:T(8,128)S(1)} async-done(((f32[32,8,256]{2,1,0:T(8,128)}), f32[32,8,256]{2,1,0:T(8,128)S(1)}, u32[]{:S(2)}, u32[]{:S(2)}) %all-to-all-start.3) | async-done | bytes 262176 | tf_op jit(solution)/shard_map/all_to_all | solution.py:24
  247.9 11.7 %cholesky.50 = f32[128,128]{1,0:T(8,128)S(1)} custom-call(f32[128,128]{1,0:T(8,128)S(1)} %cholesky.118), custom_call_target="Cholesky" | custom-call | tf_op jit(solution)/shard_map/jit(cholesky)/cholesky | solution.py:72
  259.6 9.8 %custom-call.21 = f32[1,128,128]{1,2,0:T(8,128)S(1)} custom-call(f32[1,128,128]{2,1,0:T(8,128)S(1)} %get-tuple-element.34), custom_call_target="InvertDiagBlocksLowerTriangular" | custom-call | tf_op jit(solution)/shard_map/jit(cholesky)/cholesky | solution.py:72
  269.9 11.7 %cholesky.105 = f32[128,128]{1,0:T(8,128)S(1)} custom-call(f32[128,128]{1,0:T(8,128)S(1)} %convolution_subtract_fusion.3), custom_call_target="Cholesky" | custom-call | tf_op jit(solution)/shard_map/jit(cholesky)/cholesky | solution.py:72
  283.8 10.0 %custom-call.24 = f32[1,128,128]{1,2,0:T(8,128)S(1)} custom-call(f32[1,128,128]{2,1,0:T(8,128)S(1)} %get-tuple-element.29), custom_call_target="InvertDiagBlocksLowerTriangular" | custom-call | tf_op jit(solution)/shard_map/jit(_solve_triangular)/triangular_solve | solution.py:79
  293.9 4.1 %while.1 = (s32[]{:T(128)}, f32[256,256]{1,0:T(8,128)S(1)}, s32[2,2]{1,0:T(2,128)S(1)}, f32[2,128,128]{2,1,0:T(8,128)S(1)}, s32[]{:T(128)}) while((s32[]{:T(128)}, f32[256,256]{1,0:T(8,128)S(1)}, s32[2,2]{1,0:T(2,128)S(1)}, f32[2,128,128]{2,1,0:T(8,128)S(1)}, s32[]{:T(128)}) %tuple.33), condition=%wide.while_cond, body=%wide.while_body.sunk | while | flops 2 | bytes 131189 | solution.py:73
  294.5 1.4 bitcast_dynamic-update-slice_fusion.2
  296.5 1.4 bitcast_dynamic-update-slice_fusion.2
  298.0 19.7 %custom-call.22 = f32[2,128,128]{1,2,0:T(8,128)S(1)} custom-call(f32[2,128,128]{2,1,0:T(8,128)S(1)} %get-tuple-element.10), custom_call_target="InvertDiagBlocksLowerTriangular" | custom-call | tf_op jit(solution)/shard_map/jit(_solve_triangular)/triangular_solve | solution.py:73
  317.7 9.8 %custom-call.25 = f32[1,128,128]{1,2,0:T(8,128)S(1)} custom-call(f32[1,128,128]{2,1,0:T(8,128)S(1)} %get-tuple-element.30), custom_call_target="InvertDiagBlocksLowerTriangular" | custom-call | tf_op jit(solution)/shard_map/jit(_solve_triangular)/triangular_solve | solution.py:79
  329.6 1.7 convolution_subtract_fusion
  (45 shorter events, 7.8 us)
Async XLA Ops:
  10.2 173.7 %copy-start.1 = (f32[2,128,288]{1,2,0:T(8,128)S(1)}, f32[2,128,288]{1,2,0:T(8,128)}, u32[]{:S(2)}) copy-start(f32[2,128,288]{1,2,0:T(8,128)} %param.5) | copy-start | bytes 884740
  73.7 48.8 %all-to-all-start.1 = ((f32[32,18,256]{2,1,0:T(8,128)}), f32[32,18,256]{2,1,0:T(8,128)S(1)}, u32[]{:S(2)}, u32[]{:S(2)}) async-start(f32[32,18,256]{2,1,0:T(8,128)} %broadcast_in_dim.5), calls=%async_computation.1 | async-start | bytes 1572864 | tf_op jit(solution)/shard_map/all_to_all | solution.py:24
  77.8 106.1 %all-gather.3.cloned.1.call-start = ((), (), s32[]{:S(2)}) async-start(), calls=%async_computation.4 | async-start | bytes 5013504 | tf_op jit(solution)/shard_map/all_gather | solution.py:52
  221.7 25.8 %all-to-all-start.3 = ((f32[32,8,256]{2,1,0:T(8,128)}), f32[32,8,256]{2,1,0:T(8,128)S(1)}, u32[]{:S(2)}, u32[]{:S(2)}) async-start(f32[32,8,256]{2,1,0:T(8,128)} %broadcast_in_dim.6), calls=%async_computation.3 | async-start | bytes 524288 | tf_op jit(solution)/shard_map/all_to_all | solution.py:24
  247.6 82.0 %copy-start = (f32[576,288]{0,1:T(8,128)S(1)}, f32[576,288]{0,1:T(8,128)}, u32[]{:S(2)}) copy-start(f32[576,288]{0,1:T(8,128)} %param.4) | copy-start | bytes 1990660
Sparse Core Ops, SparseCore 0:
  123.4 60.3 all-gather.2
where the time goes:
time: 340 us
  waiting for transfers between devices  126 us (37%)
  blocking collectives  96.4 us (28%)
  other arithmetic  73.8 us (22%)
  between operations  15.7 us (5%)
  local copies, waits for them, and re-layouts  11.5 us (3%)
  starting transfers between devices  8.48 us (2%)
  matrix products  8.17 us (2%)
    all_to_all x2, blocking collectives, sum_at_owner(): blocks = lax.all_to_all(in_blocks(value, dim, size), axis, 0, 0, tiled=True)  96.4 us
    all_to_all x2, waiting for transfers between devices, copy_for_each(): lax.all_to_all(jnp.broadcast_to(value[None], (size, *value.shape)), axis,...  65.1 us
    all_gather x1, waiting for transfers between devices, broadcast(): lax.all_gather(value, axis)  60.5 us
    another operation x6, other arithmetic, shards(): factor = jnp.linalg.cholesky(system)  34 us
    another operation x3, other arithmetic, shards(): jax.scipy.linalg.solve_triangular(diag_block, row_scaled[:, lowest:lowest...  19.8 us
    another operation x3, other arithmetic, shards(): jax.scipy.linalg.solve_triangular(factor, row_terms.T, lower=True)  19.7 us
    all_to_all x2, starting transfers between devices, copy_for_each(): lax.all_to_all(jnp.broadcast_to(value[None], (size, *value.shape)), axis,...  8.43 us
  transfers between devices with their start and end apart: 3, of which 3 were waited for; matrix products, arithmetic and copies ran while one was open for 0% of the time, Pallas kernels for 0%

commit v1 on v0

v1 whole, which is shorter than its diff:
```python
import jax
import jax.numpy as jnp
from jax import lax
from jax.sharding import PartitionSpec as P

highest = lax.Precision.HIGHEST


def dot(a, b):
    return jnp.dot(a, b, precision=highest)


def shards(kron_inverse, activations):
    rows, cols = kron_inverse.shape
    blocks, width = activations.shape[:2]
    wide = blocks * width
    planes = lax.axis_size("row")
    devices = lax.axis_size("col")
    depth = devices // 2
    row = lax.axis_index("row")
    col = lax.axis_index("col")
    lines = [[2 * z + k for z in range(depth)] for k in range(2)]
    pairs = [[2 * z, 2 * z + 1] for z in range(depth)]

    def over_core(value):
        return lax.all_to_all(value, "col", 0, 0, tiled=True, axis_index_groups=pairs)

    def over_z(value):
        return lax.all_to_all(value, "col", 0, 0, tiled=True, axis_index_groups=lines)

    def over_plane(value):
        return lax.all_to_all(value, "row", 0, 0, tiled=True)

    def copies(value, count):
        return jnp.broadcast_to(value[None], (count, *value.shape))

    half = rows // 2
    share = half // depth
    slab = wide // planes
    spare = -slab * share % wide
    extra = (slab * share + spare) // wide
    stacked = activations.reshape(wide, cols)
    partial = dot(kron_inverse, stacked.T)
    summed = jnp.sum(over_core(partial.reshape(2, half, wide)), axis=0)
    mine = lax.dynamic_slice_in_dim(stacked, row * slab, slab, 0)
    mine = mine.reshape(slab, depth, share).transpose(1, 0, 2).reshape(depth, slab * share)
    mine = jnp.pad(mine, ((0, 0), (0, spare))).reshape(depth, extra, wide)
    got = over_z(jnp.concatenate([summed.reshape(depth, share, wide), mine], axis=1))
    piece = jnp.sum(got[:, :share], axis=0)
    theirs = got[:, share:].reshape(depth, slab * share + spare)[:, : slab * share]
    theirs = theirs.reshape(depth, slab, share).transpose(1, 0, 2).reshape(slab, depth * share)
    level = over_plane(copies(piece, planes))
    small = dot(theirs, level.reshape(planes * share, wide))
    small = jnp.sum(over_core(small.reshape(2, slab // 2, wide)), axis=0)
    small = jnp.sum(over_z(copies(small, depth)), axis=0)
    terms = over_z(jnp.concatenate([copies(piece, depth), level], axis=1))
    small = over_core(copies(over_plane(copies(small, planes)), 2))
    system = jnp.eye(wide, dtype=jnp.float32) + small.transpose(1, 0, 2, 3).reshape(wide, wide)
    factor = jnp.linalg.cholesky(system)
    inverse = jax.scipy.linalg.solve_triangular(factor, jnp.eye(wide, dtype=jnp.float32), lower=True)
    row_half = terms[:, :share].reshape(half, wide)
    col_terms = terms[:, share:].reshape(half, wide)
    row_terms = over_core(copies(row_half, 2)).reshape(rows, wide)
    row_scaled = dot(row_terms, inverse.T)
    col_scaled = dot(col_terms, inverse.T)
    updated = kron_inverse - dot(row_scaled, col_scaled.T)
    own = rows // devices
    scaled = lax.dynamic_slice_in_dim(row_scaled, col * own, own, 0)
    gains = [
        dot(scaled[:, at : at + width], inverse[at : at + width, at : at + width])
        for at in range(0, wide, width)
    ]
    return updated, jnp.stack(gains)


def solution(mesh):
    return jax.shard_map(
        shards,
        mesh=mesh,
        in_specs=(P("row", "col"), P(None, None, "col")),
        out_specs=(P("row", "col"), P(None, ("row", "col"), None)),
        check_vma=False,
    )
```

time: 340 us -> 185 us (0.54)
  waiting for transfers between devices: 126 us -> 25.3 us
  blocking collectives: 96.4 us -> 51.9 us
  starting transfers between devices: 8.48 us -> 30.8 us
  other arithmetic: 73.8 us -> 56.1 us
  between operations: 15.7 us -> 2.3 us
    all_gather x1 -> x0, waiting for transfers between devices: 60.5 us -> none  [broadcast(): lax.all_gather(value, axis)]
    all_to_all x2 -> x4, blocking collectives: 96.4 us -> 51.9 us  [the longest x1 26.9 us: over_z(): lax.all_to_all(value, 'col', 0, 0, tiled=True, axis_index_groups=lines)]
    all_to_all x2 -> x5, waiting for transfers between devices: 65.1 us -> 25.3 us  [the longest x2 12.4 us: over_plane(): return lax.all_to_all(value, 'row', 0, 0, tiled=True)]
    all_to_all x2 -> x5, starting transfers between devices: 8.43 us -> 30.8 us  [the longest x1 10.3 us: over_core(): lax.all_to_all(value, 'col', 0, 0, tiled=True, axis_index_groups=pairs)]
    another operation x7 -> x4, other arithmetic: 39.5 us -> 19.9 us  [the longest x3 19.9 us: shards(): jax.scipy.linalg.solve_triangular(factor, jnp.eye(wide, dtype=jnp.float32...]
  transfers between devices with their start and end apart: 3 -> 5, of which waited for: 3 -> 4; matrix products, arithmetic and copies ran while one was open for 0% -> 34% of each run, Pallas kernels for 0% -> 0%
where the time goes in v1:
time: 185 us; the launch traced here: 184 us
  other arithmetic  56.1 us (30%)
  blocking collectives  51.9 us (28%)
  starting transfers between devices  30.8 us (17%)
  waiting for transfers between devices  25.3 us (14%)
  local copies, waits for them, and re-layouts  10.8 us (6%)
  matrix products  6.75 us (4%)
  between operations  2.3 us (1%)
    another operation x6, other arithmetic, shards(): factor = jnp.linalg.cholesky(system)  34 us
    all_to_all x1, blocking collectives, over_z(): lax.all_to_all(value, 'col', 0, 0, tiled=True, axis_index_groups=lines)  26.9 us
    all_to_all x3, blocking collectives, over_core(): lax.all_to_all(value, 'col', 0, 0, tiled=True, axis_index_groups=pairs)  25 us
    another operation x3, other arithmetic, shards(): jax.scipy.linalg.solve_triangular(factor, jnp.eye(wide, dtype=jnp.float32...  19.9 us
    all_to_all x2, waiting for transfers between devices, over_plane(): return lax.all_to_all(value, 'row', 0, 0, tiled=True)  12.4 us
    all_to_all x2, waiting for transfers between devices, over_z(): lax.all_to_all(value, 'col', 0, 0, tiled=True, axis_index_groups=lines)  12 us
    all_to_all x1, starting transfers between devices, over_core(): lax.all_to_all(value, 'col', 0, 0, tiled=True, axis_index_groups=pairs)  10.3 us
    all_to_all x2, starting transfers between devices, over_plane(): return lax.all_to_all(value, 'row', 0, 0, tiled=True)  10.3 us
  transfers between devices with their start and end apart: 5, of which 4 were waited for; matrix products, arithmetic and copies ran while one was open for 34% of the time, Pallas kernels for 0%

profile of v1, /device:TPU:1, one launch (start us, length us, event | category | flops | bytes accessed | tf_op | source)
XLA Modules:
  0.0 183.9 jit_solution(10280956646499200506)
XLA Ops:
  0.6 1.5 copy.36
  2.6 1.9 %fusion.20 = f32[2,288,256]{2,1,0:T(8,128)} fusion(f32[2,288,288]{2,1,0:T(8,128)S(1)} %bitcast.59, f32[256,288,1]{0,1,2:T(8,128)S(1)} %reshape.97), kind=kOutput, calls=%fused_computation.51 | convolution fusion | flops 509607936 | bytes 1548288 | tf_op jit(solution)/shard_map/dot_general | solution.py:10
  4.5 10.3 %all-to-all-start = ((f32[2,288,256]{2,1,0:T(8,128)}), f32[2,288,256]{2,1,0:T(8,128)S(1)}, u32[]{:S(2)}, u32[]{:S(2)}) async-start(f32[2,288,256]{2,1,0:T(8,128)} %fusion.20), calls=%async_computation | async-start | bytes 1179648 | tf_op jit(solution)/shard_map/all_to_all | solution.py:26
  15.4 0.9 all-to-all-done
  16.4 26.9 %all_to_all.45 = f32[16,20,256]{2,1,0:T(8,128)S(1)} all-to-all(f32[16,20,256]{2,1,0:T(8,128)S(1)} %pad_maximum_fusion.1), channel_id=1, replica_groups={{0,2,4,6,8,10,12,14,16,18,20,22,24,26,28,30},{1,3,5,7,9,11,13,15,17,19,..., dimensions={0} | all-to-all | bytes 655360 | tf_op jit(solution)/shard_map/all_to_all | solution.py:29
  44.0 6.8 %all-to-all-start.2 = ((f32[16,18,256]{2,1,0:T(8,128)}), f32[16,18,256]{2,1,0:T(8,128)S(1)}, u32[]{:S(2)}, u32[]{:S(2)}) async-start(f32[16,18,256]{2,1,0:T(8,128)} %broadcast_in_dim.13), calls=%async_computation.2 | async-start | bytes 786432 | tf_op jit(solution)/shard_map/all_to_all | solution.py:32
  51.1 7.7 %all-to-all-done.2 = f32[16,18,256]{2,1,0:T(8,128)S(1)} async-done(((f32[16,18,256]{2,1,0:T(8,128)}), f32[16,18,256]{2,1,0:T(8,128)S(1)}, u32[]{:S(2)}, u32[]{:S(2)}) %all-to-all-start.2) | async-done | bytes 294944 | tf_op jit(solution)/shard_map/all_to_all | solution.py:32
  59.0 12.3 %all_to_all.46 = f32[2,8,256]{2,1,0:T(8,128)S(1)} all-to-all(f32[2,8,256]{2,1,0:T(8,128)S(1)} %fusion.21), channel_id=1, replica_groups={{0,1},{2,3},{4,5},{6,7},{8,9},{10,11},{12,13},{14,15},{16,17},{18,19},{..., dimensions={0} | all-to-all | bytes 32768 | tf_op jit(solution)/shard_map/all_to_all | solution.py:26
  72.0 6.4 %all-to-all-start.6 = ((f32[16,8,256]{2,1,0:T(8,128)}), f32[16,8,256]{2,1,0:T(8,128)S(1)}, u32[]{:S(2)}, u32[]{:S(2)}) async-start(f32[16,8,256]{2,1,0:T(8,128)} %broadcast_in_dim.16), calls=%async_computation.6 | async-start | bytes 262144 | tf_op jit(solution)/shard_map/all_to_all | solution.py:29
  78.4 12.0 %all-to-all-done.6 = f32[16,8,256]{2,1,0:T(8,128)S(1)} async-done(((f32[16,8,256]{2,1,0:T(8,128)}), f32[16,8,256]{2,1,0:T(8,128)S(1)}, u32[]{:S(2)}, u32[]{:S(2)}) %all-to-all-start.6) | async-done | bytes 131104 | tf_op jit(solution)/shard_map/all_to_all | solution.py:29
  91.1 3.5 %all-to-all-start.7 = ((f32[16,8,256]{2,1,0:T(8,128)}), f32[16,8,256]{2,1,0:T(8,128)S(1)}, u32[]{:S(2)}, u32[]{:S(2)}) async-start(f32[16,8,256]{2,1,0:T(8,128)} %broadcast_in_dim.17), calls=%async_computation.7 | async-start | bytes 262144 | tf_op jit(solution)/shard_map/all_to_all | solution.py:32
  94.7 1.9 %pad_maximum_fusion = f32[16,36,256]{2,1,0:T(8,128)} fusion(f32[16,18,256]{2,1,0:T(8,128)S(1)} %all-to-all-done.2, f32[16,18,256]{2,1,0:T(8,128)} %broadcast_in_dim.13), kind=kLoop, calls=%fused_computation.7 | loop fusion | flops 147456 | bytes 1179648 | tf_op jit(solution)/shard_map/concatenate | solution.py:56
  96.6 4.7 %all-to-all-done.7 = f32[16,8,256]{2,1,0:T(8,128)S(1)} async-done(((f32[16,8,256]{2,1,0:T(8,128)}), f32[16,8,256]{2,1,0:T(8,128)S(1)}, u32[]{:S(2)}, u32[]{:S(2)}) %all-to-all-start.7) | async-done | bytes 131104 | tf_op jit(solution)/shard_map/all_to_all | solution.py:32
  101.3 8.3 %all_to_all.47 = f32[2,16,8,256]{3,2,1,0:T(8,128)S(1)} all-to-all(f32[2,16,8,256]{3,2,1,0:T(8,128)S(1)} %broadcast_in_dim.18), channel_id=1, replica_groups={{0,1},{2,3},{4,5},{6,7},{8,9},{10,11},{12,13},{14,15},{16,17},{18,19},{..., dimensions={0} | all-to-all | bytes 524288 | tf_op jit(solution)/shard_map/all_to_all | solution.py:26
  109.6 3.8 %all-to-all-start.3 = ((f32[16,36,256]{2,1,0:T(8,128)}), f32[16,36,256]{2,1,0:T(8,128)S(1)}, u32[]{:S(2)}, u32[]{:S(2)}) async-start(f32[16,36,256]{2,1,0:T(8,128)} %pad_maximum_fusion), calls=%async_computation.3 | async-start | bytes 1310720 | tf_op jit(solution)/shard_map/all_to_all | solution.py:29
  113.8 11.7 %cholesky.50 = f32[128,128]{1,0:T(8,128)S(1)} custom-call(f32[128,128]{1,0:T(8,128)S(1)} %cholesky.118), custom_call_target="Cholesky" | custom-call | tf_op jit(solution)/shard_map/jit(cholesky)/cholesky | solution.py:59
  125.6 9.8 %custom-call.15 = f32[1,128,128]{1,2,0:T(8,128)S(1)} custom-call(f32[1,128,128]{2,1,0:T(8,128)S(1)} %get-tuple-element.33), custom_call_target="InvertDiagBlocksLowerTriangular" | custom-call | tf_op jit(solution)/shard_map/jit(cholesky)/cholesky | solution.py:59
  135.9 11.7 %cholesky.105 = f32[128,128]{1,0:T(8,128)S(1)} custom-call(f32[128,128]{1,0:T(8,128)S(1)} %convolution_subtract_fusion.2), custom_call_target="Cholesky" | custom-call | tf_op jit(solution)/shard_map/jit(cholesky)/cholesky | solution.py:59
  149.7 4.1 %while.1 = (s32[]{:T(128)}, f32[256,256]{1,0:T(8,128)S(1)}, s32[2,2]{1,0:T(2,128)S(1)}, f32[2,128,128]{2,1,0:T(8,128)S(1)}, s32[]{:T(128)}) while((s32[]{:T(128)}, f32[256,256]{1,0:T(8,128)S(1)}, s32[2,2]{1,0:T(2,128)S(1)}, f32[2,128,128]{2,1,0:T(8,128)S(1)}, s32[]{:T(128)}) %tuple.32), condition=%wide.while_cond, body=%wide.while_body.sunk | while | flops 2 | bytes 131181 | solution.py:60
  150.4 1.3 bitcast_dynamic-update-slice_fusion.2
  152.4 1.3 bitcast_dynamic-update-slice_fusion.2
  153.8 19.9 %custom-call.16 = f32[2,128,128]{1,2,0:T(8,128)S(1)} custom-call(f32[2,128,128]{2,1,0:T(8,128)S(1)} %get-tuple-element.9), custom_call_target="InvertDiagBlocksLowerTriangular" | custom-call | tf_op jit(solution)/shard_map/jit(_solve_triangular)/triangular_solve | solution.py:60
  174.9 4.5 %all_to_all.48 = f32[2,288,256]{2,1,0:T(8,128)S(1)} all-to-all(f32[2,288,256]{2,1,0:T(8,128)S(1)} %broadcast_in_dim.15), channel_id=1, replica_groups={{0,1},{2,3},{4,5},{6,7},{8,9},{10,11},{12,13},{14,15},{16,17},{18,19},{..., dimensions={0} | all-to-all | bytes 1179648 | tf_op jit(solution)/shard_map/all_to_all | solution.py:26
  182.2 1.7 convolution_subtract_fusion
  (68 shorter events, 10.8 us)
Async XLA Ops:
  0.6 1.5 copy-start.1
  4.5 11.7 %all-to-all-start = ((f32[2,288,256]{2,1,0:T(8,128)}), f32[2,288,256]{2,1,0:T(8,128)S(1)}, u32[]{:S(2)}, u32[]{:S(2)}) async-start(f32[2,288,256]{2,1,0:T(8,128)} %fusion.20), calls=%async_computation | async-start | bytes 1179648 | tf_op jit(solution)/shard_map/all_to_all | solution.py:26
  44.0 14.7 %all-to-all-start.2 = ((f32[16,18,256]{2,1,0:T(8,128)}), f32[16,18,256]{2,1,0:T(8,128)S(1)}, u32[]{:S(2)}, u32[]{:S(2)}) async-start(f32[16,18,256]{2,1,0:T(8,128)} %broadcast_in_dim.13), calls=%async_computation.2 | async-start | bytes 786432 | tf_op jit(solution)/shard_map/all_to_all | solution.py:32
  72.0 18.5 %all-to-all-start.6 = ((f32[16,8,256]{2,1,0:T(8,128)}), f32[16,8,256]{2,1,0:T(8,128)S(1)}, u32[]{:S(2)}, u32[]{:S(2)}) async-start(f32[16,8,256]{2,1,0:T(8,128)} %broadcast_in_dim.16), calls=%async_computation.6 | async-start | bytes 262144 | tf_op jit(solution)/shard_map/all_to_all | solution.py:29
  91.1 10.1 %all-to-all-start.7 = ((f32[16,8,256]{2,1,0:T(8,128)}), f32[16,8,256]{2,1,0:T(8,128)S(1)}, u32[]{:S(2)}, u32[]{:S(2)}) async-start(f32[16,8,256]{2,1,0:T(8,128)} %broadcast_in_dim.17), calls=%async_computation.7 | async-start | bytes 262144 | tf_op jit(solution)/shard_map/all_to_all | solution.py:32
  109.6 65.1 %all-to-all-start.3 = ((f32[16,36,256]{2,1,0:T(8,128)}), f32[16,36,256]{2,1,0:T(8,128)S(1)}, u32[]{:S(2)}, u32[]{:S(2)}) async-start(f32[16,36,256]{2,1,0:T(8,128)} %pad_maximum_fusion), calls=%async_computation.3 | async-start | bytes 1310720 | tf_op jit(solution)/shard_map/all_to_all | solution.py:29
  181.1 1.1 copy-start

commit v2 on v1

v2 whole, which is shorter than its diff:
```python
import jax
import jax.numpy as jnp
from jax import lax
from jax.experimental import pallas as pl
from jax.experimental.pallas import tpu as pltpu
from jax.sharding import PartitionSpec as P

highest = lax.Precision.HIGHEST
f32 = jnp.float32


def dot(a, b, dims=((1,), (0,))):
    return lax.dot_general(a, b, (dims, ((), ())), precision=highest, preferred_element_type=f32)


def rough(a, b):
    return jnp.dot(a.astype(jnp.bfloat16), b.astype(jnp.bfloat16), preferred_element_type=f32)


def unit(size):
    rows = lax.broadcasted_iota(jnp.int32, (size, size), 0)
    return (rows == lax.broadcasted_iota(jnp.int32, (size, size), 1)).astype(f32)


def invert(block, out_ref, work_ref):
    size = block.shape[0]
    eye = unit(size)
    scale_col = lax.rsqrt(jnp.sum(block * eye, axis=1, keepdims=True))
    scale_row = lax.rsqrt(jnp.sum(block * eye, axis=0, keepdims=True))
    scaled = block * scale_col * scale_row
    off = scaled - eye
    step = jnp.minimum(1.0, 1.9 / (1.0 + jnp.sqrt(jnp.sum(off * off))))
    rest = eye - step * scaled
    guess = eye + rest
    rest = rough(rest, rest)
    for turn in range(3):
        more = rough(guess, rest)
        if turn < 2:
            rest = rough(rest, rest)
        guess = guess + more
    guess = guess * step
    rest = eye - dot(guess, scaled)
    out_ref[...] = guess + rough(rest, guess)
    miss = jnp.sum(rest * rest)

    @pl.when(jnp.logical_not(miss < 1e-2))
    def _():
        work_ref[...] = scaled
        lane = lax.broadcasted_iota(jnp.int32, (1, size), 1)
        line = lax.broadcasted_iota(jnp.int32, (size, 1), 0)

        def sweep(at, carry):
            value = work_ref[...]
            row = work_ref[pl.ds(at, 1), :]
            here = lane == at
            col = jnp.sum(jnp.where(here, value, 0.0), axis=1, keepdims=True)
            pivot = 1.0 / jnp.sum(jnp.where(here, row, 0.0), axis=1, keepdims=True)
            row = jnp.where(here, pivot, row * pivot)
            col = jnp.where(line == at, 0.0, col)
            value = jnp.where(here, 0.0, value)
            work_ref[...] = jnp.where(line == at, row, value - col * row)
            return carry

        lax.fori_loop(0, size, sweep, 0)
        out_ref[...] = work_ref[...]

    guess = out_ref[...]
    rest = eye - dot(guess, scaled)
    out_ref[...] = (guess + rough(rest, guess)) * scale_col * scale_row


def small_kernel(terms_ref, whole_ref, gain_ref, first_ref, last_ref, work_ref):
    wide = terms_ref.shape[0]
    width = wide // 2
    eye = unit(width)
    invert(terms_ref[:width, :width] + eye, first_ref, work_ref)
    first = first_ref[...]
    cross = terms_ref[:width, width:]
    carry = dot(first, cross)
    invert(terms_ref[width:, width:] + eye - dot(cross, carry, ((0,), (0,))), last_ref, work_ref)
    last = last_ref[...]
    corner = dot(carry, last)
    whole_ref[:width, :width] = first + dot(corner, carry, ((1,), (1,)))
    whole_ref[:width, width:] = -corner
    whole_ref[width:, :width] = -corner.T
    whole_ref[width:, width:] = last
    gain_ref[:width, :width] = first
    gain_ref[:width, width:] = -corner
    gain_ref[width:, :width] = jnp.zeros((width, width), f32)
    gain_ref[width:, width:] = last


def small_inverse(terms):
    wide = terms.shape[0]
    return pl.pallas_call(
        small_kernel,
        out_shape=[jax.ShapeDtypeStruct((wide, wide), f32)] * 2,
        scratch_shapes=[pltpu.VMEM((wide // 2, wide // 2), f32)] * 3,
    )(terms)


def shards(kron_inverse, activations):
    rows, cols = kron_inverse.shape
    blocks, width = activations.shape[:2]
    wide = blocks * width
    planes = lax.axis_size("row")
    devices = lax.axis_size("col")
    depth = devices // 2
    row = lax.axis_index("row")
    col = lax.axis_index("col")
    lines = [[2 * z + k for z in range(depth)] for k in range(2)]
    pairs = [[2 * z, 2 * z + 1] for z in range(depth)]

    def over_core(value):
        return lax.all_to_all(value, "col", 0, 0, tiled=True, axis_index_groups=pairs)

    def over_z(value):
        return lax.all_to_all(value, "col", 0, 0, tiled=True, axis_index_groups=lines)

    def over_plane(value):
        return lax.all_to_all(value, "row", 0, 0, tiled=True)

    def copies(value, count):
        return jnp.broadcast_to(value[None], (count, *value.shape))

    half = rows // 2
    share = half // depth
    slab = wide // planes

    def whole(value):
        left = value[:, :share].reshape(half, width)
        return jnp.concatenate([left, value[:, share:].reshape(half, width)], axis=1)

    spare = -slab * share % (4 * width)
    stacked = activations.reshape(wide, cols)
    partial = dot(kron_inverse, stacked.T)
    summed = jnp.sum(over_core(partial.reshape(2, half, wide)), axis=0)
    mine = lax.dynamic_slice_in_dim(stacked, row * slab, slab, 0)
    mine = mine.reshape(slab, depth, share).transpose(1, 0, 2).reshape(depth, slab * share)
    mine = jnp.pad(mine, ((0, 0), (0, spare))).reshape(depth, -1, width)
    parts = [summed[:, at : at + width].reshape(depth, share, width) for at in range(0, wide, width)]
    got = over_z(jnp.concatenate([*parts, mine], axis=1))
    piece = jnp.sum(got[:, : blocks * share], axis=0)
    theirs = got[:, blocks * share :].reshape(depth, slab * share + spare)[:, : slab * share]
    theirs = theirs.reshape(depth, slab, share).transpose(1, 0, 2).reshape(slab, depth * share)
    level = over_plane(copies(piece, planes))
    terms = dot(theirs, whole(level))
    terms = jnp.sum(over_core(terms.reshape(2, slab // 2, wide)), axis=0)
    terms = jnp.concatenate([terms[:, :width], terms[:, width:]], axis=0)
    cut = -(-blocks * share // planes)
    users = blocks * share // cut
    part = lax.dynamic_slice_in_dim(level, jnp.minimum(row, users - 1) * cut, cut, 1)
    line = over_z(jnp.concatenate([copies(terms, depth), copies(piece, depth), part], axis=1))
    terms = jnp.sum(line[:, :slab], axis=0)
    row_half = whole(line[:, slab : slab + blocks * share])
    part = line[:, slab + blocks * share :].reshape(depth * cut, width)
    disc = over_plane(copies(jnp.concatenate([terms, part], axis=0), planes))
    terms = over_core(copies(disc[:, :slab], 2))
    row_terms = over_core(copies(row_half, 2)).reshape(rows, wide)
    col_terms = disc[:users, slab:].reshape(blocks, users // blocks, depth, cut, width)
    col_terms = col_terms.transpose(2, 1, 3, 0, 4).reshape(half, wide)
    terms = terms.reshape(2, planes, blocks, slab // 2, width).transpose(1, 0, 3, 2, 4)
    inverse, gain = small_inverse(terms.reshape(wide, wide))
    scaled = dot(col_terms, inverse)
    updated = kron_inverse - dot(row_terms, scaled, ((1,), (1,)))
    own = rows // devices
    gains = dot(lax.dynamic_slice_in_dim(row_terms, col * own, own, 0), gain)
    return updated, gains.reshape(own, blocks, width).transpose(1, 0, 2)


def solution(mesh):
    return jax.shard_map(
        shards,
        mesh=mesh,
        in_specs=(P("row", "col"), P(None, None, "col")),
        out_specs=(P("row", "col"), P(None, ("row", "col"), None)),
        check_vma=False,
    )
```

time: 185 us -> 137 us (0.74)
  other arithmetic: 56.1 us -> 1.17 us
  blocking collectives: 51.9 us -> 74.6 us
  waiting for transfers between devices: 25.3 us -> 17 us
  starting transfers between devices: 30.8 us -> 24.6 us
  Pallas kernels: 0 us -> 5.69 us
  local copies, waits for them, and re-layouts: 10.8 us -> 7.03 us
    another operation x10 -> x0, other arithmetic: 54 us -> none  [the longest x6 34 us: shards(): factor = jnp.linalg.cholesky(system)]
    all_to_all x1 -> x2, blocking collectives: 26.9 us -> 51.3 us  [over_z(): lax.all_to_all(value, 'col', 0, 0, tiled=True, axis_index_groups=lines)]
    all_to_all x2 -> x0, waiting for transfers between devices: 12 us -> none  [over_z(): lax.all_to_all(value, 'col', 0, 0, tiled=True, axis_index_groups=lines)]
    all_to_all x2 -> x0, starting transfers between devices: 10.2 us -> none  [over_z(): lax.all_to_all(value, 'col', 0, 0, tiled=True, axis_index_groups=lines)]
    pallas_call x0 -> x1, Pallas kernels: none -> 5.69 us  [small_inverse(): pl.pallas_call(small_kernel, out_shape=[jax.ShapeDtypeStruct((wide, wide)...]
    another operation x9 -> x0, local copies, waits for them, and re-layouts: 4.12 us -> none
    all_to_all x1 -> x2, starting transfers between devices: 10.3 us -> 14.3 us  [over_core(): lax.all_to_all(value, 'col', 0, 0, tiled=True, axis_index_groups=pairs)]
    all_to_all x2, waiting for transfers between devices: 12.4 us -> 16.1 us  [over_plane(): return lax.all_to_all(value, 'row', 0, 0, tiled=True)]
  transfers between devices with their start and end apart: 5 -> 4, of which waited for: 4 -> 3; matrix products, arithmetic and copies ran while one was open for 34% -> 2% of each run, Pallas kernels for 0% -> 4%
where the time goes in v2:
time: 137 us; the launch traced here: 136 us
  blocking collectives  74.6 us (54%)
  starting transfers between devices  24.6 us (18%)
  waiting for transfers between devices  17 us (12%)
  local copies, waits for them, and re-layouts  7.03 us (5%)
  Pallas kernels  5.69 us (4%)
  matrix products  5.39 us (4%)
    all_to_all x2, blocking collectives, over_z(): lax.all_to_all(value, 'col', 0, 0, tiled=True, axis_index_groups=lines)  51.3 us
    all_to_all x2, blocking collectives, over_core(): lax.all_to_all(value, 'col', 0, 0, tiled=True, axis_index_groups=pairs)  23.2 us
    all_to_all x2, waiting for transfers between devices, over_plane(): return lax.all_to_all(value, 'row', 0, 0, tiled=True)  16.1 us
    all_to_all x2, starting transfers between devices, over_core(): lax.all_to_all(value, 'col', 0, 0, tiled=True, axis_index_groups=pairs)  14.3 us
    all_to_all x2, starting transfers between devices, over_plane(): return lax.all_to_all(value, 'row', 0, 0, tiled=True)  10.3 us
    pallas_call x1, Pallas kernels, small_inverse(): pl.pallas_call(small_kernel, out_shape=[jax.ShapeDtypeStruct((wide, wide)...  5.69 us
    dot_general x5, matrix products, dot(): lax.dot_general(a, b, (dims, ((), ())), precision=highest, preferred_elem...  5.39 us
  transfers between devices with their start and end apart: 4, of which 3 were waited for; matrix products, arithmetic and copies ran while one was open for 2% of the time, Pallas kernels for 4%

profile of v2, /device:TPU:1, one launch (start us, length us, event | category | flops | bytes accessed | tf_op | source)
XLA Modules:
  0.0 136.5 jit_solution(16051205309050271057)
XLA Ops:
  0.6 1.3 copy.11
  1.9 0.2 reshape.91
  2.2 0.3 copy.18
  2.5 1.9 %fusion.14 = f32[2,288,256]{2,1,0:T(8,128)} fusion(f32[2,288,288]{2,1,0:T(8,128)S(1)} %bitcast.36, f32[256,288,1]{0,1,2:T(8,128)S(1)} %reshape.91), kind=kOutput, calls=%fused_computation.27 | convolution fusion | flops 509607936 | bytes 1548288 | tf_op jit(solution)/shard_map/dot_general | solution.py:13
  4.4 10.5 %all-to-all-start = ((f32[2,288,256]{2,1,0:T(8,128)}), f32[2,288,256]{2,1,0:T(8,128)S(1)}, u32[]{:S(2)}, u32[]{:S(2)}) async-start(f32[2,288,256]{2,1,0:T(8,128)} %fusion.14), calls=%async_computation | async-start | bytes 1179648 | tf_op jit(solution)/shard_map/all_to_all | solution.py:115
  15.4 0.9 all-to-all-done
  16.4 24.8 %all_to_all.40 = f32[16,40,128]{2,1,0:T(8,128)S(1)} all-to-all(f32[16,40,128]{2,1,0:T(8,128)S(1)} %pad_maximum_fusion.1), channel_id=1, replica_groups={{0,2,4,6,8,10,12,14,16,18,20,22,24,26,28,30},{1,3,5,7,9,11,13,15,17,19,..., dimensions={0} | all-to-all | bytes 655360 | tf_op jit(solution)/shard_map/all_to_all | solution.py:118
  41.3 0.7 broadcast_in_dim.10
  42.0 6.8 %all-to-all-start.2 = ((f32[16,36,128]{2,1,0:T(8,128)}), f32[16,36,128]{2,1,0:T(8,128)S(1)}, u32[]{:S(2)}, u32[]{:S(2)}) async-start(f32[16,36,128]{2,1,0:T(8,128)} %broadcast_in_dim.10), calls=%async_computation.2 | async-start | bytes 655360 | tf_op jit(solution)/shard_map/all_to_all | solution.py:121
  49.1 7.4 %all-to-all-done.2 = f32[16,36,128]{2,1,0:T(8,128)S(1)} async-done(((f32[16,36,128]{2,1,0:T(8,128)}), f32[16,36,128]{2,1,0:T(8,128)S(1)}, u32[]{:S(2)}, u32[]{:S(2)}) %all-to-all-start.2) | async-done | bytes 294944 | tf_op jit(solution)/shard_map/all_to_all | solution.py:121
  56.7 11.4 %all_to_all.41 = f32[2,8,256]{2,1,0:T(8,128)S(1)} all-to-all(f32[2,8,256]{2,1,0:T(8,128)S(1)} %fusion.3), channel_id=1, replica_groups={{0,1},{2,3},{4,5},{6,7},{8,9},{10,11},{12,13},{14,15},{16,17},{18,19},{..., dimensions={0} | all-to-all | bytes 32768 | tf_op jit(solution)/shard_map/all_to_all | solution.py:115
  68.2 1.0 pad_maximum_fusion
  69.2 26.5 %all_to_all.42 = f32[16,55,128]{2,1,0:T(8,128)S(1)} all-to-all(f32[16,55,128]{2,1,0:T(8,128)S(1)} %pad_maximum_fusion), channel_id=1, replica_groups={{0,2,4,6,8,10,12,14,16,18,20,22,24,26,28,30},{1,3,5,7,9,11,13,15,17,19,..., dimensions={0} | all-to-all | bytes 901120 | tf_op jit(solution)/shard_map/all_to_all | solution.py:118
  95.8 0.8 broadcast_in_dim.13
  96.6 3.6 %all-to-all-start.6 = ((f32[16,64,128]{2,1,0:T(8,128)}), f32[16,64,128]{2,1,0:T(8,128)S(1)}, u32[]{:S(2)}, u32[]{:S(2)}) async-start(f32[16,64,128]{2,1,0:T(8,128)} %broadcast_in_dim.13), calls=%async_computation.6 | async-start | bytes 1048576 | tf_op jit(solution)/shard_map/all_to_all | solution.py:121
  100.3 8.8 %all-to-all-done.6 = f32[16,64,128]{2,1,0:T(8,128)S(1)} async-done(((f32[16,64,128]{2,1,0:T(8,128)}), f32[16,64,128]{2,1,0:T(8,128)S(1)}, u32[]{:S(2)}, u32[]{:S(2)}) %all-to-all-start.6) | async-done | bytes 524320 | tf_op jit(solution)/shard_map/all_to_all | solution.py:121
  109.6 11.8 %all_to_all.43 = f32[2,16,16,128]{3,2,1,0:T(8,128)S(1)} all-to-all(f32[2,16,16,128]{3,2,1,0:T(8,128)S(1)} %broadcast_in_dim.14), channel_id=1, replica_groups={{0,1},{2,3},{4,5},{6,7},{8,9},{10,11},{12,13},{14,15},{16,17},{18,19},{..., dimensions={0} | all-to-all | bytes 524288 | tf_op jit(solution)/shard_map/all_to_all | solution.py:115
  121.4 0.9 broadcast_in_dim.12
  122.2 3.9 %all-to-all-start.5 = ((f32[2,288,256]{2,1,0:T(8,128)}), f32[2,288,256]{2,1,0:T(8,128)S(1)}, u32[]{:S(2)}, u32[]{:S(2)}) async-start(f32[2,288,256]{2,1,0:T(8,128)} %broadcast_in_dim.12), calls=%async_computation.5 | async-start | bytes 1179648 | tf_op jit(solution)/shard_map/all_to_all | solution.py:115
  126.1 0.7 copy.17
  126.8 5.7 %shard_map.41 = (f32[256,256]{1,0:T(8,128)}, f32[256,256]{1,0:T(8,128)}) custom-call(f32[256,256]{1,0:T(8,128)} %bitcast.42), custom_call_target="tpu_custom_call" | custom-call | tf_op jit(solution)/shard_map/pallas_call | solution.py:95
  132.5 1.4 fusion
  133.9 1.7 %convolution_subtract_fusion = f32[576,288]{0,1:T(8,128)} fusion(f32[576,288]{0,1:T(8,128)S(1)} %copy-done, f32[576,256]{1,0:T(8,128)S(1)} %bitcast.37, f32[288,256]{1,0:T(8,128)S(1)} %fusion), kind=kOutput, calls=%fused_computation | convolution fusion | flops 509773824 | bytes 2211840 | tf_op jit(solution)/shard_map/dot_general | solution.py:13
  135.9 0.6 reshape.90
  (50 shorter events, 2.0 us)
Async XLA Ops:
  0.6 1.5 %copy-start = (f32[576,288]{0,1:T(8,128)S(1)}, f32[576,288]{0,1:T(8,128)}, u32[]{:S(2)}) copy-start(f32[576,288]{0,1:T(8,128)} %param.2) | copy-start | bytes 1990660
  4.4 10.5 %copy-start.1 = (f32[2,128,288]{1,2,0:T(8,128)S(1)}, f32[2,128,288]{1,2,0:T(8,128)}, u32[]{:S(2)}) copy-start(f32[2,128,288]{1,2,0:T(8,128)} %param.3) | copy-start | bytes 884740
  4.4 11.9 %all-to-all-start = ((f32[2,288,256]{2,1,0:T(8,128)}), f32[2,288,256]{2,1,0:T(8,128)S(1)}, u32[]{:S(2)}, u32[]{:S(2)}) async-start(f32[2,288,256]{2,1,0:T(8,128)} %fusion.14), calls=%async_computation | async-start | bytes 1179648 | tf_op jit(solution)/shard_map/all_to_all | solution.py:115
  42.0 14.4 %all-to-all-start.2 = ((f32[16,36,128]{2,1,0:T(8,128)}), f32[16,36,128]{2,1,0:T(8,128)S(1)}, u32[]{:S(2)}, u32[]{:S(2)}) async-start(f32[16,36,128]{2,1,0:T(8,128)} %broadcast_in_dim.10), calls=%async_computation.2 | async-start | bytes 655360 | tf_op jit(solution)/shard_map/all_to_all | solution.py:121
  96.6 12.5 %all-to-all-start.6 = ((f32[16,64,128]{2,1,0:T(8,128)}), f32[16,64,128]{2,1,0:T(8,128)S(1)}, u32[]{:S(2)}, u32[]{:S(2)}) async-start(f32[16,64,128]{2,1,0:T(8,128)} %broadcast_in_dim.13), calls=%async_computation.6 | async-start | bytes 1048576 | tf_op jit(solution)/shard_map/all_to_all | solution.py:121
  122.2 11.6 %all-to-all-start.5 = ((f32[2,288,256]{2,1,0:T(8,128)}), f32[2,288,256]{2,1,0:T(8,128)S(1)}, u32[]{:S(2)}, u32[]{:S(2)}) async-start(f32[2,288,256]{2,1,0:T(8,128)} %broadcast_in_dim.12), calls=%async_computation.5 | async-start | bytes 1179648 | tf_op jit(solution)/shard_map/all_to_all | solution.py:115
  133.9 1.7 %copy-start.2 = (f32[256,256]{1,0:T(8,128)S(1)}, f32[256,256]{1,0:T(8,128)}, u32[]{:S(2)}) copy-start(f32[256,256]{1,0:T(8,128)} %get-tuple-element.5) | copy-start | bytes 786436

commit v3 on v2

--- a/solution.py
+++ b/solution.py
@@ -4,6 +4,7 @@
 from jax.experimental import pallas as pl
 from jax.experimental.pallas import tpu as pltpu
 from jax.sharding import PartitionSpec as P
+
 
 highest = lax.Precision.HIGHEST
 f32 = jnp.float32
@@ -69,34 +70,47 @@
     out_ref[...] = (guess + rough(rest, guess)) * scale_col * scale_row
 
 
-def small_kernel(terms_ref, whole_ref, gain_ref, first_ref, last_ref, work_ref):
-    wide = terms_ref.shape[0]
-    width = wide // 2
+def closing_kernel(terms_ref, rows_ref, cols_ref, own_ref, start_ref, out_ref, gain_ref, first_ref, last_ref, work_ref):
+    depth = terms_ref.shape[1]
+    width = first_ref.shape[0]
+    step = terms_ref.shape[2] // 2
+    blocks = [[None, None], [None, None]]
+    for high in range(2):
+        for right in range(2):
+            part = terms_ref[:, high * depth // 2 : (high + 1) * depth // 2, right * step : (right + 1) * step]
+            blocks[high][right] = jnp.transpose(part, (1, 0, 2, 3)).reshape(width, width)
     eye = unit(width)
-    invert(terms_ref[:width, :width] + eye, first_ref, work_ref)
+    invert(blocks[0][0] + eye, first_ref, work_ref)
     first = first_ref[...]
-    cross = terms_ref[:width, width:]
+    cross = blocks[0][1]
     carry = dot(first, cross)
-    invert(terms_ref[width:, width:] + eye - dot(cross, carry, ((0,), (0,))), last_ref, work_ref)
+    invert(blocks[1][1] + eye - dot(cross, carry, ((0,), (0,))), last_ref, work_ref)
     last = last_ref[...]
     corner = dot(carry, last)
-    whole_ref[:width, :width] = first + dot(corner, carry, ((1,), (1,)))
-    whole_ref[:width, width:] = -corner
-    whole_ref[width:, :width] = -corner.T
-    whole_ref[width:, width:] = last
-    gain_ref[:width, :width] = first
-    gain_ref[:width, width:] = -corner
-    gain_ref[width:, :width] = jnp.zeros((width, width), f32)
-    gain_ref[width:, width:] = last
+    whole = first + dot(corner, carry, ((1,), (1,)))
+    left, right = cols_ref[:, :width], cols_ref[:, width:]
+    left, right = (
+        dot(left, whole) - dot(right, corner, ((1,), (1,))),
+        dot(right, last) - dot(left, corner),
+    )
+    out = start_ref[...] - dot(left, rows_ref[:, :width], ((1,), (1,)))
+    out_ref[...] = out - dot(right, rows_ref[:, width:], ((1,), (1,)))
+    left, right = own_ref[:, :width], own_ref[:, width:]
+    gain_ref[:, 0] = dot(left, first)
+    gain_ref[:, 1] = dot(right, last) - dot(left, corner)
 
 
-def small_inverse(terms):
-    wide = terms.shape[0]
+def closing(terms, row_terms, col_terms, own, start):
+    width = own.shape[1] // 2
     return pl.pallas_call(
-        small_kernel,
-        out_shape=[jax.ShapeDtypeStruct((wide, wide), f32)] * 2,
-        scratch_shapes=[pltpu.VMEM((wide // 2, wide // 2), f32)] * 3,
-    )(terms)
+        closing_kernel,
+        out_shape=[
+            jax.ShapeDtypeStruct(start.shape, f32),
+            jax.ShapeDtypeStruct((own.shape[0], 2, width), f32),
+        ],
+        in_specs=[pl.BlockSpec(memory_space=pltpu.VMEM)] * 5,
+        scratch_shapes=[pltpu.VMEM((width, width), f32)] * 3,
+    )(terms, row_terms, col_terms, own, start)
 
 
 def shards(kron_inverse, activations):
@@ -109,10 +123,9 @@
     row = lax.axis_index("row")
     col = lax.axis_index("col")
     lines = [[2 * z + k for z in range(depth)] for k in range(2)]
-    pairs = [[2 * z, 2 * z + 1] for z in range(depth)]
 
-    def over_core(value):
-        return lax.all_to_all(value, "col", 0, 0, tiled=True, axis_index_groups=pairs)
+    def from_partner(value):
+        return lax.ppermute(value, "col", [(at, at ^ 1) for at in range(devices)])
 
     def over_z(value):
         return lax.all_to_all(value, "col", 0, 0, tiled=True, axis_index_groups=lines)
@@ -132,20 +145,22 @@
         return jnp.concatenate([left, value[:, share:].reshape(half, width)], axis=1)
 
     spare = -slab * share % (4 * width)
-    stacked = activations.reshape(wide, cols)
-    partial = dot(kron_inverse, stacked.T)
-    summed = jnp.sum(over_core(partial.reshape(2, half, wide)), axis=0)
-    mine = lax.dynamic_slice_in_dim(stacked, row * slab, slab, 0)
+    core = col % 2
+    partial = jnp.stack([dot(kron_inverse, block.T) for block in activations])
+    other = lax.dynamic_slice_in_dim(partial, (1 - core) * half, half, 1)
+    summed = lax.dynamic_slice_in_dim(partial, core * half, half, 1) + from_partner(other)
+    mine = lax.dynamic_slice_in_dim(activations.reshape(wide, cols), row * slab, slab, 0)
     mine = mine.reshape(slab, depth, share).transpose(1, 0, 2).reshape(depth, slab * share)
     mine = jnp.pad(mine, ((0, 0), (0, spare))).reshape(depth, -1, width)
-    parts = [summed[:, at : at + width].reshape(depth, share, width) for at in range(0, wide, width)]
+    parts = [summed[at].reshape(depth, share, width) for at in range(blocks)]
     got = over_z(jnp.concatenate([*parts, mine], axis=1))
     piece = jnp.sum(got[:, : blocks * share], axis=0)
     theirs = got[:, blocks * share :].reshape(depth, slab * share + spare)[:, : slab * share]
     theirs = theirs.reshape(depth, slab, share).transpose(1, 0, 2).reshape(slab, depth * share)
     level = over_plane(copies(piece, planes))
     terms = dot(theirs, whole(level))
-    terms = jnp.sum(over_core(terms.reshape(2, slab // 2, wide)), axis=0)
+    other = lax.dynamic_slice_in_dim(terms, (1 - core) * (slab // 2), slab // 2, 0)
+    terms = lax.dynamic_slice_in_dim(terms, core * (slab // 2), slab // 2, 0) + from_partner(other)
     terms = jnp.concatenate([terms[:, :width], terms[:, width:]], axis=0)
     cut = -(-blocks * share // planes)
     users = blocks * share // cut
@@ -155,17 +170,21 @@
     row_half = whole(line[:, slab : slab + blocks * share])
     part = line[:, slab + blocks * share :].reshape(depth * cut, width)
     disc = over_plane(copies(jnp.concatenate([terms, part], axis=0), planes))
-    terms = over_core(copies(disc[:, :slab], 2))
-    row_terms = over_core(copies(row_half, 2)).reshape(rows, wide)
+    row_other = from_partner(row_half)
+
+    def in_order(value, other):
+        low = jnp.where(core == 0, value, other)
+        return jnp.stack([low, jnp.where(core == 0, other, value)])
+
+    row_terms = in_order(row_half, row_other).reshape(rows, wide)
+    own = rows // devices
+    own_terms = lax.dynamic_slice_in_dim(row_terms, col * own, own, 0)
+    terms = disc[:, :slab]
+    terms = in_order(terms, from_partner(terms))
     col_terms = disc[:users, slab:].reshape(blocks, users // blocks, depth, cut, width)
     col_terms = col_terms.transpose(2, 1, 3, 0, 4).reshape(half, wide)
-    terms = terms.reshape(2, planes, blocks, slab // 2, width).transpose(1, 0, 3, 2, 4)
-    inverse, gain = small_inverse(terms.reshape(wide, wide))
-    scaled = dot(col_terms, inverse)
-    updated = kron_inverse - dot(row_terms, scaled, ((1,), (1,)))
-    own = rows // devices
-    gains = dot(lax.dynamic_slice_in_dim(row_terms, col * own, own, 0), gain)
-    return updated, gains.reshape(own, blocks, width).transpose(1, 0, 2)
+    updated, gains = closing(terms, row_terms, col_terms, own_terms, kron_inverse.T)
+    return updated.T, gains.transpose(1, 0, 2)
 
 
 def solution(mesh):

time: 137 us -> 133 us (0.971)
  blocking collectives: 74.6 us -> 51.3 us
  starting transfers between devices: 24.6 us -> 42 us
  local copies, waits for them, and re-layouts: 7.03 us -> 4.47 us
  Pallas kernels: 5.69 us -> 8.13 us
  waiting for transfers between devices: 17 us -> 18.9 us
    ppermute x0 -> x4, starting transfers between devices: none -> 31.6 us  [from_partner(): return lax.ppermute(value, 'col', [(at, at ^ 1) for at in range(devices)])]
    all_to_all x2 -> x0, blocking collectives: 23.2 us -> none  [over_core(): lax.all_to_all(value, 'col', 0, 0, tiled=True, axis_index_groups=pairs)]
    all_to_all x2 -> x0, starting transfers between devices: 14.3 us -> none  [over_core(): lax.all_to_all(value, 'col', 0, 0, tiled=True, axis_index_groups=pairs)]
    pallas_call x1, Pallas kernels: 5.69 us -> 8.13 us  [closing(): pl.pallas_call(closing_kernel, out_shape=[jax.ShapeDtypeStruct(start.shap...]
    reshape x6 -> x1, local copies, waits for them, and re-layouts: 1.63 us -> 0.02 us  [shards(): activations.reshape(wide, cols)]
    ppermute x0 -> x4, waiting for transfers between devices: none -> 1.39 us  [from_partner(): return lax.ppermute(value, 'col', [(at, at ^ 1) for at in range(devices)])]
    dot_general x5 -> x3, matrix products: 5.39 us -> 4.78 us  [dot(): lax.dot_general(a, b, (dims, ((), ())), precision=highest, preferred_elem...]
  transfers between devices with their start and end apart: 4 -> 6, of which waited for: 3 -> 4; matrix products, arithmetic and copies ran while one was open for 2% -> 3% of each run, Pallas kernels for 4% -> 0%
where the time goes in v3:
time: 133 us
  blocking collectives  51.3 us (39%)
  starting transfers between devices  42 us (32%)
  waiting for transfers between devices  18.9 us (14%)
  Pallas kernels  8.13 us (6%)
  matrix products  4.78 us (4%)
  local copies, waits for them, and re-layouts  4.47 us (3%)
  other arithmetic  2 us (2%)
    all_to_all x2, blocking collectives, over_z(): lax.all_to_all(value, 'col', 0, 0, tiled=True, axis_index_groups=lines)  51.3 us
    ppermute x4, starting transfers between devices, from_partner(): return lax.ppermute(value, 'col', [(at, at ^ 1) for at in range(devices)])  31.6 us
    all_to_all x2, waiting for transfers between devices, over_plane(): return lax.all_to_all(value, 'row', 0, 0, tiled=True)  17.5 us
    all_to_all x2, starting transfers between devices, over_plane(): return lax.all_to_all(value, 'row', 0, 0, tiled=True)  10.3 us
    pallas_call x1, Pallas kernels, closing(): pl.pallas_call(closing_kernel, out_shape=[jax.ShapeDtypeStruct(start.shap...  8.13 us
    dot_general x3, matrix products, dot(): lax.dot_general(a, b, (dims, ((), ())), precision=highest, preferred_elem...  4.78 us
  transfers between devices with their start and end apart: 6, of which 4 were waited for; matrix products, arithmetic and copies ran while one was open for 3% of the time, Pallas kernels for 0%

profile of v3, /device:TPU:1, one launch (start us, length us, event | category | flops | bytes accessed | tf_op | source)
XLA Modules:
  0.0 132.6 jit_solution(7723256497184530393)
XLA Ops:
  0.7 2.9 %convolution_bitcast_fusion.1 = f32[1,576,128]{2,1,0:T(8,128)S(1)} fusion(f32[576,288]{0,1:T(8,128)} %param.2, f32[2,128,288]{1,2,0:T(8,128)} %param.3), kind=kOutput, calls=%fused_computation.1 | convolution fusion | flops 254803968 | bytes 1179648 | tf_op jit(solution)/shard_map/dot_general | solution.py:14
  3.6 1.7 %convolution_bitcast_fusion = f32[1,576,128]{2,1,0:T(8,128)S(1)} fusion(f32[576,288]{0,1:T(8,128)S(1)} %copy-done, f32[2,128,288]{1,2,0:T(8,128)S(1)} %copy-done.2), kind=kOutput, calls=%fused_computation | convolution fusion | flops 254803968 | bytes 1179648 | tf_op jit(solution)/shard_map/dot_general | solution.py:14
  5.3 8.7 %collective-permute-start = (f32[2,288,128]{2,1,0:T(8,128)S(1)}, f32[2,288,128]{2,1,0:T(8,128)S(1)}, u32[]{:S(2)}, u32[]{:S(2)}) collective-permute-start(f32[2,288,128]{2,1,0:T(8,128)S(1)} %fusion), channel_id=1, source_target_pairs={{0,1},{1,0},{2,3},{3,2},{4,5},{5,4},{6,7},{7,6},{8,9},{9,8},{10,11... | collective-permute-start | bytes 884744 | tf_op jit(solution)/shard_map/ppermute | solution.py:128
  14.3 0.1 reshape.53
  14.6 0.6 collective-permute-done
  15.4 24.8 %all_to_all.20 = f32[16,40,128]{2,1,0:T(8,128)S(1)} all-to-all(f32[16,40,128]{2,1,0:T(8,128)S(1)} %pad_maximum_fusion.2), channel_id=1, replica_groups={{0,2,4,6,8,10,12,14,16,18,20,22,24,26,28,30},{1,3,5,7,9,11,13,15,17,19,..., dimensions={0} | all-to-all | bytes 655360 | tf_op jit(solution)/shard_map/all_to_all | solution.py:131
  40.3 0.7 broadcast_in_dim.6
  41.0 6.8 %all-to-all-start.1 = ((f32[16,36,128]{2,1,0:T(8,128)}), f32[16,36,128]{2,1,0:T(8,128)S(1)}, u32[]{:S(2)}, u32[]{:S(2)}) async-start(f32[16,36,128]{2,1,0:T(8,128)} %broadcast_in_dim.6), calls=%async_computation.1 | async-start | bytes 655360 | tf_op jit(solution)/shard_map/all_to_all | solution.py:134
  48.1 7.3 %all-to-all-done.1 = f32[16,36,128]{2,1,0:T(8,128)S(1)} async-done(((f32[16,36,128]{2,1,0:T(8,128)}), f32[16,36,128]{2,1,0:T(8,128)S(1)}, u32[]{:S(2)}, u32[]{:S(2)}) %all-to-all-start.1) | async-done | bytes 294944 | tf_op jit(solution)/shard_map/all_to_all | solution.py:134
  55.5 0.2 fusion.3
  55.8 9.9 %collective-permute-start.1 = (f32[8,256]{1,0:T(8,128)S(1)}, f32[8,256]{1,0:T(8,128)S(1)}, u32[]{:S(2)}, u32[]{:S(2)}) collective-permute-start(f32[8,256]{1,0:T(8,128)S(1)} %constant_dynamic-slice_fusion.2), channel_id=1, source_target_pairs={{0,1},{1,0},{2,3},{3,2},{4,5},{5,4},{6,7},{7,6},{8,9},{9,8},{10,11... | collective-permute-start | bytes 24584 | tf_op jit(solution)/shard_map/ppermute | solution.py:128
  65.7 0.8 collective-permute-done.1
  66.5 1.0 pad_maximum_fusion.1
  67.5 26.5 %all_to_all.21 = f32[16,55,128]{2,1,0:T(8,128)S(1)} all-to-all(f32[16,55,128]{2,1,0:T(8,128)S(1)} %pad_maximum_fusion.1), channel_id=1, replica_groups={{0,2,4,6,8,10,12,14,16,18,20,22,24,26,28,30},{1,3,5,7,9,11,13,15,17,19,..., dimensions={0} | all-to-all | bytes 901120 | tf_op jit(solution)/shard_map/all_to_all | solution.py:131
  94.2 8.9 %collective-permute-start.3 = (f32[288,256]{1,0:T(8,128)S(1)}, f32[288,256]{1,0:T(8,128)S(1)}, u32[]{:S(2)}, u32[]{:S(2)}) collective-permute-start(f32[288,256]{1,0:T(8,128)S(1)} %constant_dynamic-update-slice_fusion), channel_id=1, source_target_pairs={{0,1},{1,0},{2,3},{3,2},{4,5},{5,4},{6,7},{7,6},{8,9},{9,8},{10,11... | collective-permute-start | bytes 884744 | tf_op jit(solution)/shard_map/ppermute | solution.py:128
  103.1 0.8 broadcast_in_dim.8
  104.0 3.6 %all-to-all-start.3 = ((f32[16,64,128]{2,1,0:T(8,128)}), f32[16,64,128]{2,1,0:T(8,128)S(1)}, u32[]{:S(2)}, u32[]{:S(2)}) async-start(f32[16,64,128]{2,1,0:T(8,128)} %broadcast_in_dim.8), calls=%async_computation.3 | async-start | bytes 1048576 | tf_op jit(solution)/shard_map/all_to_all | solution.py:134
  107.6 10.1 %all-to-all-done.3 = f32[16,64,128]{2,1,0:T(8,128)S(1)} async-done(((f32[16,64,128]{2,1,0:T(8,128)}), f32[16,64,128]{2,1,0:T(8,128)S(1)}, u32[]{:S(2)}, u32[]{:S(2)}) %all-to-all-start.3) | async-done | bytes 524320 | tf_op jit(solution)/shard_map/all_to_all | solution.py:134
  117.8 4.1 %collective-permute-start.2 = (f32[16,16,128]{2,1,0:T(8,128)S(1)}, f32[16,16,128]{2,1,0:T(8,128)S(1)}, u32[]{:S(2)}, u32[]{:S(2)}) collective-permute-start(f32[16,16,128]{2,1,0:T(8,128)S(1)} %slice.74), channel_id=1, source_target_pairs={{0,1},{1,0},{2,3},{3,2},{4,5},{5,4},{6,7},{7,6},{8,9},{9,8},{10,11... | collective-permute-start | bytes 393224 | tf_op jit(solution)/shard_map/ppermute | solution.py:128
  122.0 0.7 constant_dynamic-slice_fusion.own_ref
  122.8 0.2 copy.12
  123.0 0.7 copy.19
  123.8 0.7 pad_maximum_fusion.3.terms_ref
  124.5 8.1 %shard_map.41 = (f32[288,576]{1,0:T(8,128)}, f32[18,2,128]{2,1,0:T(2,128)}) custom-call(f32[2,16,16,128]{3,2,1,0:T(8,128)} %pad_maximum_fusion.3.terms_ref, f32[576,256]{1,0:T(8,128)} %bitcast.44, f32[288,256]{1,0:T(8,128)} %bitcast.47, f32[18,256]{1,0:T(8,128)} %constant_dynamic-slice_fusion.own_ref, f32[288,576]{1,0:T(8,128)} %bitcast.42), custom_call_target="tpu_custom_call" | custom-call | tf_op jit(solution)/shard_map/pallas_call | solution.py:105
  (52 shorter events, 1.4 us)
Async XLA Ops:
  0.6 2.9 %copy-start = (f32[576,288]{0,1:T(8,128)S(1)}, f32[576,288]{0,1:T(8,128)}, u32[]{:S(2)}) copy-start(f32[576,288]{0,1:T(8,128)} %param.2) | copy-start | bytes 1990660
  0.6 2.9 %copy-start.2 = (f32[2,128,288]{1,2,0:T(8,128)S(1)}, f32[2,128,288]{1,2,0:T(8,128)}, u32[]{:S(2)}) copy-start(f32[2,128,288]{1,2,0:T(8,128)} %param.3) | copy-start | bytes 884740
  5.3 9.9 %collective-permute-start = (f32[2,288,128]{2,1,0:T(8,128)S(1)}, f32[2,288,128]{2,1,0:T(8,128)S(1)}, u32[]{:S(2)}, u32[]{:S(2)}) collective-permute-start(f32[2,288,128]{2,1,0:T(8,128)S(1)} %fusion), channel_id=1, source_target_pairs={{0,1},{1,0},{2,3},{3,2},{4,5},{5,4},{6,7},{7,6},{8,9},{9,8},{10,11... | collective-permute-start | bytes 884744 | tf_op jit(solution)/shard_map/ppermute | solution.py:128
  41.0 14.4 %all-to-all-start.1 = ((f32[16,36,128]{2,1,0:T(8,128)}), f32[16,36,128]{2,1,0:T(8,128)S(1)}, u32[]{:S(2)}, u32[]{:S(2)}) async-start(f32[16,36,128]{2,1,0:T(8,128)} %broadcast_in_dim.6), calls=%async_computation.1 | async-start | bytes 655360 | tf_op jit(solution)/shard_map/all_to_all | solution.py:134
  55.8 10.7 %collective-permute-start.1 = (f32[8,256]{1,0:T(8,128)S(1)}, f32[8,256]{1,0:T(8,128)S(1)}, u32[]{:S(2)}, u32[]{:S(2)}) collective-permute-start(f32[8,256]{1,0:T(8,128)S(1)} %constant_dynamic-slice_fusion.2), channel_id=1, source_target_pairs={{0,1},{1,0},{2,3},{3,2},{4,5},{5,4},{6,7},{7,6},{8,9},{9,8},{10,11... | collective-permute-start | bytes 24584 | tf_op jit(solution)/shard_map/ppermute | solution.py:128
  94.2 13.4 %collective-permute-start.3 = (f32[288,256]{1,0:T(8,128)S(1)}, f32[288,256]{1,0:T(8,128)S(1)}, u32[]{:S(2)}, u32[]{:S(2)}) collective-permute-start(f32[288,256]{1,0:T(8,128)S(1)} %constant_dynamic-update-slice_fusion), channel_id=1, source_target_pairs={{0,1},{1,0},{2,3},{3,2},{4,5},{5,4},{6,7},{7,6},{8,9},{9,8},{10,11... | collective-permute-start | bytes 884744 | tf_op jit(solution)/shard_map/ppermute | solution.py:128
  104.0 13.8 %all-to-all-start.3 = ((f32[16,64,128]{2,1,0:T(8,128)}), f32[16,64,128]{2,1,0:T(8,128)S(1)}, u32[]{:S(2)}, u32[]{:S(2)}) async-start(f32[16,64,128]{2,1,0:T(8,128)} %broadcast_in_dim.8), calls=%async_computation.3 | async-start | bytes 1048576 | tf_op jit(solution)/shard_map/all_to_all | solution.py:134
  117.8 6.0 %collective-permute-start.2 = (f32[16,16,128]{2,1,0:T(8,128)S(1)}, f32[16,16,128]{2,1,0:T(8,128)S(1)}, u32[]{:S(2)}, u32[]{:S(2)}) collective-permute-start(f32[16,16,128]{2,1,0:T(8,128)S(1)} %slice.74), channel_id=1, source_target_pairs={{0,1},{1,0},{2,3},{3,2},{4,5},{5,4},{6,7},{7,6},{8,9},{9,8},{10,11... | collective-permute-start | bytes 393224 | tf_op jit(solution)/shard_map/ppermute | solution.py:128
  121.9 0.8 copy-start.1

commit v4 on v3

--- a/solution.py
+++ b/solution.py
@@ -68,6 +68,30 @@
     guess = out_ref[...]
     rest = eye - dot(guess, scaled)
     out_ref[...] = (guess + rough(rest, guess)) * scale_col * scale_row
+
+
+def opening_kernel(core_ref, start_ref, lines_ref, keep_ref, send_ref):
+    blocks, half, width = keep_ref.shape
+    lines = jnp.concatenate([lines_ref[at] for at in range(blocks)], axis=1)
+    value = dot(start_ref[...], lines, ((0,), (0,)))
+
+    def store(low_ref, high_ref):
+        for at in range(blocks):
+            low_ref[at] = value[:half, at * width : (at + 1) * width]
+            high_ref[at] = value[half:, at * width : (at + 1) * width]
+
+    pl.when(core_ref[0] == 0)(lambda: store(keep_ref, send_ref))
+    pl.when(core_ref[0] != 0)(lambda: store(send_ref, keep_ref))
+
+
+def opening(core, start, lines):
+    blocks, _, width = lines.shape
+    in_vmem = pl.BlockSpec(memory_space=pltpu.VMEM)
+    return pl.pallas_call(
+        opening_kernel,
+        out_shape=[pltpu.VMEM((blocks, start.shape[1] // 2, width), f32)] * 2,
+        in_specs=[pl.BlockSpec(memory_space=pltpu.SMEM), in_vmem, in_vmem],
+    )(core.reshape(1), start, lines)
 
 
 def closing_kernel(terms_ref, rows_ref, cols_ref, own_ref, start_ref, out_ref, gain_ref, first_ref, last_ref, work_ref):
@@ -110,7 +134,7 @@
         ],
         in_specs=[pl.BlockSpec(memory_space=pltpu.VMEM)] * 5,
         scratch_shapes=[pltpu.VMEM((width, width), f32)] * 3,
-    )(terms, row_terms, col_terms, own, start)
+    )(*(pltpu.with_memory_space_constraint(x, pltpu.VMEM) for x in (terms, row_terms, col_terms, own)), start)
 
 
 def shards(kron_inverse, activations):
@@ -122,13 +146,17 @@
     depth = devices // 2
     row = lax.axis_index("row")
     col = lax.axis_index("col")
+    near = 4 if depth % 4 == 0 else 1
+    far = depth // near
     lines = [[2 * z + k for z in range(depth)] for k in range(2)]
+    close = [[2 * (near * j + q) + k for q in range(near)] for j in range(far) for k in range(2)]
+    apart = [[2 * (near * j + q) + k for j in range(far)] for q in range(near) for k in range(2)]
 
     def from_partner(value):
         return lax.ppermute(value, "col", [(at, at ^ 1) for at in range(devices)])
 
-    def over_z(value):
-        return lax.all_to_all(value, "col", 0, 0, tiled=True, axis_index_groups=lines)
+    def over_z(value, groups):
+        return lax.all_to_all(value, "col", 0, 0, tiled=True, axis_index_groups=groups)
 
     def over_plane(value):
         return lax.all_to_all(value, "row", 0, 0, tiled=True)
@@ -146,14 +174,13 @@
 
     spare = -slab * share % (4 * width)
     core = col % 2
-    partial = jnp.stack([dot(kron_inverse, block.T) for block in activations])
-    other = lax.dynamic_slice_in_dim(partial, (1 - core) * half, half, 1)
-    summed = lax.dynamic_slice_in_dim(partial, core * half, half, 1) + from_partner(other)
+    keep, send = opening(core, kron_inverse.T, activations.transpose(0, 2, 1))
+    summed = keep + from_partner(send)
     mine = lax.dynamic_slice_in_dim(activations.reshape(wide, cols), row * slab, slab, 0)
     mine = mine.reshape(slab, depth, share).transpose(1, 0, 2).reshape(depth, slab * share)
     mine = jnp.pad(mine, ((0, 0), (0, spare))).reshape(depth, -1, width)
     parts = [summed[at].reshape(depth, share, width) for at in range(blocks)]
-    got = over_z(jnp.concatenate([*parts, mine], axis=1))
+    got = over_z(jnp.concatenate([*parts, mine], axis=1), lines)
     piece = jnp.sum(got[:, : blocks * share], axis=0)
     theirs = got[:, blocks * share :].reshape(depth, slab * share + spare)[:, : slab * share]
     theirs = theirs.reshape(depth, slab, share).transpose(1, 0, 2).reshape(slab, depth * share)
@@ -165,10 +192,24 @@
     cut = -(-blocks * share // planes)
     users = blocks * share // cut
     part = lax.dynamic_slice_in_dim(level, jnp.minimum(row, users - 1) * cut, cut, 1)
-    line = over_z(jnp.concatenate([copies(terms, depth), copies(piece, depth), part], axis=1))
-    terms = jnp.sum(line[:, :slab], axis=0)
-    row_half = whole(line[:, slab : slab + blocks * share])
-    part = line[:, slab + blocks * share :].reshape(depth * cut, width)
+    held = blocks * share
+
+    def padded(value):
+        return jnp.pad(value, ((0, 0), (0, -value.shape[1] % 8), (0, 0)))
+
+    part = padded(part.reshape(far, near * cut, width))
+    there = over_z(jnp.concatenate([copies(terms, far), padded(copies(piece, far)), part], axis=1), apart)
+    terms = jnp.sum(there[:, :slab], axis=0)
+    tall = held + -held % 8
+    pieces = there[:, slab : slab + tall].reshape(far * tall, width)
+    part = there[:, slab + tall : slab + tall + near * cut].reshape(far, near, cut, width)
+    part = padded(part.transpose(1, 0, 2, 3).reshape(near, far * cut, width))
+    there = over_z(jnp.concatenate([copies(terms, near), copies(pieces, near), part], axis=1), close)
+    terms = jnp.sum(there[:, :slab], axis=0)
+    pieces = there[:, slab : slab + far * tall].reshape(near, far, tall, width).transpose(1, 0, 2, 3)
+    row_half = whole(pieces.reshape(depth, tall, width)[:, :held])
+    part = there[:, slab + far * tall :][:, : far * cut].reshape(near, far, cut, width)
+    part = part.transpose(1, 0, 2, 3).reshape(depth * cut, width)
     disc = over_plane(copies(jnp.concatenate([terms, part], axis=0), planes))
     row_other = from_partner(row_half)
 

time: 133 us -> 131 us (0.985)
  blocking collectives: 51.3 us -> 58.2 us
  matrix products: 4.78 us -> 0.21 us
  starting transfers between devices: 42 us -> 38 us
  Pallas kernels: 8.13 us -> 10.3 us
  other arithmetic: 2 us -> 0.29 us
    all_to_all x2 -> x3, blocking collectives: 51.3 us -> 58.2 us  [over_z(): lax.all_to_all(value, 'col', 0, 0, tiled=True, axis_index_groups=groups)]
    dot_general x3 -> x1, matrix products: 4.78 us -> 0.21 us  [dot(): lax.dot_general(a, b, (dims, ((), ())), precision=highest, preferred_elem...]
    ppermute x4, starting transfers between devices: 31.6 us -> 27.7 us  [from_partner(): return lax.ppermute(value, 'col', [(at, at ^ 1) for at in range(devices)])]
    pallas_call x0 -> x1, Pallas kernels: none -> 2.46 us  [opening(): pl.pallas_call(opening_kernel, out_shape=[pltpu.VMEM((blocks, start.shape...]
  transfers between devices with their start and end apart: 6 -> 6, of which waited for: 4 -> 5; matrix products, arithmetic and copies ran while one was open for 3% -> 2% of each run, Pallas kernels for 0% -> 0%
where the time goes in v4:
time: 131 us
  blocking collectives  58.2 us (44%)
  starting transfers between devices  38 us (29%)
  waiting for transfers between devices  19.3 us (15%)
  Pallas kernels  10.3 us (8%)
  local copies, waits for them, and re-layouts  3.24 us (2%)
    all_to_all x3, blocking collectives, over_z(): lax.all_to_all(value, 'col', 0, 0, tiled=True, axis_index_groups=groups)  58.2 us
    ppermute x4, starting transfers between devices, from_partner(): return lax.ppermute(value, 'col', [(at, at ^ 1) for at in range(devices)])  27.7 us
    all_to_all x2, waiting for transfers between devices, over_plane(): return lax.all_to_all(value, 'row', 0, 0, tiled=True)  17.5 us
    all_to_all x2, starting transfers between devices, over_plane(): return lax.all_to_all(value, 'row', 0, 0, tiled=True)  10.3 us
    pallas_call x1, Pallas kernels, closing(): pl.pallas_call(closing_kernel, out_shape=[jax.ShapeDtypeStruct(start.shap...  7.8 us
  transfers between devices with their start and end apart: 6, of which 5 were waited for; matrix products, arithmetic and copies ran while one was open for 2% of the time, Pallas kernels for 0%

profile of v4, /device:TPU:1, one launch (start us, length us, event | category | flops | bytes accessed | tf_op | source)
XLA Modules:
  0.0 130.7 jit_solution(7291412365159103017)
XLA Ops:
  0.7 2.5 %shard_map.41 = (f32[2,288,128]{2,1,0:T(8,128)S(1)}, f32[2,288,128]{2,1,0:T(8,128)S(1)}) custom-call(s32[1]{0:T(128)} %bitcast.core_ref, f32[288,576]{1,0:T(8,128)} %bitcast.47, f32[2,288,128]{2,1,0:T(8,128)} %bitcast.52), custom_call_target="tpu_custom_call" | custom-call | tf_op jit(solution)/shard_map/pallas_call | solution.py:90
  3.1 8.7 %collective-permute-start = (f32[2,288,128]{2,1,0:T(8,128)S(1)}, f32[2,288,128]{2,1,0:T(8,128)S(1)}, u32[]{:S(2)}, u32[]{:S(2)}) collective-permute-start(f32[2,288,128]{2,1,0:T(8,128)S(1)} %get-tuple-element.7), channel_id=1, source_target_pairs={{0,1},{1,0},{2,3},{3,2},{4,5},{5,4},{6,7},{7,6},{8,9},{9,8},{10,11... | collective-permute-start | bytes 884744 | tf_op jit(solution)/shard_map/ppermute | solution.py:156
  12.1 0.1 reshape.77
  12.3 0.1 reshape.78
  12.4 0.6 collective-permute-done
  13.2 24.8 %all_to_all.25 = f32[16,40,128]{2,1,0:T(8,128)S(1)} all-to-all(f32[16,40,128]{2,1,0:T(8,128)S(1)} %pad_maximum_fusion.1), channel_id=1, replica_groups={{0,2,4,6,8,10,12,14,16,18,20,22,24,26,28,30},{1,3,5,7,9,11,13,15,17,19,..., dimensions={0} | all-to-all | bytes 655360 | tf_op jit(solution)/shard_map/all_to_all | solution.py:159
  38.1 0.7 broadcast_in_dim.14
  38.8 6.8 %all-to-all-start.1 = ((f32[16,36,128]{2,1,0:T(8,128)}), f32[16,36,128]{2,1,0:T(8,128)S(1)}, u32[]{:S(2)}, u32[]{:S(2)}) async-start(f32[16,36,128]{2,1,0:T(8,128)} %broadcast_in_dim.14), calls=%async_computation.1 | async-start | bytes 655360 | tf_op jit(solution)/shard_map/all_to_all | solution.py:162
  45.8 0.1 reshape.82
  45.9 7.3 %all-to-all-done.1 = f32[16,36,128]{2,1,0:T(8,128)S(1)} async-done(((f32[16,36,128]{2,1,0:T(8,128)}), f32[16,36,128]{2,1,0:T(8,128)S(1)}, u32[]{:S(2)}, u32[]{:S(2)}) %all-to-all-start.1) | async-done | bytes 294944 | tf_op jit(solution)/shard_map/all_to_all | solution.py:162
  53.3 0.2 fusion
  53.6 9.9 %collective-permute-start.1 = (f32[8,256]{1,0:T(8,128)S(1)}, f32[8,256]{1,0:T(8,128)S(1)}, u32[]{:S(2)}, u32[]{:S(2)}) collective-permute-start(f32[8,256]{1,0:T(8,128)S(1)} %constant_dynamic-slice_fusion.2), channel_id=1, source_target_pairs={{0,1},{1,0},{2,3},{3,2},{4,5},{5,4},{6,7},{7,6},{8,9},{9,8},{10,11... | collective-permute-start | bytes 24584 | tf_op jit(solution)/shard_map/ppermute | solution.py:156
  63.5 0.8 collective-permute-done.1
  64.3 18.4 %all_to_all.26 = f32[4,72,128]{2,1,0:T(8,128)S(1)} all-to-all(f32[4,72,128]{2,1,0:T(8,128)S(1)} %select_maximum_fusion.1), channel_id=1, replica_groups={{0,8,16,24},{1,9,17,25},{2,10,18,26},{3,11,19,27},{4,12,20,28},{5,13,21..., dimensions={0} | all-to-all | bytes 294912 | tf_op jit(solution)/shard_map/all_to_all | solution.py:159
  82.9 15.0 %all_to_all.27 = f32[4,192,128]{2,1,0:T(8,128)S(1)} all-to-all(f32[4,192,128]{2,1,0:T(8,128)S(1)} %select_maximum_fusion), channel_id=1, replica_groups={{0,2,4,6},{1,3,5,7},{8,10,12,14},{9,11,13,15},{16,18,20,22},{17,19,21,2..., dimensions={0} | all-to-all | bytes 786432 | tf_op jit(solution)/shard_map/all_to_all | solution.py:159
  98.2 5.0 %collective-permute-start.3 = (f32[288,256]{1,0:T(8,128)S(1)}, f32[288,256]{1,0:T(8,128)S(1)}, u32[]{:S(2)}, u32[]{:S(2)}) collective-permute-start(f32[288,256]{1,0:T(8,128)S(1)} %constant_dynamic-update-slice_fusion), channel_id=1, source_target_pairs={{0,1},{1,0},{2,3},{3,2},{4,5},{5,4},{6,7},{7,6},{8,9},{9,8},{10,11... | collective-permute-start | bytes 884744 | tf_op jit(solution)/shard_map/ppermute | solution.py:156
  103.1 0.8 broadcast_in_dim.20
  104.0 3.6 %all-to-all-start.4 = ((f32[16,64,128]{2,1,0:T(8,128)}), f32[16,64,128]{2,1,0:T(8,128)S(1)}, u32[]{:S(2)}, u32[]{:S(2)}) async-start(f32[16,64,128]{2,1,0:T(8,128)} %broadcast_in_dim.20), calls=%async_computation.4 | async-start | bytes 1048576 | tf_op jit(solution)/shard_map/all_to_all | solution.py:162
  107.6 10.1 %all-to-all-done.4 = f32[16,64,128]{2,1,0:T(8,128)S(1)} async-done(((f32[16,64,128]{2,1,0:T(8,128)}), f32[16,64,128]{2,1,0:T(8,128)S(1)}, u32[]{:S(2)}, u32[]{:S(2)}) %all-to-all-start.4) | async-done | bytes 524320 | tf_op jit(solution)/shard_map/all_to_all | solution.py:162
  117.8 4.1 %collective-permute-start.2 = (f32[16,16,128]{2,1,0:T(8,128)S(1)}, f32[16,16,128]{2,1,0:T(8,128)S(1)}, u32[]{:S(2)}, u32[]{:S(2)}) collective-permute-start(f32[16,16,128]{2,1,0:T(8,128)S(1)} %slice.95), channel_id=1, source_target_pairs={{0,1},{1,0},{2,3},{3,2},{4,5},{5,4},{6,7},{7,6},{8,9},{9,8},{10,11... | collective-permute-start | bytes 393224 | tf_op jit(solution)/shard_map/ppermute | solution.py:156
  122.0 0.1 reshape.95
  122.1 0.2 copy.23
  122.4 0.5 collective-permute-done.2
  122.9 7.8 %shard_map.42 = (f32[288,576]{1,0:T(8,128)}, f32[18,2,128]{2,1,0:T(2,128)}) custom-call(f32[2,16,16,128]{3,2,1,0:T(8,128)S(1)} %pad_maximum_fusion.2.terms_ref, f32[576,256]{1,0:T(8,128)S(1)} %bitcast.45, f32[288,256]{1,0:T(8,128)S(1)} %bitcast.46, f32[18,256]{1,0:T(8,128)S(1)} %constant_dynamic-slice_fusion.own_ref, f32[288,576]{1,0:T(8,128)} %bitcast.48), custom_call_target="tpu_custom_call" | custom-call | tf_op jit(solution)/shard_map/pallas_call | solution.py:129
  (62 shorter events, 1.2 us)
Async XLA Ops:
  0.6 11.2 %copy-start = (f32[2,128,288]{1,2,0:T(8,128)S(1)}, f32[2,128,288]{1,2,0:T(8,128)}, u32[]{:S(2)}) copy-start(f32[2,128,288]{1,2,0:T(8,128)} %param.3) | copy-start | bytes 884740
  3.1 9.9 %collective-permute-start = (f32[2,288,128]{2,1,0:T(8,128)S(1)}, f32[2,288,128]{2,1,0:T(8,128)S(1)}, u32[]{:S(2)}, u32[]{:S(2)}) collective-permute-start(f32[2,288,128]{2,1,0:T(8,128)S(1)} %get-tuple-element.7), channel_id=1, source_target_pairs={{0,1},{1,0},{2,3},{3,2},{4,5},{5,4},{6,7},{7,6},{8,9},{9,8},{10,11... | collective-permute-start | bytes 884744 | tf_op jit(solution)/shard_map/ppermute | solution.py:156
  38.8 14.4 %all-to-all-start.1 = ((f32[16,36,128]{2,1,0:T(8,128)}), f32[16,36,128]{2,1,0:T(8,128)S(1)}, u32[]{:S(2)}, u32[]{:S(2)}) async-start(f32[16,36,128]{2,1,0:T(8,128)} %broadcast_in_dim.14), calls=%async_computation.1 | async-start | bytes 655360 | tf_op jit(solution)/shard_map/all_to_all | solution.py:162
  53.6 10.7 %collective-permute-start.1 = (f32[8,256]{1,0:T(8,128)S(1)}, f32[8,256]{1,0:T(8,128)S(1)}, u32[]{:S(2)}, u32[]{:S(2)}) collective-permute-start(f32[8,256]{1,0:T(8,128)S(1)} %constant_dynamic-slice_fusion.2), channel_id=1, source_target_pairs={{0,1},{1,0},{2,3},{3,2},{4,5},{5,4},{6,7},{7,6},{8,9},{9,8},{10,11... | collective-permute-start | bytes 24584 | tf_op jit(solution)/shard_map/ppermute | solution.py:156
  98.2 9.4 %collective-permute-start.3 = (f32[288,256]{1,0:T(8,128)S(1)}, f32[288,256]{1,0:T(8,128)S(1)}, u32[]{:S(2)}, u32[]{:S(2)}) collective-permute-start(f32[288,256]{1,0:T(8,128)S(1)} %constant_dynamic-update-slice_fusion), channel_id=1, source_target_pairs={{0,1},{1,0},{2,3},{3,2},{4,5},{5,4},{6,7},{7,6},{8,9},{9,8},{10,11... | collective-permute-start | bytes 884744 | tf_op jit(solution)/shard_map/ppermute | solution.py:156
  104.0 13.8 %all-to-all-start.4 = ((f32[16,64,128]{2,1,0:T(8,128)}), f32[16,64,128]{2,1,0:T(8,128)S(1)}, u32[]{:S(2)}, u32[]{:S(2)}) async-start(f32[16,64,128]{2,1,0:T(8,128)} %broadcast_in_dim.20), calls=%async_computation.4 | async-start | bytes 1048576 | tf_op jit(solution)/shard_map/all_to_all | solution.py:162
  117.8 5.1 %collective-permute-start.2 = (f32[16,16,128]{2,1,0:T(8,128)S(1)}, f32[16,16,128]{2,1,0:T(8,128)S(1)}, u32[]{:S(2)}, u32[]{:S(2)}) collective-permute-start(f32[16,16,128]{2,1,0:T(8,128)S(1)} %slice.95), channel_id=1, source_target_pairs={{0,1},{1,0},{2,3},{3,2},{4,5},{5,4},{6,7},{7,6},{8,9},{9,8},{10,11... | collective-permute-start | bytes 393224 | tf_op jit(solution)/shard_map/ppermute | solution.py:156

commit v5 on v3

v5 whole, which is shorter than its diff:
```python
import jax
import jax.numpy as jnp
from jax import lax
from jax.experimental import pallas as pl
from jax.experimental.pallas import tpu as pltpu
from jax.sharding import PartitionSpec as P


highest = lax.Precision.HIGHEST
f32 = jnp.float32


def dot(a, b, dims=((1,), (0,))):
    return lax.dot_general(a, b, (dims, ((), ())), precision=highest, preferred_element_type=f32)


def rough(a, b):
    return jnp.dot(a.astype(jnp.bfloat16), b.astype(jnp.bfloat16), preferred_element_type=f32)


def unit(size):
    rows = lax.broadcasted_iota(jnp.int32, (size, size), 0)
    return (rows == lax.broadcasted_iota(jnp.int32, (size, size), 1)).astype(f32)


def expanded(block):
    eye = unit(block.shape[0])
    scale_col = lax.rsqrt(jnp.sum(block * eye, axis=1, keepdims=True))
    scale_row = lax.rsqrt(jnp.sum(block * eye, axis=0, keepdims=True))
    scaled = block * scale_col * scale_row
    off = scaled - eye
    step = jnp.minimum(1.0, 1.9 / (1.0 + jnp.sqrt(jnp.sum(off * off))))
    rest = eye - step * scaled
    guess = eye + rest
    rest = rough(rest, rest)
    for turn in range(3):
        more = rough(guess, rest)
        if turn < 2:
            rest = rough(rest, rest)
        guess = guess + more
    guess = guess * step
    rest = eye - dot(guess, scaled)
    miss = jnp.sum(rest * rest)
    guess = guess + rough(rest, guess)
    rest = eye - dot(guess, scaled)
    return (guess + rough(rest, guess)) * scale_col * scale_row, miss


def eliminated(block, work_ref):
    size = block.shape[0]
    lane = lax.broadcasted_iota(jnp.int32, (1, size), 1)
    line = lax.broadcasted_iota(jnp.int32, (size, 1), 0)
    work_ref[...] = block

    def sweep(at, carry):
        value = work_ref[...]
        row = work_ref[pl.ds(at, 1), :]
        here = lane == at
        col = jnp.sum(jnp.where(here, value, 0.0), axis=1, keepdims=True)
        pivot = 1.0 / jnp.sum(jnp.where(here, row, 0.0), axis=1, keepdims=True)
        row = jnp.where(here, pivot, row * pivot)
        col = jnp.where(line == at, 0.0, col)
        value = jnp.where(here, 0.0, value)
        work_ref[...] = jnp.where(line == at, row, value - col * row)
        return carry

    lax.fori_loop(0, size, sweep, 0)
    guess = work_ref[...]
    return guess + dot(unit(size) - dot(guess, block), guess)


def opening_kernel(core_ref, start_ref, lines_ref, keep_ref, send_ref):
    blocks, half, width = keep_ref.shape
    lines = jnp.concatenate([lines_ref[at] for at in range(blocks)], axis=1)
    value = dot(start_ref[...], lines, ((0,), (0,)))

    def store(low_ref, high_ref):
        for at in range(blocks):
            low_ref[at] = value[:half, at * width : (at + 1) * width]
            high_ref[at] = value[half:, at * width : (at + 1) * width]

    pl.when(core_ref[0] == 0)(lambda: store(keep_ref, send_ref))
    pl.when(core_ref[0] != 0)(lambda: store(send_ref, keep_ref))


def opening(core, start, lines):
    blocks, _, width = lines.shape
    in_vmem = pl.BlockSpec(memory_space=pltpu.VMEM)
    return pl.pallas_call(
        opening_kernel,
        out_shape=[pltpu.VMEM((blocks, start.shape[1] // 2, width), f32)] * 2,
        in_specs=[pl.BlockSpec(memory_space=pltpu.SMEM), in_vmem, in_vmem],
    )(core.reshape(1), start, lines)


def closing_kernel(terms_ref, rows_ref, cols_ref, own_ref, start_ref, out_ref, gain_ref, work_ref):
    depth = terms_ref.shape[1]
    step = terms_ref.shape[2] // 2
    width = work_ref.shape[0]

    def block(high, right):
        part = terms_ref[:, high * depth // 2 : (high + 1) * depth // 2, right * step : (right + 1) * step]
        return jnp.transpose(part, (1, 0, 2, 3)).reshape(width, width)

    def solve(inverse):
        first, miss = inverse(block(0, 0) + unit(width))
        cross = block(0, 1)
        carry = dot(first, cross)
        last, more = inverse(block(1, 1) + unit(width) - dot(cross, carry, ((0,), (0,))))
        both = jnp.concatenate([first, carry], axis=1)

        def gains(ref):
            value = dot(ref[:, :width], both)
            return value[:, :width], dot(ref[:, width:] - value[:, width:], last)

        gain_ref[:, 0], gain_ref[:, 1] = gains(own_ref)
        low, high = gains(cols_ref)
        low = low - dot(high, carry, ((1,), (1,)))
        out_ref[...] = start_ref[...] - dot(jnp.concatenate([low, high], axis=1), rows_ref[...], ((1,), (1,)))
        return miss + more

    miss = solve(expanded)

    @pl.when(jnp.logical_not(miss < 1e-2))
    def _():
        solve(lambda value: (eliminated(value, work_ref), 0.0))


def closing(*operands):
    own, start = operands[3:]
    width = own.shape[1] // 2
    in_vmem = pl.BlockSpec(memory_space=pltpu.VMEM)
    return pl.pallas_call(
        closing_kernel,
        out_shape=[
            jax.ShapeDtypeStruct(start.shape, f32),
            jax.ShapeDtypeStruct((own.shape[0], 2, width), f32),
        ],
        in_specs=[in_vmem] * len(operands),
        scratch_shapes=[pltpu.VMEM((width, width), f32)],
    )(*(pltpu.with_memory_space_constraint(x, pltpu.VMEM) for x in operands))


def shards(kron_inverse, activations):
    rows, cols = kron_inverse.shape
    blocks, width = activations.shape[:2]
    wide = blocks * width
    planes = lax.axis_size("row")
    devices = lax.axis_size("col")
    depth = devices // 2
    row = lax.axis_index("row")
    col = lax.axis_index("col")
    lines = [[2 * z + k for z in range(depth)] for k in range(2)]

    def from_partner(value):
        return lax.ppermute(value, "col", [(at, at ^ 1) for at in range(devices)])

    def over_z(value):
        return lax.all_to_all(value, "col", 0, 0, tiled=True, axis_index_groups=lines)

    def over_plane(value):
        return lax.all_to_all(value, "row", 0, 0, tiled=True)

    def copies(value, count):
        return jnp.broadcast_to(value[None], (count, *value.shape))

    half = rows // 2
    share = half // depth
    slab = wide // planes

    def whole(value):
        left = value[:, :share].reshape(half, width)
        return jnp.concatenate([left, value[:, share:].reshape(half, width)], axis=1)

    spare = -slab * share % (4 * width)
    core = col % 2
    keep, send = opening(core, kron_inverse.T, activations.transpose(0, 2, 1))
    summed = keep + from_partner(send)
    mine = lax.dynamic_slice_in_dim(activations.reshape(wide, cols), row * slab, slab, 0)
    mine = mine.reshape(slab, depth, share).transpose(1, 0, 2).reshape(depth, slab * share)
    mine = jnp.pad(mine, ((0, 0), (0, spare))).reshape(depth, -1, width)
    parts = [summed[at].reshape(depth, share, width) for at in range(blocks)]
    got = over_z(jnp.concatenate([*parts, mine], axis=1))
    piece = jnp.sum(got[:, : blocks * share], axis=0)
    theirs = got[:, blocks * share :].reshape(depth, slab * share + spare)[:, : slab * share]
    theirs = theirs.reshape(depth, slab, share).transpose(1, 0, 2).reshape(slab, depth * share)
    again = lax.optimization_barrier(piece)
    level = over_plane(copies(piece, planes))
    terms = dot(theirs, whole(level))
    other = lax.dynamic_slice_in_dim(terms, (1 - core) * (slab // 2), slab // 2, 0)
    terms = lax.dynamic_slice_in_dim(terms, core * (slab // 2), slab // 2, 0) + from_partner(other)
    terms = jnp.concatenate([terms[:, :width], terms[:, width:]], axis=0)
    cut = -(-blocks * share // planes)
    users = blocks * share // cut
    part = lax.dynamic_slice_in_dim(level, jnp.minimum(row, users - 1) * cut, cut, 1)
    line = over_z(jnp.concatenate([copies(terms, depth), copies(again, depth), part], axis=1))
    terms = jnp.sum(line[:, :slab], axis=0)
    row_half = whole(line[:, slab : slab + blocks * share])
    part = line[:, slab + blocks * share :].reshape(depth * cut, width)
    disc = over_plane(copies(jnp.concatenate([terms, part], axis=0), planes))
    row_other = from_partner(row_half)

    def in_order(value, other):
        low = jnp.where(core == 0, value, other)
        return jnp.stack([low, jnp.where(core == 0, other, value)])

    row_terms = in_order(row_half, row_other).reshape(rows, wide)
    own = rows // devices
    own_terms = lax.dynamic_slice_in_dim(row_terms, col * own, own, 0)
    terms = disc[:, :slab]
    terms = in_order(terms, from_partner(terms))
    col_terms = disc[:users, slab:].reshape(blocks, users // blocks, depth, cut, width)
    col_terms = col_terms.transpose(2, 1, 3, 0, 4).reshape(half, wide)
    updated, gains = closing(terms, row_terms, col_terms, own_terms, kron_inverse.T)
    return updated.T, gains.transpose(1, 0, 2)


def solution(mesh):
    return jax.shard_map(
        shards,
        mesh=mesh,
        in_specs=(P("row", "col"), P(None, None, "col")),
        out_specs=(P("row", "col"), P(None, ("row", "col"), None)),
        check_vma=False,
    )
```

time: 133 us -> 127 us (0.955)
  matrix products: 4.78 us -> 0.21 us
  other arithmetic: 2 us -> 0.29 us
    dot_general x3 -> x1, matrix products: 4.78 us -> 0.21 us  [dot(): lax.dot_general(a, b, (dims, ((), ())), precision=highest, preferred_elem...]
    pallas_call x0 -> x1, Pallas kernels: none -> 2.46 us  [opening(): pl.pallas_call(opening_kernel, out_shape=[pltpu.VMEM((blocks, start.shape...]
    pallas_call x1, Pallas kernels: 8.13 us -> 6.4 us  [closing(): pl.pallas_call(closing_kernel, out_shape=[jax.ShapeDtypeStruct(start.shap...]
  transfers between devices with their start and end apart: 6 -> 6, of which waited for: 4 -> 5; matrix products, arithmetic and copies ran while one was open for 3% -> 2% of each run, Pallas kernels for 0% -> 0%
where the time goes in v5:
time: 127 us
  blocking collectives  51.3 us (40%)
  starting transfers between devices  41.9 us (33%)
  waiting for transfers between devices  19.3 us (15%)
  Pallas kernels  8.86 us (7%)
  local copies, waits for them, and re-layouts  3.69 us (3%)
    all_to_all x2, blocking collectives, over_z(): lax.all_to_all(value, 'col', 0, 0, tiled=True, axis_index_groups=lines)  51.3 us
    ppermute x4, starting transfers between devices, from_partner(): return lax.ppermute(value, 'col', [(at, at ^ 1) for at in range(devices)])  31.6 us
    all_to_all x2, waiting for transfers between devices, over_plane(): return lax.all_to_all(value, 'row', 0, 0, tiled=True)  17.5 us
    all_to_all x2, starting transfers between devices, over_plane(): return lax.all_to_all(value, 'row', 0, 0, tiled=True)  10.3 us
    pallas_call x1, Pallas kernels, closing(): pl.pallas_call(closing_kernel, out_shape=[jax.ShapeDtypeStruct(start.shap...  6.4 us
  transfers between devices with their start and end apart: 6, of which 5 were waited for; matrix products, arithmetic and copies ran while one was open for 2% of the time, Pallas kernels for 0%

profile of v5, /device:TPU:1, one launch (start us, length us, event | category | flops | bytes accessed | tf_op | source)
XLA Modules:
  0.0 126.7 jit_solution(8329111004482589478)
XLA Ops:
  0.7 2.5 %shard_map.41 = (f32[2,288,128]{2,1,0:T(8,128)S(1)}, f32[2,288,128]{2,1,0:T(8,128)S(1)}) custom-call(s32[1]{0:T(128)} %bitcast.core_ref, f32[288,576]{1,0:T(8,128)} %bitcast.32, f32[2,288,128]{2,1,0:T(8,128)} %bitcast.38), custom_call_target="tpu_custom_call" | custom-call | tf_op jit(solution)/shard_map/pallas_call | solution.py:89
  3.1 8.7 %collective-permute-start = (f32[2,288,128]{2,1,0:T(8,128)S(1)}, f32[2,288,128]{2,1,0:T(8,128)S(1)}, u32[]{:S(2)}, u32[]{:S(2)}) collective-permute-start(f32[2,288,128]{2,1,0:T(8,128)S(1)} %get-tuple-element.7), channel_id=1, source_target_pairs={{0,1},{1,0},{2,3},{3,2},{4,5},{5,4},{6,7},{7,6},{8,9},{9,8},{10,11... | collective-permute-start | bytes 884744 | tf_op jit(solution)/shard_map/ppermute | solution.py:156
  12.1 0.1 reshape.58
  12.3 0.1 reshape.59
  12.4 0.6 collective-permute-done
  13.2 24.8 %all_to_all.20 = f32[16,40,128]{2,1,0:T(8,128)S(1)} all-to-all(f32[16,40,128]{2,1,0:T(8,128)S(1)} %pad_maximum_fusion.2), channel_id=1, replica_groups={{0,2,4,6,8,10,12,14,16,18,20,22,24,26,28,30},{1,3,5,7,9,11,13,15,17,19,..., dimensions={0} | all-to-all | bytes 655360 | tf_op jit(solution)/shard_map/all_to_all | solution.py:159
  38.1 0.7 broadcast_in_dim.8
  38.8 6.8 %all-to-all-start.1 = ((f32[16,36,128]{2,1,0:T(8,128)}), f32[16,36,128]{2,1,0:T(8,128)S(1)}, u32[]{:S(2)}, u32[]{:S(2)}) async-start(f32[16,36,128]{2,1,0:T(8,128)} %broadcast_in_dim.8), calls=%async_computation.1 | async-start | bytes 655360 | tf_op jit(solution)/shard_map/all_to_all | solution.py:162
  45.8 0.1 reshape.63
  45.9 7.3 %all-to-all-done.1 = f32[16,36,128]{2,1,0:T(8,128)S(1)} async-done(((f32[16,36,128]{2,1,0:T(8,128)}), f32[16,36,128]{2,1,0:T(8,128)S(1)}, u32[]{:S(2)}, u32[]{:S(2)}) %all-to-all-start.1) | async-done | bytes 294944 | tf_op jit(solution)/shard_map/all_to_all | solution.py:162
  53.3 0.2 fusion
  53.6 9.9 %collective-permute-start.1 = (f32[8,256]{1,0:T(8,128)S(1)}, f32[8,256]{1,0:T(8,128)S(1)}, u32[]{:S(2)}, u32[]{:S(2)}) collective-permute-start(f32[8,256]{1,0:T(8,128)S(1)} %constant_dynamic-slice_fusion.2), channel_id=1, source_target_pairs={{0,1},{1,0},{2,3},{3,2},{4,5},{5,4},{6,7},{7,6},{8,9},{9,8},{10,11... | collective-permute-start | bytes 24584 | tf_op jit(solution)/shard_map/ppermute | solution.py:156
  63.5 0.8 collective-permute-done.1
  64.4 26.5 %all_to_all.21 = f32[16,55,128]{2,1,0:T(8,128)S(1)} all-to-all(f32[16,55,128]{2,1,0:T(8,128)S(1)} %pad_maximum_fusion.1), channel_id=1, replica_groups={{0,2,4,6,8,10,12,14,16,18,20,22,24,26,28,30},{1,3,5,7,9,11,13,15,17,19,..., dimensions={0} | all-to-all | bytes 901120 | tf_op jit(solution)/shard_map/all_to_all | solution.py:159
  91.1 8.9 %collective-permute-start.3 = (f32[288,256]{1,0:T(8,128)S(1)}, f32[288,256]{1,0:T(8,128)S(1)}, u32[]{:S(2)}, u32[]{:S(2)}) collective-permute-start(f32[288,256]{1,0:T(8,128)S(1)} %constant_dynamic-update-slice_fusion), channel_id=1, source_target_pairs={{0,1},{1,0},{2,3},{3,2},{4,5},{5,4},{6,7},{7,6},{8,9},{9,8},{10,11... | collective-permute-start | bytes 884744 | tf_op jit(solution)/shard_map/ppermute | solution.py:156
  100.0 0.8 broadcast_in_dim.11
  100.8 3.6 %all-to-all-start.3 = ((f32[16,64,128]{2,1,0:T(8,128)}), f32[16,64,128]{2,1,0:T(8,128)S(1)}, u32[]{:S(2)}, u32[]{:S(2)}) async-start(f32[16,64,128]{2,1,0:T(8,128)} %broadcast_in_dim.11), calls=%async_computation.3 | async-start | bytes 1048576 | tf_op jit(solution)/shard_map/all_to_all | solution.py:162
  104.5 10.1 %all-to-all-done.3 = f32[16,64,128]{2,1,0:T(8,128)S(1)} async-done(((f32[16,64,128]{2,1,0:T(8,128)}), f32[16,64,128]{2,1,0:T(8,128)S(1)}, u32[]{:S(2)}, u32[]{:S(2)}) %all-to-all-start.3) | async-done | bytes 524320 | tf_op jit(solution)/shard_map/all_to_all | solution.py:162
  114.6 4.1 %collective-permute-start.2 = (f32[16,16,128]{2,1,0:T(8,128)S(1)}, f32[16,16,128]{2,1,0:T(8,128)S(1)}, u32[]{:S(2)}, u32[]{:S(2)}) collective-permute-start(f32[16,16,128]{2,1,0:T(8,128)S(1)} %slice.74), channel_id=1, source_target_pairs={{0,1},{1,0},{2,3},{3,2},{4,5},{5,4},{6,7},{7,6},{8,9},{9,8},{10,11... | collective-permute-start | bytes 393224 | tf_op jit(solution)/shard_map/ppermute | solution.py:156
  118.8 0.1 reshape.70
  119.0 0.2 copy.12
  119.2 0.5 collective-permute-done.2
  119.8 0.6 copy-done
  120.3 6.4 %shard_map.42 = (f32[288,576]{1,0:T(8,128)}, f32[18,2,128]{2,1,0:T(2,128)}) custom-call(f32[2,16,16,128]{3,2,1,0:T(8,128)S(1)} %pad_maximum_fusion.3.terms_ref, f32[576,256]{1,0:T(8,128)S(1)} %bitcast.35, f32[288,256]{1,0:T(8,128)S(1)} %bitcast.36, f32[18,256]{1,0:T(8,128)S(1)} %constant_dynamic-slice_fusion.own_ref, f32[288,576]{1,0:T(8,128)S(1)} %bitcast.33), custom_call_target="tpu_custom_call" | custom-call | tf_op jit(solution)/shard_map/pallas_call | solution.py:133
  (49 shorter events, 1.1 us)
Async XLA Ops:
  0.6 11.2 %copy-start.1 = (f32[2,128,288]{1,2,0:T(8,128)S(1)}, f32[2,128,288]{1,2,0:T(8,128)}, u32[]{:S(2)}) copy-start(f32[2,128,288]{1,2,0:T(8,128)} %param.3) | copy-start | bytes 884740
  3.1 9.9 %collective-permute-start = (f32[2,288,128]{2,1,0:T(8,128)S(1)}, f32[2,288,128]{2,1,0:T(8,128)S(1)}, u32[]{:S(2)}, u32[]{:S(2)}) collective-permute-start(f32[2,288,128]{2,1,0:T(8,128)S(1)} %get-tuple-element.7), channel_id=1, source_target_pairs={{0,1},{1,0},{2,3},{3,2},{4,5},{5,4},{6,7},{7,6},{8,9},{9,8},{10,11... | collective-permute-start | bytes 884744 | tf_op jit(solution)/shard_map/ppermute | solution.py:156
  38.8 14.4 %all-to-all-start.1 = ((f32[16,36,128]{2,1,0:T(8,128)}), f32[16,36,128]{2,1,0:T(8,128)S(1)}, u32[]{:S(2)}, u32[]{:S(2)}) async-start(f32[16,36,128]{2,1,0:T(8,128)} %broadcast_in_dim.8), calls=%async_computation.1 | async-start | bytes 655360 | tf_op jit(solution)/shard_map/all_to_all | solution.py:162
  53.6 10.7 %collective-permute-start.1 = (f32[8,256]{1,0:T(8,128)S(1)}, f32[8,256]{1,0:T(8,128)S(1)}, u32[]{:S(2)}, u32[]{:S(2)}) collective-permute-start(f32[8,256]{1,0:T(8,128)S(1)} %constant_dynamic-slice_fusion.2), channel_id=1, source_target_pairs={{0,1},{1,0},{2,3},{3,2},{4,5},{5,4},{6,7},{7,6},{8,9},{9,8},{10,11... | collective-permute-start | bytes 24584 | tf_op jit(solution)/shard_map/ppermute | solution.py:156
  91.1 13.4 %collective-permute-start.3 = (f32[288,256]{1,0:T(8,128)S(1)}, f32[288,256]{1,0:T(8,128)S(1)}, u32[]{:S(2)}, u32[]{:S(2)}) collective-permute-start(f32[288,256]{1,0:T(8,128)S(1)} %constant_dynamic-update-slice_fusion), channel_id=1, source_target_pairs={{0,1},{1,0},{2,3},{3,2},{4,5},{5,4},{6,7},{7,6},{8,9},{9,8},{10,11... | collective-permute-start | bytes 884744 | tf_op jit(solution)/shard_map/ppermute | solution.py:156
  100.8 13.8 %all-to-all-start.3 = ((f32[16,64,128]{2,1,0:T(8,128)}), f32[16,64,128]{2,1,0:T(8,128)S(1)}, u32[]{:S(2)}, u32[]{:S(2)}) async-start(f32[16,64,128]{2,1,0:T(8,128)} %broadcast_in_dim.11), calls=%async_computation.3 | async-start | bytes 1048576 | tf_op jit(solution)/shard_map/all_to_all | solution.py:162
  114.6 5.1 %collective-permute-start.2 = (f32[16,16,128]{2,1,0:T(8,128)S(1)}, f32[16,16,128]{2,1,0:T(8,128)S(1)}, u32[]{:S(2)}, u32[]{:S(2)}) collective-permute-start(f32[16,16,128]{2,1,0:T(8,128)S(1)} %slice.74), channel_id=1, source_target_pairs={{0,1},{1,0},{2,3},{3,2},{4,5},{5,4},{6,7},{7,6},{8,9},{9,8},{10,11... | collective-permute-start | bytes 393224 | tf_op jit(solution)/shard_map/ppermute | solution.py:156
  119.2 1.1 copy-start

commit v6 on v5

--- a/solution.py
+++ b/solution.py
@@ -93,20 +93,90 @@
     )(core.reshape(1), start, lines)
 
 
-def closing_kernel(terms_ref, rows_ref, cols_ref, own_ref, start_ref, out_ref, gain_ref, work_ref):
-    depth = terms_ref.shape[1]
-    step = terms_ref.shape[2] // 2
+def spread_kernel(got_ref, out_ref):
+    piece = jnp.sum(got_ref[:, : out_ref.shape[1]], axis=0)
+    for at in range(out_ref.shape[0]):
+        out_ref[at] = piece
+
+
+def spread(got, planes, held):
+    return pl.pallas_call(
+        spread_kernel,
+        out_shape=pltpu.VMEM((planes, held, got.shape[2]), f32),
+        in_specs=[pl.BlockSpec(memory_space=pltpu.VMEM)],
+    )(pltpu.with_memory_space_constraint(got, pltpu.VMEM))
+
+
+def slab_kernel(row_ref, got_ref, level_ref, send_ref, right_ref):
+    depth, held, width = level_ref.shape
+    share = held // 2
+    tall = right_ref.shape[1]
+    row = row_ref[0]
+    slab = 2 * width // depth
+    groups = width // slab
+    packed = got_ref[:, held : held + tall // groups, :]
+    packed = jnp.broadcast_to(packed[:, :, None, :], (depth, tall // groups, groups, width))
+    packed = pltpu.roll(packed.reshape(depth * tall, width), slab, 1, stride=slab, stride_axis=0)
+    right_ref[...] = jnp.zeros(right_ref.shape, f32)
+    right_ref[:, :share, :width] = level_ref[:, :share, :]
+    right_ref[:, :share, width:] = level_ref[:, share:, :]
+    terms = dot(packed[:, :slab], right_ref[...].reshape(depth * tall, 2 * width), ((0,), (0,)))
+    terms = pltpu.roll(terms, jnp.where(row == 0, 0, 2 * width - slab * row), 1)
+    lane = lax.broadcasted_iota(jnp.int32, (slab, width), 1)
+    block = jnp.where(lane < slab, terms[:, width:], 0.0)
+    turned = jnp.concatenate([block, jnp.zeros((width - slab, width), f32)], axis=0).T
+    block = jnp.where(row < depth // 2, block[: slab // 2], turned[slab // 2 : slab])
+    block = jnp.concatenate([block[at : at + 1] for at in reversed(range(slab // 2))], axis=0)
+    block = jnp.sum(pltpu.roll(block, 0, 1, stride=slab, stride_axis=0), axis=0, keepdims=True)
+    piece = level_ref[row]
+    cut = send_ref.shape[1] - slab - held - 1
+    part = level_ref[:, pl.ds(jnp.minimum(row, held // cut - 1) * cut, cut), :]
+    for at in range(depth):
+        send_ref[at, :slab] = terms[:, :width]
+        send_ref[at, slab : slab + held] = piece
+        send_ref[at, slab + held : slab + held + cut] = part[at]
+        send_ref[at, slab + held + cut :] = block
+
+
+def slab_terms(row, got, level, cut):
+    depth, held, width = level.shape
+    slab = 2 * width // depth
+    tall = -(-held // 2 // 8) * 8
+    in_vmem = pl.BlockSpec(memory_space=pltpu.VMEM)
+    return pl.pallas_call(
+        slab_kernel,
+        out_shape=pltpu.VMEM((depth, slab + held + cut + 1, width), f32),
+        in_specs=[pl.BlockSpec(memory_space=pltpu.SMEM), in_vmem, in_vmem],
+        scratch_shapes=[pltpu.VMEM((depth, tall, 2 * width), f32)],
+    )(row.reshape(1), *(pltpu.with_memory_space_constraint(x, pltpu.VMEM) for x in (got, level)))
+
+
+def closing_kernel(mine_ref, other_ref, rows_ref, cols_ref, own_ref, start_ref, out_ref, gain_ref, work_ref):
     width = work_ref.shape[0]
-
-    def block(high, right):
-        part = terms_ref[:, high * depth // 2 : (high + 1) * depth // 2, right * step : (right + 1) * step]
-        return jnp.transpose(part, (1, 0, 2, 3)).reshape(width, width)
+    slab = mine_ref.shape[0] - 2 * width
+    groups = width // slab
+    terms = mine_ref[...] + other_ref[...]
+
+    far = [terms[2 * width + n + m : 2 * width + n + m + 1] for n in range(groups) for m in (0, groups)]
+    far = jnp.concatenate([jnp.broadcast_to(part, (slab // 2, width)) for part in far], axis=0)
+    far = pltpu.roll(far, slab, 1, stride=slab, stride_axis=0)
+
+    def stepped(value):
+        parts = [value[n * slab : (n + 1) * slab] for n in range(groups)]
+        return jnp.concatenate([pltpu.roll(part, n * slab, 1) if n else part for n, part in enumerate(parts)], axis=0)
+
+    across = lax.broadcasted_iota(jnp.int32, (width, width), 1) // slab
+    down = lax.broadcasted_iota(jnp.int32, (width, width), 0) // slab
+    upper, lower, far = stepped(terms[:width]), stepped(terms[width : 2 * width]), stepped(far)
+    upper_turned, lower_turned = upper.T, lower.T
+    cross = jnp.where(across < down, upper, jnp.where(across > down, lower_turned, far))
+    upper = jnp.where(across >= down, upper, upper_turned) + unit(width)
+    lower = jnp.where(across >= down, lower, lower_turned) + unit(width)
 
     def solve(inverse):
-        first, miss = inverse(block(0, 0) + unit(width))
-        cross = block(0, 1)
+        first, miss = inverse(upper)
         carry = dot(first, cross)
-        last, more = inverse(block(1, 1) + unit(width) - dot(cross, carry, ((0,), (0,))))
+        last, more = inverse(lower - dot(cross, carry, ((0,), (0,))))
         both = jnp.concatenate([first, carry], axis=1)
 
         def gains(ref):
@@ -127,7 +197,7 @@
 
 
 def closing(*operands):
-    own, start = operands[3:]
+    own, start = operands[4:]
     width = own.shape[1] // 2
     in_vmem = pl.BlockSpec(memory_space=pltpu.VMEM)
     return pl.pallas_call(
@@ -172,32 +242,26 @@
         left = value[:, :share].reshape(half, width)
         return jnp.concatenate([left, value[:, share:].reshape(half, width)], axis=1)
 
-    spare = -slab * share % (4 * width)
     core = col % 2
-    keep, send = opening(core, kron_inverse.T, activations.transpose(0, 2, 1))
+    turned = activations.transpose(0, 2, 1)
+    keep, send = opening(core, kron_inverse.T, turned)
     summed = keep + from_partner(send)
-    mine = lax.dynamic_slice_in_dim(activations.reshape(wide, cols), row * slab, slab, 0)
-    mine = mine.reshape(slab, depth, share).transpose(1, 0, 2).reshape(depth, slab * share)
-    mine = jnp.pad(mine, ((0, 0), (0, spare))).reshape(depth, -1, width)
+    groups = width // slab
+    mine = lax.dynamic_slice(turned, (row // groups, 0, row % groups * slab), (1, cols, slab))
+    mine = jnp.pad(mine.reshape(depth, share, slab), ((0, 0), (0, -share % groups), (0, 0)))
+    mine = jnp.flip(mine.reshape(depth, -1, groups, slab), 2).reshape(depth, -1, width)
     parts = [summed[at].reshape(depth, share, width) for at in range(blocks)]
     got = over_z(jnp.concatenate([*parts, mine], axis=1))
-    piece = jnp.sum(got[:, : blocks * share], axis=0)
-    theirs = got[:, blocks * share :].reshape(depth, slab * share + spare)[:, : slab * share]
-    theirs = theirs.reshape(depth, slab, share).transpose(1, 0, 2).reshape(slab, depth * share)
-    again = lax.optimization_barrier(piece)
-    level = over_plane(copies(piece, planes))
-    terms = dot(theirs, whole(level))
-    other = lax.dynamic_slice_in_dim(terms, (1 - core) * (slab // 2), slab // 2, 0)
-    terms = lax.dynamic_slice_in_dim(terms, core * (slab // 2), slab // 2, 0) + from_partner(other)
-    terms = jnp.concatenate([terms[:, :width], terms[:, width:]], axis=0)
-    cut = -(-blocks * share // planes)
-    users = blocks * share // cut
-    part = lax.dynamic_slice_in_dim(level, jnp.minimum(row, users - 1) * cut, cut, 1)
-    line = over_z(jnp.concatenate([copies(terms, depth), copies(again, depth), part], axis=1))
+    held = blocks * share
+    level = over_plane(spread(got, planes, held))
+    cut = -(-held // planes)
+    users = held // cut
+    line = over_z(slab_terms(row, got, level, cut))
+    row_half = whole(line[:, slab : slab + held])
     terms = jnp.sum(line[:, :slab], axis=0)
-    row_half = whole(line[:, slab : slab + blocks * share])
-    part = line[:, slab + blocks * share :].reshape(depth * cut, width)
-    disc = over_plane(copies(jnp.concatenate([terms, part], axis=0), planes))
+    far = jnp.sum(line[:, slab + held + cut :], axis=0)
+    part = line[:, slab + held : slab + held + cut].reshape(depth * cut, width)
+    disc = over_plane(copies(jnp.concatenate([terms, part, far], axis=0), planes))
     row_other = from_partner(row_half)
 
     def in_order(value, other):
@@ -207,11 +271,11 @@
     row_terms = in_order(row_half, row_other).reshape(rows, wide)
     own = rows // devices
     own_terms = lax.dynamic_slice_in_dim(row_terms, col * own, own, 0)
-    terms = disc[:, :slab]
-    terms = in_order(terms, from_partner(terms))
-    col_terms = disc[:users, slab:].reshape(blocks, users // blocks, depth, cut, width)
+    terms = jnp.concatenate([disc[:, :slab].reshape(wide, width), disc[:, slab + depth * cut]], axis=0)
+    other = from_partner(terms)
+    col_terms = disc[:users, slab : slab + depth * cut].reshape(blocks, users // blocks, depth, cut, width)
     col_terms = col_terms.transpose(2, 1, 3, 0, 4).reshape(half, wide)
-    updated, gains = closing(terms, row_terms, col_terms, own_terms, kron_inverse.T)
+    updated, gains = closing(terms, other, row_terms, col_terms, own_terms, kron_inverse.T)
     return updated.T, gains.transpose(1, 0, 2)
 
 

time: 127 us -> 121 us (0.953)
  blocking collectives: 51.3 us -> 70.4 us
  starting transfers between devices: 41.9 us -> 25.6 us
  waiting for transfers between devices: 19.3 us -> 12 us
  local copies, waits for them, and re-layouts: 3.69 us -> 2.09 us
    all_to_all x0 -> x1, blocking collectives: none -> 14.2 us  [over_plane(): return lax.all_to_all(value, 'row', 0, 0, tiled=True)]
    ppermute x4 -> x3, starting transfers between devices: 31.6 us -> 21.8 us  [from_partner(): return lax.ppermute(value, 'col', [(at, at ^ 1) for at in range(devices)])]
    all_to_all x2 -> x1, waiting for transfers between devices: 17.5 us -> 10.7 us  [over_plane(): return lax.all_to_all(value, 'row', 0, 0, tiled=True)]
    all_to_all x2 -> x1, starting transfers between devices: 10.3 us -> 3.79 us  [over_plane(): return lax.all_to_all(value, 'row', 0, 0, tiled=True)]
    all_to_all x2, blocking collectives: 51.3 us -> 56.1 us  [over_z(): lax.all_to_all(value, 'col', 0, 0, tiled=True, axis_index_groups=lines)]
  transfers between devices with their start and end apart: 6 -> 4, of which waited for: 5 -> 3; matrix products, arithmetic and copies ran while one was open for 2% -> 1% of each run, Pallas kernels for 0% -> 0%
where the time goes in v6:
time: 121 us
  blocking collectives  70.4 us (58%)
  starting transfers between devices  25.6 us (21%)
  waiting for transfers between devices  12 us (10%)
  Pallas kernels  9.64 us (8%)
  local copies, waits for them, and re-layouts  2.09 us (2%)
    all_to_all x2, blocking collectives, over_z(): lax.all_to_all(value, 'col', 0, 0, tiled=True, axis_index_groups=lines)  56.1 us
    ppermute x3, starting transfers between devices, from_partner(): return lax.ppermute(value, 'col', [(at, at ^ 1) for at in range(devices)])  21.8 us
    all_to_all x1, blocking collectives, over_plane(): return lax.all_to_all(value, 'row', 0, 0, tiled=True)  14.2 us
    all_to_all x1, waiting for transfers between devices, over_plane(): return lax.all_to_all(value, 'row', 0, 0, tiled=True)  10.7 us
    pallas_call x1, Pallas kernels, closing(): pl.pallas_call(closing_kernel, out_shape=[jax.ShapeDtypeStruct(start.shap...  6.53 us
    all_to_all x1, starting transfers between devices, over_plane(): return lax.all_to_all(value, 'row', 0, 0, tiled=True)  3.79 us
    pallas_call x1, Pallas kernels, opening(): pl.pallas_call(opening_kernel, out_shape=[pltpu.VMEM((blocks, start.shape...  2.46 us
  transfers between devices with their start and end apart: 4, of which 3 were waited for; matrix products, arithmetic and copies ran while one was open for 1% of the time, Pallas kernels for 0%

profile of v6, /device:TPU:1, one launch (start us, length us, event | category | flops | bytes accessed | tf_op | source)
XLA Modules:
  0.0 120.9 jit_solution(5978251189114654041)
XLA Ops:
  0.6 0.0 copy-start.1
  0.7 2.5 %shard_map.41 = (f32[2,288,128]{2,1,0:T(8,128)S(1)}, f32[2,288,128]{2,1,0:T(8,128)S(1)}) custom-call(s32[1]{0:T(128)} %bitcast.1.core_ref, f32[288,576]{1,0:T(8,128)} %bitcast.28, f32[2,288,128]{2,1,0:T(8,128)} %bitcast.35), custom_call_target="tpu_custom_call" | custom-call | tf_op jit(solution)/shard_map/pallas_call | solution.py:89
  3.1 8.7 %collective-permute-start = (f32[2,288,128]{2,1,0:T(8,128)S(1)}, f32[2,288,128]{2,1,0:T(8,128)S(1)}, u32[]{:S(2)}, u32[]{:S(2)}) collective-permute-start(f32[2,288,128]{2,1,0:T(8,128)S(1)} %get-tuple-element.7), channel_id=1, source_target_pairs={{0,1},{1,0},{2,3},{3,2},{4,5},{5,4},{6,7},{7,6},{8,9},{9,8},{10,11... | collective-permute-start | bytes 884744 | tf_op jit(solution)/shard_map/ppermute | solution.py:226
  11.9 0.0 copy-done.1
  11.9 0.1 dynamic-slice_bitcast_fusion
  12.1 0.1 reshape.54
  12.2 0.8 collective-permute-done
  13.2 24.8 %all_to_all.20.got_ref = f32[16,39,128]{2,1,0:T(8,128)S(1)} all-to-all(f32[16,39,128]{2,1,0:T(8,128)S(1)} %pad_maximum_fusion.1), channel_id=1, replica_groups={{0,2,4,6,8,10,12,14,16,18,20,22,24,26,28,30},{1,3,5,7,9,11,13,15,17,19,..., dimensions={0} | all-to-all | bytes 638976 | tf_op jit(solution)/shard_map/all_to_all | solution.py:229
  38.1 14.2 %all_to_all.21.level_ref = f32[16,36,128]{2,1,0:T(8,128)S(1)} all-to-all(f32[16,36,128]{2,1,0:T(8,128)S(1)} %shard_map.42), channel_id=1, replica_groups=mesh['row'=16,'col'=32] {'row'}, dimensions={0} | all-to-all | bytes 589824 | tf_op jit(solution)/shard_map/all_to_all | solution.py:232
  52.3 0.6 shard_map.43
  52.9 31.3 %all_to_all.22 = f32[16,56,128]{2,1,0:T(8,128)S(1)} all-to-all(f32[16,56,128]{2,1,0:T(8,128)S(1)} %shard_map.43), channel_id=1, replica_groups={{0,2,4,6,8,10,12,14,16,18,20,22,24,26,28,30},{1,3,5,7,9,11,13,15,17,19,..., dimensions={0} | all-to-all | bytes 917504 | tf_op jit(solution)/shard_map/all_to_all | solution.py:229
  84.4 8.7 %collective-permute-start.2 = (f32[288,256]{1,0:T(8,128)S(1)}, f32[288,256]{1,0:T(8,128)S(1)}, u32[]{:S(2)}, u32[]{:S(2)}) collective-permute-start(f32[288,256]{1,0:T(8,128)S(1)} %constant_dynamic-update-slice_fusion), channel_id=1, source_target_pairs={{0,1},{1,0},{2,3},{3,2},{4,5},{5,4},{6,7},{7,6},{8,9},{9,8},{10,11... | collective-permute-start | bytes 884744 | tf_op jit(solution)/shard_map/ppermute | solution.py:226
  93.2 0.9 broadcast_in_dim.2
  94.1 3.8 %all-to-all-start.3 = ((f32[16,65,128]{2,1,0:T(8,128)}), f32[16,65,128]{2,1,0:T(8,128)S(1)}, u32[]{:S(2)}, u32[]{:S(2)}) async-start(f32[16,65,128]{2,1,0:T(8,128)} %broadcast_in_dim.2), calls=%async_computation.3 | async-start | bytes 1179648 | tf_op jit(solution)/shard_map/all_to_all | solution.py:232
  97.9 0.0 collective-permute-done.2
  97.9 10.7 %all-to-all-done.3 = f32[16,65,128]{2,1,0:T(8,128)S(1)} async-done(((f32[16,65,128]{2,1,0:T(8,128)}), f32[16,65,128]{2,1,0:T(8,128)S(1)}, u32[]{:S(2)}, u32[]{:S(2)}) %all-to-all-start.3) | async-done | bytes 532512 | tf_op jit(solution)/shard_map/all_to_all | solution.py:232
  108.6 4.4 %collective-permute-start.1 = (f32[272,128]{1,0:T(8,128)S(1)}, f32[272,128]{1,0:T(8,128)S(1)}, u32[]{:S(2)}, u32[]{:S(2)}) collective-permute-start(f32[272,128]{1,0:T(8,128)S(1)} %pad_maximum_fusion.2.mine_ref), channel_id=1, source_target_pairs={{0,1},{1,0},{2,3},{3,2},{4,5},{5,4},{6,7},{7,6},{8,9},{9,8},{10,11... | collective-permute-start | bytes 417800 | tf_op jit(solution)/shard_map/ppermute | solution.py:226
  113.1 0.1 reshape.52
  113.2 0.0 copy-start
  113.2 0.2 copy.23
  113.5 0.5 collective-permute-done.1.other_ref
  114.0 0.4 copy-done
  114.3 6.5 %shard_map.44 = (f32[288,576]{1,0:T(8,128)}, f32[18,2,128]{2,1,0:T(2,128)}) custom-call(f32[272,128]{1,0:T(8,128)S(1)} %pad_maximum_fusion.2.mine_ref, f32[272,128]{1,0:T(8,128)S(1)} %collective-permute-done.1.other_ref, f32[576,256]{1,0:T(8,128)S(1)} %bitcast.31, f32[288,256]{1,0:T(8,128)S(1)} %bitcast.32, ...), custom_call_target="tpu_custom_call" | custom-call | tf_op jit(solution)/shard_map/pallas_call | solution.py:203
  (27 shorter events, 0.6 us)
Async XLA Ops:
  0.6 11.3 %copy-start.1 = (f32[2,128,288]{1,2,0:T(8,128)S(1)}, f32[2,128,288]{1,2,0:T(8,128)}, u32[]{:S(2)}) copy-start(f32[2,128,288]{1,2,0:T(8,128)} %param.3) | copy-start | bytes 884740
  3.1 9.9 %collective-permute-start = (f32[2,288,128]{2,1,0:T(8,128)S(1)}, f32[2,288,128]{2,1,0:T(8,128)S(1)}, u32[]{:S(2)}, u32[]{:S(2)}) collective-permute-start(f32[2,288,128]{2,1,0:T(8,128)S(1)} %get-tuple-element.7), channel_id=1, source_target_pairs={{0,1},{1,0},{2,3},{3,2},{4,5},{5,4},{6,7},{7,6},{8,9},{9,8},{10,11... | collective-permute-start | bytes 884744 | tf_op jit(solution)/shard_map/ppermute | solution.py:226
  84.4 13.5 %collective-permute-start.2 = (f32[288,256]{1,0:T(8,128)S(1)}, f32[288,256]{1,0:T(8,128)S(1)}, u32[]{:S(2)}, u32[]{:S(2)}) collective-permute-start(f32[288,256]{1,0:T(8,128)S(1)} %constant_dynamic-update-slice_fusion), channel_id=1, source_target_pairs={{0,1},{1,0},{2,3},{3,2},{4,5},{5,4},{6,7},{7,6},{8,9},{9,8},{10,11... | collective-permute-start | bytes 884744 | tf_op jit(solution)/shard_map/ppermute | solution.py:226
  94.1 14.5 %all-to-all-start.3 = ((f32[16,65,128]{2,1,0:T(8,128)}), f32[16,65,128]{2,1,0:T(8,128)S(1)}, u32[]{:S(2)}, u32[]{:S(2)}) async-start(f32[16,65,128]{2,1,0:T(8,128)} %broadcast_in_dim.2), calls=%async_computation.3 | async-start | bytes 1179648 | tf_op jit(solution)/shard_map/all_to_all | solution.py:232
  108.6 5.3 %collective-permute-start.1 = (f32[272,128]{1,0:T(8,128)S(1)}, f32[272,128]{1,0:T(8,128)S(1)}, u32[]{:S(2)}, u32[]{:S(2)}) collective-permute-start(f32[272,128]{1,0:T(8,128)S(1)} %pad_maximum_fusion.2.mine_ref), channel_id=1, source_target_pairs={{0,1},{1,0},{2,3},{3,2},{4,5},{5,4},{6,7},{7,6},{8,9},{9,8},{10,11... | collective-permute-start | bytes 417800 | tf_op jit(solution)/shard_map/ppermute | solution.py:226
  113.2 1.1 copy-start

commit v7 on v6

--- a/solution.py
+++ b/solution.py
@@ -1,3 +1,5 @@
+import functools
+
 import jax
 import jax.numpy as jnp
 from jax import lax
@@ -29,13 +31,14 @@
     scale_row = lax.rsqrt(jnp.sum(block * eye, axis=0, keepdims=True))
     scaled = block * scale_col * scale_row
     off = scaled - eye
-    step = jnp.minimum(1.0, 1.9 / (1.0 + jnp.sqrt(jnp.sum(off * off))))
-    rest = eye - step * scaled
+    square = rough(off, off)
+    step = jnp.minimum(1.0, 1.9 / (1.0 + jnp.sqrt(jnp.sqrt(jnp.sum(square * square)))))
+    rest = (1.0 - step) * eye - step * off
     guess = eye + rest
-    rest = rough(rest, rest)
-    for turn in range(3):
+    rest = (1.0 - step) * (rest - step * off) + step * step * square
+    for turn in range(2):
         more = rough(guess, rest)
-        if turn < 2:
+        if turn < 1:
             rest = rough(rest, rest)
         guess = guess + more
     guess = guess * step
@@ -50,22 +53,22 @@
     size = block.shape[0]
     lane = lax.broadcasted_iota(jnp.int32, (1, size), 1)
     line = lax.broadcasted_iota(jnp.int32, (size, 1), 0)
-    work_ref[...] = block
+    work_ref[:size, :size] = block
 
     def sweep(at, carry):
-        value = work_ref[...]
-        row = work_ref[pl.ds(at, 1), :]
+        value = work_ref[:size, :size]
+        row = jnp.sum(jnp.where(line == at, value, 0.0), axis=0, keepdims=True)
         here = lane == at
         col = jnp.sum(jnp.where(here, value, 0.0), axis=1, keepdims=True)
         pivot = 1.0 / jnp.sum(jnp.where(here, row, 0.0), axis=1, keepdims=True)
         row = jnp.where(here, pivot, row * pivot)
         col = jnp.where(line == at, 0.0, col)
         value = jnp.where(here, 0.0, value)
-        work_ref[...] = jnp.where(line == at, row, value - col * row)
+        work_ref[:size, :size] = jnp.where(line == at, row, value - col * row)
         return carry
 
     lax.fori_loop(0, size, sweep, 0)
-    guess = work_ref[...]
+    guess = work_ref[:size, :size]
     return guess + dot(unit(size) - dot(guess, block), guess)
 
 
@@ -129,30 +132,59 @@
     block = jnp.concatenate([block[at : at + 1] for at in reversed(range(slab // 2))], axis=0)
     block = jnp.sum(pltpu.roll(block, 0, 1, stride=slab, stride_axis=0), axis=0, keepdims=True)
     piece = level_ref[row]
-    cut = send_ref.shape[1] - slab - held - 1
-    part = level_ref[:, pl.ds(jnp.minimum(row, held // cut - 1) * cut, cut), :]
+    cut = held // depth
+    rest = held % depth
+    part = level_ref[:, pl.ds(cut * row, cut), :]
+    spare = level_ref[:, pl.ds(cut * depth + lax.rem(row, rest), 1), :]
     for at in range(depth):
         send_ref[at, :slab] = terms[:, :width]
         send_ref[at, slab : slab + held] = piece
         send_ref[at, slab + held : slab + held + cut] = part[at]
-        send_ref[at, slab + held + cut :] = block
-
-
-def slab_terms(row, got, level, cut):
+        send_ref[at, slab + held + cut : slab + held + cut + 1] = spare[at]
+        send_ref[at, slab + held + cut + 1 :] = block
+
+
+def slab_terms(row, got, level):
     depth, held, width = level.shape
+    cut = held // depth
     slab = 2 * width // depth
     tall = -(-held // 2 // 8) * 8
     in_vmem = pl.BlockSpec(memory_space=pltpu.VMEM)
     return pl.pallas_call(
         slab_kernel,
-        out_shape=pltpu.VMEM((depth, slab + held + cut + 1, width), f32),
+        out_shape=pltpu.VMEM((depth, slab + held + cut + 2, width), f32),
         in_specs=[pl.BlockSpec(memory_space=pltpu.SMEM), in_vmem, in_vmem],
         scratch_shapes=[pltpu.VMEM((depth, tall, 2 * width), f32)],
     )(row.reshape(1), *(pltpu.with_memory_space_constraint(x, pltpu.VMEM) for x in (got, level)))
 
 
+def plane_kernel(row_ref, line_ref, send_ref, *, slab):
+    planes, rows, _ = send_ref.shape
+    depth, tall, _ = line_ref.shape
+    cut, turns = divmod(rows - slab - 1, depth)
+    terms = jnp.sum(line_ref[:, :slab], axis=0)
+    far = jnp.sum(line_ref[:, tall - 1 :], axis=0)
+    spare = line_ref[pl.ds(row_ref[0] // (depth // turns) * turns, turns), tall - 2]
+    for at in range(planes):
+        send_ref[at, :slab] = terms
+        for z in range(depth):
+            first = slab + z * cut
+            send_ref[at, first : first + cut] = line_ref[z, tall - 2 - cut : tall - 2]
+        send_ref[at, rows - 1 - turns : rows - 1] = spare
+        send_ref[at, rows - 1 :] = far
+
+
+def plane_terms(row, line, rows, slab):
+    planes = line.shape[0]
+    return pl.pallas_call(
+        functools.partial(plane_kernel, slab=slab),
+        out_shape=jax.ShapeDtypeStruct((planes, rows, line.shape[2]), f32),
+        in_specs=[pl.BlockSpec(memory_space=pltpu.SMEM), pl.BlockSpec(memory_space=pltpu.VMEM)],
+    )(row.reshape(1), pltpu.with_memory_space_constraint(line, pltpu.VMEM))
+
+
 def closing_kernel(mine_ref, other_ref, rows_ref, cols_ref, own_ref, start_ref, out_ref, gain_ref, work_ref):
-    width = work_ref.shape[0]
+    width = work_ref.shape[0] // 2
     slab = mine_ref.shape[0] - 2 * width
     groups = width // slab
     terms = mine_ref[...] + other_ref[...]
@@ -173,20 +205,15 @@
     upper = jnp.where(across >= down, upper, upper_turned) + unit(width)
     lower = jnp.where(across >= down, lower, lower_turned) + unit(width)
 
+    top = jnp.concatenate([upper, cross], axis=1)
+    system = jnp.concatenate([top, jnp.concatenate([cross.T, lower], axis=1)], axis=0)
+
     def solve(inverse):
         first, miss = inverse(upper)
-        carry = dot(first, cross)
-        last, more = inverse(lower - dot(cross, carry, ((0,), (0,))))
-        both = jnp.concatenate([first, carry], axis=1)
-
-        def gains(ref):
-            value = dot(ref[:, :width], both)
-            return value[:, :width], dot(ref[:, width:] - value[:, width:], last)
-
-        gain_ref[:, 0], gain_ref[:, 1] = gains(own_ref)
-        low, high = gains(cols_ref)
-        low = low - dot(high, carry, ((1,), (1,)))
-        out_ref[...] = start_ref[...] - dot(jnp.concatenate([low, high], axis=1), rows_ref[...], ((1,), (1,)))
+        full, more = inverse(system)
+        gain_ref[:, 0] = dot(own_ref[:, :width], first)
+        gain_ref[:, 1] = dot(own_ref[...], full[:, width:])
+        out_ref[...] = start_ref[...] - dot(dot(cols_ref[...], full), rows_ref[...], ((1,), (1,)))
         return miss + more
 
     miss = solve(expanded)
@@ -207,7 +234,7 @@
             jax.ShapeDtypeStruct((own.shape[0], 2, width), f32),
         ],
         in_specs=[in_vmem] * len(operands),
-        scratch_shapes=[pltpu.VMEM((width, width), f32)],
+        scratch_shapes=[pltpu.VMEM((2 * width, 2 * width), f32)],
     )(*(pltpu.with_memory_space_constraint(x, pltpu.VMEM) for x in operands))
 
 
@@ -230,9 +257,6 @@
 
     def over_plane(value):
         return lax.all_to_all(value, "row", 0, 0, tiled=True)
-
-    def copies(value, count):
-        return jnp.broadcast_to(value[None], (count, *value.shape))
 
     half = rows // 2
     share = half // depth
@@ -254,14 +278,12 @@
     got = over_z(jnp.concatenate([*parts, mine], axis=1))
     held = blocks * share
     level = over_plane(spread(got, planes, held))
-    cut = -(-held // planes)
-    users = held // cut
-    line = over_z(slab_terms(row, got, level, cut))
+    cut = held // planes
+    rest = held % planes
+    turns = depth // rest
+    line = over_z(slab_terms(row, got, level))
     row_half = whole(line[:, slab : slab + held])
-    terms = jnp.sum(line[:, :slab], axis=0)
-    far = jnp.sum(line[:, slab + held + cut :], axis=0)
-    part = line[:, slab + held : slab + held + cut].reshape(depth * cut, width)
-    disc = over_plane(copies(jnp.concatenate([terms, part, far], axis=0), planes))
+    disc = over_plane(plane_terms(row, line, slab + depth * cut + turns + 1, slab))
     row_other = from_partner(row_half)
 
     def in_order(value, other):
@@ -271,10 +293,13 @@
     row_terms = in_order(row_half, row_other).reshape(rows, wide)
     own = rows // devices
     own_terms = lax.dynamic_slice_in_dim(row_terms, col * own, own, 0)
-    terms = jnp.concatenate([disc[:, :slab].reshape(wide, width), disc[:, slab + depth * cut]], axis=0)
+    terms = jnp.concatenate([disc[:, :slab].reshape(wide, width), disc[:, -1]], axis=0)
     other = from_partner(terms)
-    col_terms = disc[:users, slab : slab + depth * cut].reshape(blocks, users // blocks, depth, cut, width)
-    col_terms = col_terms.transpose(2, 1, 3, 0, 4).reshape(half, wide)
+    part = disc[:, slab : slab + depth * cut].reshape(planes, depth, cut, width)
+    part = part.transpose(1, 0, 2, 3).reshape(depth, planes * cut, width)
+    spare = disc[:, slab + depth * cut : -1].reshape(-1, rest, turns, width)
+    spare = spare.transpose(0, 2, 1, 3).reshape(depth, rest, width)
+    col_terms = whole(jnp.concatenate([part, spare], axis=1))
     updated, gains = closing(terms, other, row_terms, col_terms, own_terms, kron_inverse.T)
     return updated.T, gains.transpose(1, 0, 2)
 

time: 121 us -> 119 us (0.983)
  local copies, waits for them, and re-layouts: 2.09 us -> 0.83 us
    all_to_all x1, waiting for transfers between devices: 10.7 us -> 9.45 us  [over_plane(): return lax.all_to_all(value, 'row', 0, 0, tiled=True)]
  transfers between devices with their start and end apart: 4 -> 4, of which waited for: 3 -> 3; matrix products, arithmetic and copies ran while one was open for 1% -> 0% of each run, Pallas kernels for 0% -> 1%
where the time goes in v7:
time: 119 us
  blocking collectives  70.4 us (59%)
  starting transfers between devices  25.3 us (21%)
  waiting for transfers between devices  11.1 us (9%)
  Pallas kernels  9.98 us (8%)
    all_to_all x2, blocking collectives, over_z(): lax.all_to_all(value, 'col', 0, 0, tiled=True, axis_index_groups=lines)  56.1 us
    ppermute x3, starting transfers between devices, from_partner(): return lax.ppermute(value, 'col', [(at, at ^ 1) for at in range(devices)])  21.5 us
    all_to_all x1, blocking collectives, over_plane(): return lax.all_to_all(value, 'row', 0, 0, tiled=True)  14.2 us
    all_to_all x1, waiting for transfers between devices, over_plane(): return lax.all_to_all(value, 'row', 0, 0, tiled=True)  9.45 us
    pallas_call x1, Pallas kernels, closing(): pl.pallas_call(closing_kernel, out_shape=[jax.ShapeDtypeStruct(start.shap...  6.01 us
    all_to_all x1, starting transfers between devices, over_plane(): return lax.all_to_all(value, 'row', 0, 0, tiled=True)  3.79 us
    pallas_call x1, Pallas kernels, opening(): pl.pallas_call(opening_kernel, out_shape=[pltpu.VMEM((blocks, start.shape...  2.46 us
  transfers between devices with their start and end apart: 4, of which 3 were waited for; matrix products, arithmetic and copies ran while one was open for 0% of the time, Pallas kernels for 1%

profile of v7, /device:TPU:1, one launch (start us, length us, event | category | flops | bytes accessed | tf_op | source)
XLA Modules:
  0.0 118.8 jit_solution(12752938472126979048)
XLA Ops:
  0.6 0.0 copy-start.1
  0.7 2.5 %shard_map.41 = (f32[2,288,128]{2,1,0:T(8,128)S(1)}, f32[2,288,128]{2,1,0:T(8,128)S(1)}) custom-call(s32[1]{0:T(128)} %bitcast.1.core_ref, f32[288,576]{1,0:T(8,128)} %bitcast.29, f32[2,288,128]{2,1,0:T(8,128)} %bitcast.35), custom_call_target="tpu_custom_call" | custom-call | tf_op jit(solution)/shard_map/pallas_call | solution.py:92
  3.1 8.7 %collective-permute-start = (f32[2,288,128]{2,1,0:T(8,128)S(1)}, f32[2,288,128]{2,1,0:T(8,128)S(1)}, u32[]{:S(2)}, u32[]{:S(2)}) collective-permute-start(f32[2,288,128]{2,1,0:T(8,128)S(1)} %get-tuple-element.7), channel_id=1, source_target_pairs={{0,1},{1,0},{2,3},{3,2},{4,5},{5,4},{6,7},{7,6},{8,9},{9,8},{10,11... | collective-permute-start | bytes 884744 | tf_op jit(solution)/shard_map/ppermute | solution.py:253
  11.9 0.0 copy-done.1
  11.9 0.1 dynamic-slice_bitcast_fusion
  12.1 0.1 reshape.65
  12.2 0.8 collective-permute-done
  13.2 24.8 %all_to_all.20.got_ref = f32[16,39,128]{2,1,0:T(8,128)S(1)} all-to-all(f32[16,39,128]{2,1,0:T(8,128)S(1)} %pad_maximum_fusion.1), channel_id=1, replica_groups={{0,2,4,6,8,10,12,14,16,18,20,22,24,26,28,30},{1,3,5,7,9,11,13,15,17,19,..., dimensions={0} | all-to-all | bytes 638976 | tf_op jit(solution)/shard_map/all_to_all | solution.py:256
  38.1 14.2 %all_to_all.21.level_ref = f32[16,36,128]{2,1,0:T(8,128)S(1)} all-to-all(f32[16,36,128]{2,1,0:T(8,128)S(1)} %shard_map.42), channel_id=1, replica_groups=mesh['row'=16,'col'=32] {'row'}, dimensions={0} | all-to-all | bytes 589824 | tf_op jit(solution)/shard_map/all_to_all | solution.py:259
  52.3 0.6 shard_map.43
  52.9 31.3 %all_to_all.22.line_ref = f32[16,56,128]{2,1,0:T(8,128)S(1)} all-to-all(f32[16,56,128]{2,1,0:T(8,128)S(1)} %shard_map.43), channel_id=1, replica_groups={{0,2,4,6,8,10,12,14,16,18,20,22,24,26,28,30},{1,3,5,7,9,11,13,15,17,19,..., dimensions={0} | all-to-all | bytes 917504 | tf_op jit(solution)/shard_map/all_to_all | solution.py:256
  84.3 8.7 %collective-permute-start.2 = (f32[288,256]{1,0:T(8,128)S(1)}, f32[288,256]{1,0:T(8,128)S(1)}, u32[]{:S(2)}, u32[]{:S(2)}) collective-permute-start(f32[288,256]{1,0:T(8,128)S(1)} %constant_dynamic-update-slice_fusion), channel_id=1, source_target_pairs={{0,1},{1,0},{2,3},{3,2},{4,5},{5,4},{6,7},{7,6},{8,9},{9,8},{10,11... | collective-permute-start | bytes 884744 | tf_op jit(solution)/shard_map/ppermute | solution.py:253
  93.1 0.9 shard_map.44
  94.0 3.8 %all-to-all-start.3 = ((f32[16,53,128]{2,1,0:T(8,128)}), f32[16,53,128]{2,1,0:T(8,128)S(1)}, u32[]{:S(2)}, u32[]{:S(2)}) async-start(f32[16,53,128]{2,1,0:T(8,128)} %shard_map.44), calls=%async_computation.3 | async-start | bytes 917504 | tf_op jit(solution)/shard_map/all_to_all | solution.py:259
  97.8 0.0 collective-permute-done.2
  97.9 9.4 %all-to-all-done.3 = f32[16,53,128]{2,1,0:T(8,128)S(1)} async-done(((f32[16,53,128]{2,1,0:T(8,128)}), f32[16,53,128]{2,1,0:T(8,128)S(1)}, u32[]{:S(2)}, u32[]{:S(2)}) %all-to-all-start.3) | async-done | bytes 434208 | tf_op jit(solution)/shard_map/all_to_all | solution.py:259
  107.4 0.1 copy.27
  107.6 4.1 %collective-permute-start.1 = (f32[272,128]{1,0:T(8,128)S(1)}, f32[272,128]{1,0:T(8,128)S(1)}, u32[]{:S(2)}, u32[]{:S(2)}) collective-permute-start(f32[272,128]{1,0:T(8,128)S(1)} %pad_maximum_fusion.4.mine_ref), channel_id=1, source_target_pairs={{0,1},{1,0},{2,3},{3,2},{4,5},{5,4},{6,7},{7,6},{8,9},{9,8},{10,11... | collective-permute-start | bytes 417800 | tf_op jit(solution)/shard_map/ppermute | solution.py:253
  111.7 0.0 copy-start
  111.8 0.8 collective-permute-done.1.other_ref
  112.6 0.2 copy-done
  112.8 6.0 %shard_map.45 = (f32[288,576]{1,0:T(8,128)}, f32[18,2,128]{2,1,0:T(2,128)}) custom-call(f32[272,128]{1,0:T(8,128)S(1)} %pad_maximum_fusion.4.mine_ref, f32[272,128]{1,0:T(8,128)S(1)} %collective-permute-done.1.other_ref, f32[576,256]{1,0:T(8,128)S(1)} %bitcast.32, f32[288,256]{1,0:T(8,128)S(1)} %pad_maximum_fusion.2.cols_ref, ...), custom_call_target="tpu_custom_call" | custom-call | tf_op jit(solution)/shard_map/pallas_call | solution.py:230
  (27 shorter events, 0.6 us)
Async XLA Ops:
  0.6 11.3 %copy-start.1 = (f32[2,128,288]{1,2,0:T(8,128)S(1)}, f32[2,128,288]{1,2,0:T(8,128)}, u32[]{:S(2)}) copy-start(f32[2,128,288]{1,2,0:T(8,128)} %param.3) | copy-start | bytes 884740
  3.1 9.9 %collective-permute-start = (f32[2,288,128]{2,1,0:T(8,128)S(1)}, f32[2,288,128]{2,1,0:T(8,128)S(1)}, u32[]{:S(2)}, u32[]{:S(2)}) collective-permute-start(f32[2,288,128]{2,1,0:T(8,128)S(1)} %get-tuple-element.7), channel_id=1, source_target_pairs={{0,1},{1,0},{2,3},{3,2},{4,5},{5,4},{6,7},{7,6},{8,9},{9,8},{10,11... | collective-permute-start | bytes 884744 | tf_op jit(solution)/shard_map/ppermute | solution.py:253
  84.3 13.4 %collective-permute-start.2 = (f32[288,256]{1,0:T(8,128)S(1)}, f32[288,256]{1,0:T(8,128)S(1)}, u32[]{:S(2)}, u32[]{:S(2)}) collective-permute-start(f32[288,256]{1,0:T(8,128)S(1)} %constant_dynamic-update-slice_fusion), channel_id=1, source_target_pairs={{0,1},{1,0},{2,3},{3,2},{4,5},{5,4},{6,7},{7,6},{8,9},{9,8},{10,11... | collective-permute-start | bytes 884744 | tf_op jit(solution)/shard_map/ppermute | solution.py:253
  94.0 13.4 %all-to-all-start.3 = ((f32[16,53,128]{2,1,0:T(8,128)}), f32[16,53,128]{2,1,0:T(8,128)S(1)}, u32[]{:S(2)}, u32[]{:S(2)}) async-start(f32[16,53,128]{2,1,0:T(8,128)} %shard_map.44), calls=%async_computation.3 | async-start | bytes 917504 | tf_op jit(solution)/shard_map/all_to_all | solution.py:259
  107.6 5.1 %collective-permute-start.1 = (f32[272,128]{1,0:T(8,128)S(1)}, f32[272,128]{1,0:T(8,128)S(1)}, u32[]{:S(2)}, u32[]{:S(2)}) collective-permute-start(f32[272,128]{1,0:T(8,128)S(1)} %pad_maximum_fusion.4.mine_ref), channel_id=1, source_target_pairs={{0,1},{1,0},{2,3},{3,2},{4,5},{5,4},{6,7},{7,6},{8,9},{9,8},{10,11... | collective-permute-start | bytes 417800 | tf_op jit(solution)/shard_map/ppermute | solution.py:253
  111.7 1.1 copy-start

commit v8 on v7

--- a/solution.py
+++ b/solution.py
@@ -6,7 +6,6 @@
 from jax.experimental import pallas as pl
 from jax.experimental.pallas import tpu as pltpu
 from jax.sharding import PartitionSpec as P
-
 
 highest = lax.Precision.HIGHEST
 f32 = jnp.float32
@@ -72,7 +71,7 @@
     return guess + dot(unit(size) - dot(guess, block), guess)
 
 
-def opening_kernel(core_ref, start_ref, lines_ref, keep_ref, send_ref):
+def opening_kernel(col_ref, start_ref, lines_ref, keep_ref, send_ref):
     blocks, half, width = keep_ref.shape
     lines = jnp.concatenate([lines_ref[at] for at in range(blocks)], axis=1)
     value = dot(start_ref[...], lines, ((0,), (0,)))
@@ -82,18 +81,18 @@
             low_ref[at] = value[:half, at * width : (at + 1) * width]
             high_ref[at] = value[half:, at * width : (at + 1) * width]
 
-    pl.when(core_ref[0] == 0)(lambda: store(keep_ref, send_ref))
-    pl.when(core_ref[0] != 0)(lambda: store(send_ref, keep_ref))
-
-
-def opening(core, start, lines):
+    pl.when(lax.rem(col_ref[0], 2) == 0)(lambda: store(keep_ref, send_ref))
+    pl.when(lax.rem(col_ref[0], 2) != 0)(lambda: store(send_ref, keep_ref))
+
+
+def opening(col, start, lines):
     blocks, _, width = lines.shape
     in_vmem = pl.BlockSpec(memory_space=pltpu.VMEM)
     return pl.pallas_call(
         opening_kernel,
         out_shape=[pltpu.VMEM((blocks, start.shape[1] // 2, width), f32)] * 2,
         in_specs=[pl.BlockSpec(memory_space=pltpu.SMEM), in_vmem, in_vmem],
-    )(core.reshape(1), start, lines)
+    )(col.reshape(1), start, lines)
 
 
 def spread_kernel(got_ref, out_ref):
@@ -158,13 +157,18 @@
     )(row.reshape(1), *(pltpu.with_memory_space_constraint(x, pltpu.VMEM) for x in (got, level)))
 
 
-def plane_kernel(row_ref, line_ref, send_ref, *, slab):
+def plane_kernel(row_ref, line_ref, send_ref, rows_ref, *, slab):
     planes, rows, _ = send_ref.shape
-    depth, tall, _ = line_ref.shape
+    depth, tall, width = line_ref.shape
     cut, turns = divmod(rows - slab - 1, depth)
     terms = jnp.sum(line_ref[:, :slab], axis=0)
     far = jnp.sum(line_ref[:, tall - 1 :], axis=0)
     spare = line_ref[pl.ds(row_ref[0] // (depth // turns) * turns, turns), tall - 2]
+    half = rows_ref.shape[0] // 2
+    share = half // depth
+    for z in range(depth):
+        rows_ref[z * share : (z + 1) * share] = line_ref[z, slab : slab + share]
+        rows_ref[half + z * share : half + (z + 1) * share] = line_ref[z, slab + share : slab + 2 * share]
     for at in range(planes):
         send_ref[at, :slab] = terms
         for z in range(depth):
@@ -174,20 +178,31 @@
         send_ref[at, rows - 1 :] = far
 
 
-def plane_terms(row, line, rows, slab):
-    planes = line.shape[0]
+def plane_terms(row, line, rows, slab, held):
+    planes, _, width = line.shape
     return pl.pallas_call(
         functools.partial(plane_kernel, slab=slab),
-        out_shape=jax.ShapeDtypeStruct((planes, rows, line.shape[2]), f32),
+        out_shape=[pltpu.VMEM((planes, rows, width), f32), pltpu.VMEM((planes * held, width), f32)],
         in_specs=[pl.BlockSpec(memory_space=pltpu.SMEM), pl.BlockSpec(memory_space=pltpu.VMEM)],
     )(row.reshape(1), pltpu.with_memory_space_constraint(line, pltpu.VMEM))
 
 
-def closing_kernel(mine_ref, other_ref, rows_ref, cols_ref, own_ref, start_ref, out_ref, gain_ref, work_ref):
+def closing_kernel(col_ref, mine_ref, other_ref, cols_ref, start_ref, out_ref, gain_ref, work_ref, left_ref, right_ref):
     width = work_ref.shape[0] // 2
-    slab = mine_ref.shape[0] - 2 * width
+    half = left_ref.shape[0] // 2
+    small = mine_ref.shape[0] - 2 * half
+    slab = small - 2 * width
     groups = width // slab
-    terms = mine_ref[...] + other_ref[...]
+    terms = mine_ref[:small] + other_ref[:small]
+
+    def place(low, high):
+        for at, part_ref in ((0, low), (half, high)):
+            left_ref[at : at + half] = part_ref[small : small + half]
+            right_ref[at : at + half] = part_ref[small + half :]
+
+    pl.when(lax.rem(col_ref[0], 2) == 0)(lambda: place(mine_ref, other_ref))
+    pl.when(lax.rem(col_ref[0], 2) != 0)(lambda: place(other_ref, mine_ref))
+    own = pl.ds(col_ref[0] * gain_ref.shape[0], gain_ref.shape[0])
 
     far = [terms[2 * width + n + m : 2 * width + n + m + 1] for n in range(groups) for m in (0, groups)]
     far = jnp.concatenate([jnp.broadcast_to(part, (slab // 2, width)) for part in far], axis=0)
@@ -211,9 +226,10 @@
     def solve(inverse):
         first, miss = inverse(upper)
         full, more = inverse(system)
-        gain_ref[:, 0] = dot(own_ref[:, :width], first)
-        gain_ref[:, 1] = dot(own_ref[...], full[:, width:])
-        out_ref[...] = start_ref[...] - dot(dot(cols_ref[...], full), rows_ref[...], ((1,), (1,)))
+        gain_ref[:, 0] = dot(left_ref[own], first)
+        gain_ref[:, 1] = dot(jnp.concatenate([left_ref[own], right_ref[own]], axis=1), full[:, width:])
+        rows = jnp.concatenate([left_ref[...], right_ref[...]], axis=1)
+        out_ref[...] = start_ref[...] - dot(dot(cols_ref[...], full), rows, ((1,), (1,)))
         return miss + more
 
     miss = solve(expanded)
@@ -223,19 +239,16 @@
         solve(lambda value: (eliminated(value, work_ref), 0.0))
 
 
-def closing(*operands):
-    own, start = operands[4:]
-    width = own.shape[1] // 2
+def closing(col, terms, other, col_terms, start, own):
+    cols, rows = start.shape
+    width = terms.shape[1]
     in_vmem = pl.BlockSpec(memory_space=pltpu.VMEM)
     return pl.pallas_call(
         closing_kernel,
-        out_shape=[
-            jax.ShapeDtypeStruct(start.shape, f32),
-            jax.ShapeDtypeStruct((own.shape[0], 2, width), f32),
-        ],
-        in_specs=[in_vmem] * len(operands),
-        scratch_shapes=[pltpu.VMEM((2 * width, 2 * width), f32)],
-    )(*(pltpu.with_memory_space_constraint(x, pltpu.VMEM) for x in operands))
+        out_shape=[jax.ShapeDtypeStruct(start.shape, f32), jax.ShapeDtypeStruct((own, 2, width), f32)],
+        in_specs=[pl.BlockSpec(memory_space=pltpu.SMEM)] + [in_vmem] * 4,
+        scratch_shapes=[pltpu.VMEM((2 * width, 2 * width), f32)] + [pltpu.VMEM((rows, width), f32)] * 2,
+    )(col.reshape(1), *(pltpu.with_memory_space_constraint(x, pltpu.VMEM) for x in (terms, other, col_terms, start)))
 
 
 def shards(kron_inverse, activations):
@@ -266,9 +279,8 @@
         left = value[:, :share].reshape(half, width)
         return jnp.concatenate([left, value[:, share:].reshape(half, width)], axis=1)
 
-    core = col % 2
     turned = activations.transpose(0, 2, 1)
-    keep, send = opening(core, kron_inverse.T, turned)
+    keep, send = opening(col, kron_inverse.T, turned)
     summed = keep + from_partner(send)
     groups = width // slab
     mine = lax.dynamic_slice(turned, (row // groups, 0, row % groups * slab), (1, cols, slab))
@@ -282,25 +294,16 @@
     rest = held % planes
     turns = depth // rest
     line = over_z(slab_terms(row, got, level))
-    row_half = whole(line[:, slab : slab + held])
-    disc = over_plane(plane_terms(row, line, slab + depth * cut + turns + 1, slab))
-    row_other = from_partner(row_half)
-
-    def in_order(value, other):
-        low = jnp.where(core == 0, value, other)
-        return jnp.stack([low, jnp.where(core == 0, other, value)])
-
-    row_terms = in_order(row_half, row_other).reshape(rows, wide)
-    own = rows // devices
-    own_terms = lax.dynamic_slice_in_dim(row_terms, col * own, own, 0)
-    terms = jnp.concatenate([disc[:, :slab].reshape(wide, width), disc[:, -1]], axis=0)
+    send, row_half = plane_terms(row, line, slab + depth * cut + turns + 1, slab, held)
+    disc = over_plane(send)
+    terms = jnp.concatenate([disc[:, :slab].reshape(wide, width), disc[:, -1], row_half], axis=0)
     other = from_partner(terms)
     part = disc[:, slab : slab + depth * cut].reshape(planes, depth, cut, width)
     part = part.transpose(1, 0, 2, 3).reshape(depth, planes * cut, width)
     spare = disc[:, slab + depth * cut : -1].reshape(-1, rest, turns, width)
     spare = spare.transpose(0, 2, 1, 3).reshape(depth, rest, width)
     col_terms = whole(jnp.concatenate([part, spare], axis=1))
-    updated, gains = closing(terms, other, row_terms, col_terms, own_terms, kron_inverse.T)
+    updated, gains = closing(col, terms, other, col_terms, kron_inverse.T, rows // devices)
     return updated.T, gains.transpose(1, 0, 2)
 
 

time: 119 us -> 115 us (0.966)
  blocking collectives: 70.4 us -> 83 us
  waiting for transfers between devices: 11.1 us -> 1.89 us
  starting transfers between devices: 25.3 us -> 18.5 us
    all_to_all x1 -> x2, blocking collectives: 14.2 us -> 26.8 us  [over_plane(): return lax.all_to_all(value, 'row', 0, 0, tiled=True)]
    all_to_all x1 -> x0, waiting for transfers between devices: 9.45 us -> none  [over_plane(): return lax.all_to_all(value, 'row', 0, 0, tiled=True)]
    all_to_all x1 -> x0, starting transfers between devices: 3.79 us -> none  [over_plane(): return lax.all_to_all(value, 'row', 0, 0, tiled=True)]
    ppermute x3 -> x2, starting transfers between devices: 21.5 us -> 18.5 us  [from_partner(): return lax.ppermute(value, 'col', [(at, at ^ 1) for at in range(devices)])]
  transfers between devices with their start and end apart: 4 -> 2, of which waited for: 3 -> 2; matrix products, arithmetic and copies ran while one was open for 0% -> 0% of each run, Pallas kernels for 1% -> 0%
where the time goes in v8:
time: 115 us; the launch traced here: 114 us
  blocking collectives  83 us (72%)
  starting transfers between devices  18.5 us (16%)
  Pallas kernels  9.27 us (8%)
  waiting for transfers between devices  1.89 us (2%)
    all_to_all x2, blocking collectives, over_z(): lax.all_to_all(value, 'col', 0, 0, tiled=True, axis_index_groups=lines)  56.1 us
    all_to_all x2, blocking collectives, over_plane(): return lax.all_to_all(value, 'row', 0, 0, tiled=True)  26.8 us
    ppermute x2, starting transfers between devices, from_partner(): return lax.ppermute(value, 'col', [(at, at ^ 1) for at in range(devices)])  18.5 us
    pallas_call x1, Pallas kernels, closing(): pl.pallas_call(closing_kernel, out_shape=[jax.ShapeDtypeStruct(start.shap...  6.04 us
    pallas_call x1, Pallas kernels, opening(): pl.pallas_call(opening_kernel, out_shape=[pltpu.VMEM((blocks, start.shape...  2.46 us
  transfers between devices with their start and end apart: 2, of which 2 were waited for; matrix products, arithmetic and copies ran while one was open for 0% of the time, Pallas kernels for 0%

profile of v8, /device:TPU:1, one launch (start us, length us, event | category | flops | bytes accessed | tf_op | source)
XLA Modules:
  0.0 114.2 jit_solution(18231798362960492214)
XLA Ops:
  0.6 0.0 copy-start.1
  0.6 2.5 %shard_map.41 = (f32[2,288,128]{2,1,0:T(8,128)S(1)}, f32[2,288,128]{2,1,0:T(8,128)S(1)}) custom-call(s32[1]{0:T(128)} %bitcast.col_ref, f32[288,576]{1,0:T(8,128)} %bitcast.24, f32[2,288,128]{2,1,0:T(8,128)} %bitcast.28), custom_call_target="tpu_custom_call" | custom-call | tf_op jit(solution)/shard_map/pallas_call | solution.py:91
  3.1 8.7 %collective-permute-start = (f32[2,288,128]{2,1,0:T(8,128)S(1)}, f32[2,288,128]{2,1,0:T(8,128)S(1)}, u32[]{:S(2)}, u32[]{:S(2)}) collective-permute-start(f32[2,288,128]{2,1,0:T(8,128)S(1)} %get-tuple-element.9), channel_id=1, source_target_pairs={{0,1},{1,0},{2,3},{3,2},{4,5},{5,4},{6,7},{7,6},{8,9},{9,8},{10,11... | collective-permute-start | bytes 884744 | tf_op jit(solution)/shard_map/ppermute | solution.py:266
  11.9 0.0 copy-done.1
  11.9 0.1 dynamic-slice_bitcast_fusion
  12.1 0.1 reshape.54
  12.2 0.8 collective-permute-done
  13.2 24.8 %all_to_all.20.got_ref = f32[16,39,128]{2,1,0:T(8,128)S(1)} all-to-all(f32[16,39,128]{2,1,0:T(8,128)S(1)} %pad_maximum_fusion.1), channel_id=1, replica_groups={{0,2,4,6,8,10,12,14,16,18,20,22,24,26,28,30},{1,3,5,7,9,11,13,15,17,19,..., dimensions={0} | all-to-all | bytes 638976 | tf_op jit(solution)/shard_map/all_to_all | solution.py:269
  38.1 14.2 %all_to_all.21.level_ref = f32[16,36,128]{2,1,0:T(8,128)S(1)} all-to-all(f32[16,36,128]{2,1,0:T(8,128)S(1)} %shard_map.42), channel_id=1, replica_groups=mesh['row'=16,'col'=32] {'row'}, dimensions={0} | all-to-all | bytes 589824 | tf_op jit(solution)/shard_map/all_to_all | solution.py:272
  52.3 0.6 shard_map.43
  52.9 31.3 %all_to_all.22.line_ref = f32[16,56,128]{2,1,0:T(8,128)S(1)} all-to-all(f32[16,56,128]{2,1,0:T(8,128)S(1)} %shard_map.43), channel_id=1, replica_groups={{0,2,4,6,8,10,12,14,16,18,20,22,24,26,28,30},{1,3,5,7,9,11,13,15,17,19,..., dimensions={0} | all-to-all | bytes 917504 | tf_op jit(solution)/shard_map/all_to_all | solution.py:269
  84.2 0.1 shard_map.44
  84.3 12.6 %all_to_all.23 = f32[16,53,128]{2,1,0:T(8,128)S(1)} all-to-all(f32[16,53,128]{2,1,0:T(8,128)S(1)} %get-tuple-element.10), channel_id=1, replica_groups=mesh['row'=16,'col'=32] {'row'}, dimensions={0} | all-to-all | bytes 868352 | tf_op jit(solution)/shard_map/all_to_all | solution.py:272
  97.0 9.8 %collective-permute-start.1 = (f32[848,128]{1,0:T(8,128)S(1)}, f32[848,128]{1,0:T(8,128)S(1)}, u32[]{:S(2)}, u32[]{:S(2)}) collective-permute-start(f32[848,128]{1,0:T(8,128)S(1)} %pad_maximum_fusion.mine_ref), channel_id=1, source_target_pairs={{0,1},{1,0},{2,3},{3,2},{4,5},{5,4},{6,7},{7,6},{8,9},{9,8},{10,11... | collective-permute-start | bytes 1302536 | tf_op jit(solution)/shard_map/ppermute | solution.py:266
  106.8 0.1 copy.27
  107.0 0.0 copy-start
  107.1 1.1 collective-permute-done.1.other_ref
  108.2 0.0 copy-done
  108.2 6.0 %shard_map.45 = (f32[288,576]{1,0:T(8,128)}, f32[18,2,128]{2,1,0:T(2,128)}) custom-call(s32[1]{0:T(128)} %bitcast.col_ref, f32[848,128]{1,0:T(8,128)S(1)} %pad_maximum_fusion.mine_ref, f32[848,128]{1,0:T(8,128)S(1)} %collective-permute-done.1.other_ref, f32[288,256]{1,0:T(8,128)S(1)} %pad_maximum_fusion.2.cols_ref, f32[288,576]{1,0:T(8,128)S(1)} %bitcast.25), custom_call_target="tpu_custom_call" | custom-call | tf_op jit(solution)/shard_map/pallas_call | solution.py:246
  (19 shorter events, 0.4 us)
Async XLA Ops:
  0.6 11.3 %copy-start.1 = (f32[2,128,288]{1,2,0:T(8,128)S(1)}, f32[2,128,288]{1,2,0:T(8,128)}, u32[]{:S(2)}) copy-start(f32[2,128,288]{1,2,0:T(8,128)} %param.3) | copy-start | bytes 884740
  3.1 9.9 %collective-permute-start = (f32[2,288,128]{2,1,0:T(8,128)S(1)}, f32[2,288,128]{2,1,0:T(8,128)S(1)}, u32[]{:S(2)}, u32[]{:S(2)}) collective-permute-start(f32[2,288,128]{2,1,0:T(8,128)S(1)} %get-tuple-element.9), channel_id=1, source_target_pairs={{0,1},{1,0},{2,3},{3,2},{4,5},{5,4},{6,7},{7,6},{8,9},{9,8},{10,11... | collective-permute-start | bytes 884744 | tf_op jit(solution)/shard_map/ppermute | solution.py:266
  97.0 11.2 %collective-permute-start.1 = (f32[848,128]{1,0:T(8,128)S(1)}, f32[848,128]{1,0:T(8,128)S(1)}, u32[]{:S(2)}, u32[]{:S(2)}) collective-permute-start(f32[848,128]{1,0:T(8,128)S(1)} %pad_maximum_fusion.mine_ref), channel_id=1, source_target_pairs={{0,1},{1,0},{2,3},{3,2},{4,5},{5,4},{6,7},{7,6},{8,9},{9,8},{10,11... | collective-permute-start | bytes 1302536 | tf_op jit(solution)/shard_map/ppermute | solution.py:266
  107.0 1.2 %copy-start = (f32[576,288]{0,1:T(8,128)S(1)}, f32[576,288]{0,1:T(8,128)}, u32[]{:S(2)}) copy-start(f32[576,288]{0,1:T(8,128)} %param.2) | copy-start | bytes 1990660

commit v9 on v8

--- a/solution.py
+++ b/solution.py
@@ -71,28 +71,58 @@
     return guess + dot(unit(size) - dot(guess, block), guess)
 
 
-def opening_kernel(col_ref, start_ref, lines_ref, keep_ref, send_ref):
-    blocks, half, width = keep_ref.shape
+def product(high, start_ref, lines_ref, out_ref):
+    blocks, half, width = out_ref.shape
     lines = jnp.concatenate([lines_ref[at] for at in range(blocks)], axis=1)
-    value = dot(start_ref[...], lines, ((0,), (0,)))
-
-    def store(low_ref, high_ref):
+
+    def store(first):
+        value = dot(start_ref[:, first : first + half], lines, ((0,), (0,)))
         for at in range(blocks):
-            low_ref[at] = value[:half, at * width : (at + 1) * width]
-            high_ref[at] = value[half:, at * width : (at + 1) * width]
-
-    pl.when(lax.rem(col_ref[0], 2) == 0)(lambda: store(keep_ref, send_ref))
-    pl.when(lax.rem(col_ref[0], 2) != 0)(lambda: store(send_ref, keep_ref))
-
-
-def opening(col, start, lines):
+            out_ref[at] = value[:, at * width : (at + 1) * width]
+
+    pl.when(high == 0)(lambda: store(0))
+    pl.when(high != 0)(lambda: store(half))
+
+
+def loading_kernel(col_ref, far_start_ref, far_lines_ref, send_ref, start_ref, lines_ref, done_ref):
+    moves = (
+        pltpu.make_async_copy(far_start_ref, start_ref, done_ref.at[0]),
+        pltpu.make_async_copy(far_lines_ref, lines_ref, done_ref.at[1]),
+    )
+    for move in moves:
+        move.start()
+    for move in moves:
+        move.wait()
+    product(1 - lax.rem(col_ref[0], 2), start_ref, lines_ref, send_ref)
+
+
+def loading(col, start, lines):
+    blocks, _, width = lines.shape
+    in_hbm = pl.BlockSpec(memory_space=pl.ANY)
+    return pl.pallas_call(
+        loading_kernel,
+        out_shape=[
+            pltpu.VMEM((blocks, start.shape[1] // 2, width), f32),
+            pltpu.VMEM(start.shape, f32),
+            pltpu.VMEM(lines.shape, f32),
+        ],
+        in_specs=[pl.BlockSpec(memory_space=pltpu.SMEM), in_hbm, in_hbm],
+        scratch_shapes=[pltpu.SemaphoreType.DMA((2,))],
+    )(col.reshape(1), start, lines)
+
+
+def keeping_kernel(col_ref, start_ref, lines_ref, out_ref):
+    product(lax.rem(col_ref[0], 2), start_ref, lines_ref, out_ref)
+
+
+def keeping(col, start, lines):
     blocks, _, width = lines.shape
     in_vmem = pl.BlockSpec(memory_space=pltpu.VMEM)
     return pl.pallas_call(
-        opening_kernel,
-        out_shape=[pltpu.VMEM((blocks, start.shape[1] // 2, width), f32)] * 2,
+        keeping_kernel,
+        out_shape=pltpu.VMEM((blocks, start.shape[1] // 2, width), f32),
         in_specs=[pl.BlockSpec(memory_space=pltpu.SMEM), in_vmem, in_vmem],
-    )(col.reshape(1), start, lines)
+    )(col.reshape(1), *(pltpu.with_memory_space_constraint(x, pltpu.VMEM) for x in (start, lines)))
 
 
 def spread_kernel(got_ref, out_ref):
@@ -195,13 +225,11 @@
     groups = width // slab
     terms = mine_ref[:small] + other_ref[:small]
 
-    def place(low, high):
-        for at, part_ref in ((0, low), (half, high)):
-            left_ref[at : at + half] = part_ref[small : small + half]
-            right_ref[at : at + half] = part_ref[small + half :]
-
-    pl.when(lax.rem(col_ref[0], 2) == 0)(lambda: place(mine_ref, other_ref))
-    pl.when(lax.rem(col_ref[0], 2) != 0)(lambda: place(other_ref, mine_ref))
+    core = lax.rem(col_ref[0], 2)
+    for at, part_ref in ((core, mine_ref), (1 - core, other_ref)):
+        at = pl.ds(pl.multiple_of(at * half, 8), half)
+        left_ref[at] = part_ref[small : small + half]
+        right_ref[at] = part_ref[small + half :]
     own = pl.ds(col_ref[0] * gain_ref.shape[0], gain_ref.shape[0])
 
     far = [terms[2 * width + n + m : 2 * width + n + m + 1] for n in range(groups) for m in (0, groups)]
@@ -279,9 +307,8 @@
         left = value[:, :share].reshape(half, width)
         return jnp.concatenate([left, value[:, share:].reshape(half, width)], axis=1)
 
-    turned = activations.transpose(0, 2, 1)
-    keep, send = opening(col, kron_inverse.T, turned)
-    summed = keep + from_partner(send)
+    send, start, turned = loading(col, kron_inverse.T, activations.transpose(0, 2, 1))
+    summed = keeping(col, start, turned) + from_partner(send)
     groups = width // slab
     mine = lax.dynamic_slice(turned, (row // groups, 0, row % groups * slab), (1, cols, slab))
     mine = jnp.pad(mine.reshape(depth, share, slab), ((0, 0), (0, -share % groups), (0, 0)))
@@ -303,7 +330,7 @@
     spare = disc[:, slab + depth * cut : -1].reshape(-1, rest, turns, width)
     spare = spare.transpose(0, 2, 1, 3).reshape(depth, rest, width)
     col_terms = whole(jnp.concatenate([part, spare], axis=1))
-    updated, gains = closing(col, terms, other, col_terms, kron_inverse.T, rows // devices)
+    updated, gains = closing(col, terms, other, col_terms, start, rows // devices)
     return updated.T, gains.transpose(1, 0, 2)
 
 

time: 115 us -> 114 us (level)
    pallas_call x1 -> x2, Pallas kernels: 2.46 us -> 2.78 us  [the longest x1 1.92 us: loading(): pl.pallas_call(loading_kernel, out_shape=[pltpu.VMEM((blocks, start.shape...]
  transfers between devices with their start and end apart: 2 -> 2, of which waited for: 2 -> 1; matrix products, arithmetic and copies ran while one was open for 0% -> 0% of each run, Pallas kernels for 0% -> 1%
where the time goes in v9:
time: 114 us
  blocking collectives  83 us (73%)
  starting transfers between devices  18.6 us (16%)
  Pallas kernels  9.54 us (8%)
    all_to_all x2, blocking collectives, over_z(): lax.all_to_all(value, 'col', 0, 0, tiled=True, axis_index_groups=lines)  56.2 us
    all_to_all x2, blocking collectives, over_plane(): return lax.all_to_all(value, 'row', 0, 0, tiled=True)  26.9 us
    ppermute x2, starting transfers between devices, from_partner(): return lax.ppermute(value, 'col', [(at, at ^ 1) for at in range(devices)])  18.6 us
    pallas_call x1, Pallas kernels, closing(): pl.pallas_call(closing_kernel, out_shape=[jax.ShapeDtypeStruct(start.shap...  6 us
  transfers between devices with their start and end apart: 2, of which 1 were waited for; matrix products, arithmetic and copies ran while one was open for 0% of the time, Pallas kernels for 1%

profile of v9, /device:TPU:1, one launch (start us, length us, event | category | flops | bytes accessed | tf_op | source)
XLA Modules:
  0.0 113.8 jit_solution(4439960229301531759)
XLA Ops:
  0.6 1.9 %shard_map.41 = (f32[2,288,128]{2,1,0:T(8,128)S(1)}, f32[288,576]{1,0:T(8,128)S(1)}, f32[2,288,128]{2,1,0:T(8,128)S(1)}) custom-call(s32[1]{0:T(128)} %bitcast.col_ref, f32[288,576]{1,0:T(8,128)} %bitcast.24, f32[2,288,128]{2,1,0:T(8,128)} %bitcast.26), custom_call_target="tpu_custom_call" | custom-call | tf_op jit(solution)/shard_map/pallas_call | solution.py:102
  2.6 8.9 %collective-permute-start = (f32[2,288,128]{2,1,0:T(8,128)S(1)}, f32[2,288,128]{2,1,0:T(8,128)S(1)}, u32[]{:S(2)}, u32[]{:S(2)}) collective-permute-start(f32[2,288,128]{2,1,0:T(8,128)S(1)} %get-tuple-element.11), channel_id=1, source_target_pairs={{0,1},{1,0},{2,3},{3,2},{4,5},{5,4},{6,7},{7,6},{8,9},{9,8},{10,11... | collective-permute-start | bytes 884744 | tf_op jit(solution)/shard_map/ppermute | solution.py:294
  11.5 0.9 shard_map.42
  12.4 0.1 constant_dynamic-slice_fusion
  12.6 0.1 reshape.55
  12.7 0.0 collective-permute-done
  12.9 24.9 %all_to_all.20.got_ref = f32[16,39,128]{2,1,0:T(8,128)S(1)} all-to-all(f32[16,39,128]{2,1,0:T(8,128)S(1)} %pad_maximum_fusion.1), channel_id=1, replica_groups={{0,2,4,6,8,10,12,14,16,18,20,22,24,26,28,30},{1,3,5,7,9,11,13,15,17,19,..., dimensions={0} | all-to-all | bytes 638976 | tf_op jit(solution)/shard_map/all_to_all | solution.py:297
  37.8 14.2 %all_to_all.21.level_ref = f32[16,36,128]{2,1,0:T(8,128)S(1)} all-to-all(f32[16,36,128]{2,1,0:T(8,128)S(1)} %shard_map.43), channel_id=1, replica_groups=mesh['row'=16,'col'=32] {'row'}, dimensions={0} | all-to-all | bytes 589824 | tf_op jit(solution)/shard_map/all_to_all | solution.py:300
  52.0 0.6 shard_map.44
  52.6 31.3 %all_to_all.22.line_ref = f32[16,56,128]{2,1,0:T(8,128)S(1)} all-to-all(f32[16,56,128]{2,1,0:T(8,128)S(1)} %shard_map.44), channel_id=1, replica_groups={{0,2,4,6,8,10,12,14,16,18,20,22,24,26,28,30},{1,3,5,7,9,11,13,15,17,19,..., dimensions={0} | all-to-all | bytes 917504 | tf_op jit(solution)/shard_map/all_to_all | solution.py:297
  83.9 0.1 shard_map.45
  84.0 12.6 %all_to_all.23 = f32[16,53,128]{2,1,0:T(8,128)S(1)} all-to-all(f32[16,53,128]{2,1,0:T(8,128)S(1)} %get-tuple-element.12), channel_id=1, replica_groups=mesh['row'=16,'col'=32] {'row'}, dimensions={0} | all-to-all | bytes 868352 | tf_op jit(solution)/shard_map/all_to_all | solution.py:300
  96.7 9.7 %collective-permute-start.1 = (f32[848,128]{1,0:T(8,128)S(1)}, f32[848,128]{1,0:T(8,128)S(1)}, u32[]{:S(2)}, u32[]{:S(2)}) collective-permute-start(f32[848,128]{1,0:T(8,128)S(1)} %pad_maximum_fusion.mine_ref), channel_id=1, source_target_pairs={{0,1},{1,0},{2,3},{3,2},{4,5},{5,4},{6,7},{7,6},{8,9},{9,8},{10,11... | collective-permute-start | bytes 1302536 | tf_op jit(solution)/shard_map/ppermute | solution.py:294
  106.5 0.1 copy.27
  106.8 1.1 collective-permute-done.1.other_ref
  107.8 6.0 %shard_map.46 = (f32[288,576]{1,0:T(8,128)}, f32[18,2,128]{2,1,0:T(2,128)}) custom-call(s32[1]{0:T(128)} %bitcast.col_ref, f32[848,128]{1,0:T(8,128)S(1)} %pad_maximum_fusion.mine_ref, f32[848,128]{1,0:T(8,128)S(1)} %collective-permute-done.1.other_ref, f32[288,256]{1,0:T(8,128)S(1)} %pad_maximum_fusion.2.cols_ref, f32[288,576]{1,0:T(8,128)S(1)} %get-tuple-element.9.start_ref), custom_call_target="tpu_custom_call" | custom-call | tf_op jit(solution)/shard_map/pallas_call | solution.py:274
  (19 shorter events, 0.4 us)
Async XLA Ops:
  2.6 10.1 %collective-permute-start = (f32[2,288,128]{2,1,0:T(8,128)S(1)}, f32[2,288,128]{2,1,0:T(8,128)S(1)}, u32[]{:S(2)}, u32[]{:S(2)}) collective-permute-start(f32[2,288,128]{2,1,0:T(8,128)S(1)} %get-tuple-element.11), channel_id=1, source_target_pairs={{0,1},{1,0},{2,3},{3,2},{4,5},{5,4},{6,7},{7,6},{8,9},{9,8},{10,11... | collective-permute-start | bytes 884744 | tf_op jit(solution)/shard_map/ppermute | solution.py:294
  96.7 11.1 %collective-permute-start.1 = (f32[848,128]{1,0:T(8,128)S(1)}, f32[848,128]{1,0:T(8,128)S(1)}, u32[]{:S(2)}, u32[]{:S(2)}) collective-permute-start(f32[848,128]{1,0:T(8,128)S(1)} %pad_maximum_fusion.mine_ref), channel_id=1, source_target_pairs={{0,1},{1,0},{2,3},{3,2},{4,5},{5,4},{6,7},{7,6},{8,9},{9,8},{10,11... | collective-permute-start | bytes 1302536 | tf_op jit(solution)/shard_map/ppermute | solution.py:294

commit v10 on v9

--- a/solution.py
+++ b/solution.py
@@ -31,7 +31,8 @@
     scaled = block * scale_col * scale_row
     off = scaled - eye
     square = rough(off, off)
-    step = jnp.minimum(1.0, 1.9 / (1.0 + jnp.sqrt(jnp.sqrt(jnp.sum(square * square)))))
+    spread = jnp.sum(jnp.sum(square * square, axis=0, keepdims=True), axis=1, keepdims=True)
+    step = jnp.minimum(1.0, 1.9 / (1.0 + jnp.sqrt(jnp.sqrt(spread))))
     rest = (1.0 - step) * eye - step * off
     guess = eye + rest
     rest = (1.0 - step) * (rest - step * off) + step * step * square
@@ -139,7 +140,7 @@
     )(pltpu.with_memory_space_constraint(got, pltpu.VMEM))
 
 
-def slab_kernel(row_ref, got_ref, level_ref, send_ref, right_ref):
+def slab_kernel(row_ref, got_ref, level_ref, send_ref, right_ref, *, seats):
     depth, held, width = level_ref.shape
     share = held // 2
     tall = right_ref.shape[1]
@@ -150,8 +151,9 @@
     packed = jnp.broadcast_to(packed[:, :, None, :], (depth, tall // groups, groups, width))
     packed = pltpu.roll(packed.reshape(depth * tall, width), slab, 1, stride=slab, stride_axis=0)
     right_ref[...] = jnp.zeros(right_ref.shape, f32)
-    right_ref[:, :share, :width] = level_ref[:, :share, :]
-    right_ref[:, :share, width:] = level_ref[:, share:, :]
+    for at, seat in enumerate(seats):
+        right_ref[at, :share, :width] = level_ref[seat, :share, :]
+        right_ref[at, :share, width:] = level_ref[seat, share:, :]
     terms = dot(packed[:, :slab], right_ref[...].reshape(depth * tall, 2 * width), ((0,), (0,)))
     terms = pltpu.roll(terms, jnp.where(row == 0, 0, 2 * width - slab * row), 1)
     lane = lax.broadcasted_iota(jnp.int32, (slab, width), 1)
@@ -165,22 +167,22 @@
     rest = held % depth
     part = level_ref[:, pl.ds(cut * row, cut), :]
     spare = level_ref[:, pl.ds(cut * depth + lax.rem(row, rest), 1), :]
-    for at in range(depth):
+    for at, seat in enumerate(seats):
         send_ref[at, :slab] = terms[:, :width]
         send_ref[at, slab : slab + held] = piece
-        send_ref[at, slab + held : slab + held + cut] = part[at]
-        send_ref[at, slab + held + cut : slab + held + cut + 1] = spare[at]
+        send_ref[at, slab + held : slab + held + cut] = part[seat]
+        send_ref[at, slab + held + cut : slab + held + cut + 1] = spare[seat]
         send_ref[at, slab + held + cut + 1 :] = block
 
 
-def slab_terms(row, got, level):
+def slab_terms(row, got, level, seats):
     depth, held, width = level.shape
     cut = held // depth
     slab = 2 * width // depth
     tall = -(-held // 2 // 8) * 8
     in_vmem = pl.BlockSpec(memory_space=pltpu.VMEM)
     return pl.pallas_call(
-        slab_kernel,
+        functools.partial(slab_kernel, seats=seats),
         out_shape=pltpu.VMEM((depth, slab + held + cut + 2, width), f32),
         in_specs=[pl.BlockSpec(memory_space=pltpu.SMEM), in_vmem, in_vmem],
         scratch_shapes=[pltpu.VMEM((depth, tall, 2 * width), f32)],
@@ -279,6 +281,13 @@
     )(col.reshape(1), *(pltpu.with_memory_space_constraint(x, pltpu.VMEM) for x in (terms, other, col_terms, start)))
 
 
+def mirrored(count):
+    order = [0]
+    while len(order) < count:
+        order = [2 * at for at in order] + [2 * at + 1 for at in order]
+    return order
+
+
 def shards(kron_inverse, activations):
     rows, cols = kron_inverse.shape
     blocks, width = activations.shape[:2]
@@ -286,9 +295,13 @@
     planes = lax.axis_size("row")
     devices = lax.axis_size("col")
     depth = devices // 2
+    along = mirrored(depth)
+    around = [seat // 2 + seat % 2 * (planes // 2) for seat in range(planes)]
+    seats = [around.index(z) for z in along]
     row = lax.axis_index("row")
+    row = row % (planes // 2) * 2 + row // (planes // 2)
     col = lax.axis_index("col")
-    lines = [[2 * z + k for z in range(depth)] for k in range(2)]
+    lines = [[2 * z + k for z in along] for k in range(2)]
 
     def from_partner(value):
         return lax.ppermute(value, "col", [(at, at ^ 1) for at in range(devices)])
@@ -297,7 +310,7 @@
         return lax.all_to_all(value, "col", 0, 0, tiled=True, axis_index_groups=lines)
 
     def over_plane(value):
-        return lax.all_to_all(value, "row", 0, 0, tiled=True)
+        return lax.all_to_all(value, "row", 0, 0, tiled=True, axis_index_groups=[around])
 
     half = rows // 2
     share = half // depth
@@ -320,7 +333,7 @@
     cut = held // planes
     rest = held % planes
     turns = depth // rest
-    line = over_z(slab_terms(row, got, level))
+    line = over_z(slab_terms(row, got, level, seats))
     send, row_half = plane_terms(row, line, slab + depth * cut + turns + 1, slab, held)
     disc = over_plane(send)
     terms = jnp.concatenate([disc[:, :slab].reshape(wide, width), disc[:, -1], row_half], axis=0)

time: 114 us -> 117 us (1.026)
  blocking collectives: 83 us -> 89.3 us
  starting transfers between devices: 18.6 us -> 15.4 us
    all_to_all x2, blocking collectives: 56.2 us -> 63.9 us  [over_z(): lax.all_to_all(value, 'col', 0, 0, tiled=True, axis_index_groups=lines)]
    ppermute x2, starting transfers between devices: 18.6 us -> 15.4 us  [from_partner(): return lax.ppermute(value, 'col', [(at, at ^ 1) for at in range(devices)])]
    all_to_all x2, blocking collectives: 26.9 us -> 25.4 us  [over_plane(): lax.all_to_all(value, 'row', 0, 0, tiled=True, axis_index_groups=[around])]
where the time goes in v10:
time: 117 us
  blocking collectives  89.3 us (76%)
  starting transfers between devices  15.4 us (13%)
  Pallas kernels  9.28 us (8%)
    all_to_all x2, blocking collectives, over_z(): lax.all_to_all(value, 'col', 0, 0, tiled=True, axis_index_groups=lines)  63.9 us
    all_to_all x2, blocking collectives, over_plane(): lax.all_to_all(value, 'row', 0, 0, tiled=True, axis_index_groups=[around])  25.4 us
    ppermute x2, starting transfers between devices, from_partner(): return lax.ppermute(value, 'col', [(at, at ^ 1) for at in range(devices)])  15.4 us
    pallas_call x1, Pallas kernels, closing(): pl.pallas_call(closing_kernel, out_shape=[jax.ShapeDtypeStruct(start.shap...  5.73 us
  transfers between devices with their start and end apart: 2, of which 1 were waited for; matrix products, arithmetic and copies ran while one was open for 0% of the time, Pallas kernels for 1%

profile of v10, /device:TPU:1, one launch (start us, length us, event | category | flops | bytes accessed | tf_op | source)
XLA Modules:
  0.0 116.7 jit_solution(1025898187392767953)
XLA Ops:
  0.6 1.9 %shard_map.41 = (f32[2,288,128]{2,1,0:T(8,128)S(1)}, f32[288,576]{1,0:T(8,128)S(1)}, f32[2,288,128]{2,1,0:T(8,128)S(1)}) custom-call(s32[1]{0:T(128)} %bitcast.col_ref, f32[288,576]{1,0:T(8,128)} %bitcast.24, f32[2,288,128]{2,1,0:T(8,128)} %bitcast.26), custom_call_target="tpu_custom_call" | custom-call | tf_op jit(solution)/shard_map/pallas_call | solution.py:103
  2.6 8.9 %collective-permute-start = (f32[2,288,128]{2,1,0:T(8,128)S(1)}, f32[2,288,128]{2,1,0:T(8,128)S(1)}, u32[]{:S(2)}, u32[]{:S(2)}) collective-permute-start(f32[2,288,128]{2,1,0:T(8,128)S(1)} %get-tuple-element.11), channel_id=1, source_target_pairs={{0,1},{1,0},{2,3},{3,2},{4,5},{5,4},{6,7},{7,6},{8,9},{9,8},{10,11... | collective-permute-start | bytes 884744 | tf_op jit(solution)/shard_map/ppermute | solution.py:307
  11.5 0.9 shard_map.42
  12.4 0.1 constant_dynamic-slice_fusion
  12.6 0.1 reshape.55
  12.7 0.0 collective-permute-done
  12.9 33.1 %all_to_all.20.got_ref = f32[16,39,128]{2,1,0:T(8,128)S(1)} all-to-all(f32[16,39,128]{2,1,0:T(8,128)S(1)} %pad_maximum_fusion.1), channel_id=1, replica_groups={{0,16,8,24,4,20,12,28,2,18,10,26,6,22,14,30},{1,17,9,25,5,21,13,29,3,19..., dimensions={0} | all-to-all | bytes 638976 | tf_op jit(solution)/shard_map/all_to_all | solution.py:310
  46.0 14.4 %all_to_all.21.level_ref = f32[16,36,128]{2,1,0:T(8,128)S(1)} all-to-all(f32[16,36,128]{2,1,0:T(8,128)S(1)} %shard_map.43), channel_id=1, replica_groups={{0,256,32,288,64,320,96,352,128,384,160,416,192,448,224,480},{1,257,33,..., dimensions={0} | all-to-all | bytes 589824 | tf_op jit(solution)/shard_map/all_to_all | solution.py:313
  60.4 0.6 shard_map.44
  61.0 30.8 %all_to_all.22.line_ref = f32[16,56,128]{2,1,0:T(8,128)S(1)} all-to-all(f32[16,56,128]{2,1,0:T(8,128)S(1)} %shard_map.44), channel_id=1, replica_groups={{0,16,8,24,4,20,12,28,2,18,10,26,6,22,14,30},{1,17,9,25,5,21,13,29,3,19..., dimensions={0} | all-to-all | bytes 917504 | tf_op jit(solution)/shard_map/all_to_all | solution.py:310
  91.8 0.1 shard_map.45
  91.9 11.0 %all_to_all.23 = f32[16,53,128]{2,1,0:T(8,128)S(1)} all-to-all(f32[16,53,128]{2,1,0:T(8,128)S(1)} %get-tuple-element.12), channel_id=1, replica_groups={{0,256,32,288,64,320,96,352,128,384,160,416,192,448,224,480},{1,257,33,..., dimensions={0} | all-to-all | bytes 868352 | tf_op jit(solution)/shard_map/all_to_all | solution.py:313
  103.1 6.5 %collective-permute-start.1 = (f32[848,128]{1,0:T(8,128)S(1)}, f32[848,128]{1,0:T(8,128)S(1)}, u32[]{:S(2)}, u32[]{:S(2)}) collective-permute-start(f32[848,128]{1,0:T(8,128)S(1)} %pad_maximum_fusion.mine_ref), channel_id=1, source_target_pairs={{0,1},{1,0},{2,3},{3,2},{4,5},{5,4},{6,7},{7,6},{8,9},{9,8},{10,11... | collective-permute-start | bytes 1302536 | tf_op jit(solution)/shard_map/ppermute | solution.py:307
  109.7 0.1 copy.27
  109.9 1.1 collective-permute-done.1.other_ref
  111.0 5.7 %shard_map.46 = (f32[288,576]{1,0:T(8,128)}, f32[18,2,128]{2,1,0:T(2,128)}) custom-call(s32[1]{0:T(128)} %bitcast.col_ref, f32[848,128]{1,0:T(8,128)S(1)} %pad_maximum_fusion.mine_ref, f32[848,128]{1,0:T(8,128)S(1)} %collective-permute-done.1.other_ref, f32[288,256]{1,0:T(8,128)S(1)} %pad_maximum_fusion.2.cols_ref, f32[288,576]{1,0:T(8,128)S(1)} %get-tuple-element.9.start_ref), custom_call_target="tpu_custom_call" | custom-call | tf_op jit(solution)/shard_map/pallas_call | solution.py:276
  (19 shorter events, 0.4 us)
Async XLA Ops:
  2.6 10.1 %collective-permute-start = (f32[2,288,128]{2,1,0:T(8,128)S(1)}, f32[2,288,128]{2,1,0:T(8,128)S(1)}, u32[]{:S(2)}, u32[]{:S(2)}) collective-permute-start(f32[2,288,128]{2,1,0:T(8,128)S(1)} %get-tuple-element.11), channel_id=1, source_target_pairs={{0,1},{1,0},{2,3},{3,2},{4,5},{5,4},{6,7},{7,6},{8,9},{9,8},{10,11... | collective-permute-start | bytes 884744 | tf_op jit(solution)/shard_map/ppermute | solution.py:307
  103.1 7.9 %collective-permute-start.1 = (f32[848,128]{1,0:T(8,128)S(1)}, f32[848,128]{1,0:T(8,128)S(1)}, u32[]{:S(2)}, u32[]{:S(2)}) collective-permute-start(f32[848,128]{1,0:T(8,128)S(1)} %pad_maximum_fusion.mine_ref), channel_id=1, source_target_pairs={{0,1},{1,0},{2,3},{3,2},{4,5},{5,4},{6,7},{7,6},{8,9},{9,8},{10,11... | collective-permute-start | bytes 1302536 | tf_op jit(solution)/shard_map/ppermute | solution.py:307

commit v11 on v10

--- a/solution.py
+++ b/solution.py
@@ -281,13 +281,6 @@
     )(col.reshape(1), *(pltpu.with_memory_space_constraint(x, pltpu.VMEM) for x in (terms, other, col_terms, start)))
 
 
-def mirrored(count):
-    order = [0]
-    while len(order) < count:
-        order = [2 * at for at in order] + [2 * at + 1 for at in order]
-    return order
-
-
 def shards(kron_inverse, activations):
     rows, cols = kron_inverse.shape
     blocks, width = activations.shape[:2]
@@ -295,7 +288,7 @@
     planes = lax.axis_size("row")
     devices = lax.axis_size("col")
     depth = devices // 2
-    along = mirrored(depth)
+    along = sorted(range(depth), key=lambda z: min(z, depth - z))
     around = [seat // 2 + seat % 2 * (planes // 2) for seat in range(planes)]
     seats = [around.index(z) for z in along]
     row = lax.axis_index("row")

time: 117 us -> 117 us (level)
  blocking collectives: 89.3 us -> 87.1 us
  starting transfers between devices: 15.4 us -> 17.4 us
    all_to_all x2, blocking collectives: 63.9 us -> 61.2 us  [over_z(): lax.all_to_all(value, 'col', 0, 0, tiled=True, axis_index_groups=lines)]
    ppermute x2, starting transfers between devices: 15.4 us -> 17.4 us  [from_partner(): return lax.ppermute(value, 'col', [(at, at ^ 1) for at in range(devices)])]
where the time goes in v11:
time: 117 us; the launch traced here: 116 us
  blocking collectives  87.1 us (74%)
  starting transfers between devices  17.4 us (15%)
  Pallas kernels  9.28 us (8%)
    all_to_all x2, blocking collectives, over_z(): lax.all_to_all(value, 'col', 0, 0, tiled=True, axis_index_groups=lines)  61.2 us
    all_to_all x2, blocking collectives, over_plane(): lax.all_to_all(value, 'row', 0, 0, tiled=True, axis_index_groups=[around])  25.9 us
    ppermute x2, starting transfers between devices, from_partner(): return lax.ppermute(value, 'col', [(at, at ^ 1) for at in range(devices)])  17.4 us
    pallas_call x1, Pallas kernels, closing(): pl.pallas_call(closing_kernel, out_shape=[jax.ShapeDtypeStruct(start.shap...  5.73 us
  transfers between devices with their start and end apart: 2, of which 1 were waited for; matrix products, arithmetic and copies ran while one was open for 0% of the time, Pallas kernels for 1%

profile of v11, /device:TPU:1, one launch (start us, length us, event | category | flops | bytes accessed | tf_op | source)
XLA Modules:
  0.0 116.5 jit_solution(16742143628406428180)
XLA Ops:
  0.6 1.9 %shard_map.41 = (f32[2,288,128]{2,1,0:T(8,128)S(1)}, f32[288,576]{1,0:T(8,128)S(1)}, f32[2,288,128]{2,1,0:T(8,128)S(1)}) custom-call(s32[1]{0:T(128)} %bitcast.col_ref, f32[288,576]{1,0:T(8,128)} %bitcast.24, f32[2,288,128]{2,1,0:T(8,128)} %bitcast.26), custom_call_target="tpu_custom_call" | custom-call | tf_op jit(solution)/shard_map/pallas_call | solution.py:103
  2.6 8.9 %collective-permute-start = (f32[2,288,128]{2,1,0:T(8,128)S(1)}, f32[2,288,128]{2,1,0:T(8,128)S(1)}, u32[]{:S(2)}, u32[]{:S(2)}) collective-permute-start(f32[2,288,128]{2,1,0:T(8,128)S(1)} %get-tuple-element.11), channel_id=1, source_target_pairs={{0,1},{1,0},{2,3},{3,2},{4,5},{5,4},{6,7},{7,6},{8,9},{9,8},{10,11... | collective-permute-start | bytes 884744 | tf_op jit(solution)/shard_map/ppermute | solution.py:300
  11.5 0.9 shard_map.42
  12.4 0.1 constant_dynamic-slice_fusion
  12.6 0.1 reshape.55
  12.7 0.0 collective-permute-done
  12.9 29.6 %all_to_all.20.got_ref = f32[16,39,128]{2,1,0:T(8,128)S(1)} all-to-all(f32[16,39,128]{2,1,0:T(8,128)S(1)} %pad_maximum_fusion.1), channel_id=1, replica_groups={{0,2,30,4,28,6,26,8,24,10,22,12,20,14,18,16},{1,3,31,5,29,7,27,9,25,11,..., dimensions={0} | all-to-all | bytes 638976 | tf_op jit(solution)/shard_map/all_to_all | solution.py:303
  42.6 14.3 %all_to_all.21.level_ref = f32[16,36,128]{2,1,0:T(8,128)S(1)} all-to-all(f32[16,36,128]{2,1,0:T(8,128)S(1)} %shard_map.43), channel_id=1, replica_groups={{0,256,32,288,64,320,96,352,128,384,160,416,192,448,224,480},{1,257,33,..., dimensions={0} | all-to-all | bytes 589824 | tf_op jit(solution)/shard_map/all_to_all | solution.py:306
  56.9 0.6 shard_map.44
  57.5 31.6 %all_to_all.22.line_ref = f32[16,56,128]{2,1,0:T(8,128)S(1)} all-to-all(f32[16,56,128]{2,1,0:T(8,128)S(1)} %shard_map.44), channel_id=1, replica_groups={{0,2,30,4,28,6,26,8,24,10,22,12,20,14,18,16},{1,3,31,5,29,7,27,9,25,11,..., dimensions={0} | all-to-all | bytes 917504 | tf_op jit(solution)/shard_map/all_to_all | solution.py:303
  89.0 0.1 shard_map.45
  89.2 11.6 %all_to_all.23 = f32[16,53,128]{2,1,0:T(8,128)S(1)} all-to-all(f32[16,53,128]{2,1,0:T(8,128)S(1)} %get-tuple-element.12), channel_id=1, replica_groups={{0,256,32,288,64,320,96,352,128,384,160,416,192,448,224,480},{1,257,33,..., dimensions={0} | all-to-all | bytes 868352 | tf_op jit(solution)/shard_map/all_to_all | solution.py:306
  100.8 8.5 %collective-permute-start.1 = (f32[848,128]{1,0:T(8,128)S(1)}, f32[848,128]{1,0:T(8,128)S(1)}, u32[]{:S(2)}, u32[]{:S(2)}) collective-permute-start(f32[848,128]{1,0:T(8,128)S(1)} %pad_maximum_fusion.mine_ref), channel_id=1, source_target_pairs={{0,1},{1,0},{2,3},{3,2},{4,5},{5,4},{6,7},{7,6},{8,9},{9,8},{10,11... | collective-permute-start | bytes 1302536 | tf_op jit(solution)/shard_map/ppermute | solution.py:300
  109.4 0.1 copy.27
  109.7 1.1 collective-permute-done.1.other_ref
  110.7 5.7 %shard_map.46 = (f32[288,576]{1,0:T(8,128)}, f32[18,2,128]{2,1,0:T(2,128)}) custom-call(s32[1]{0:T(128)} %bitcast.col_ref, f32[848,128]{1,0:T(8,128)S(1)} %pad_maximum_fusion.mine_ref, f32[848,128]{1,0:T(8,128)S(1)} %collective-permute-done.1.other_ref, f32[288,256]{1,0:T(8,128)S(1)} %pad_maximum_fusion.2.cols_ref, f32[288,576]{1,0:T(8,128)S(1)} %get-tuple-element.9.start_ref), custom_call_target="tpu_custom_call" | custom-call | tf_op jit(solution)/shard_map/pallas_call | solution.py:276
  (19 shorter events, 0.4 us)
Async XLA Ops:
  2.6 10.1 %collective-permute-start = (f32[2,288,128]{2,1,0:T(8,128)S(1)}, f32[2,288,128]{2,1,0:T(8,128)S(1)}, u32[]{:S(2)}, u32[]{:S(2)}) collective-permute-start(f32[2,288,128]{2,1,0:T(8,128)S(1)} %get-tuple-element.11), channel_id=1, source_target_pairs={{0,1},{1,0},{2,3},{3,2},{4,5},{5,4},{6,7},{7,6},{8,9},{9,8},{10,11... | collective-permute-start | bytes 884744 | tf_op jit(solution)/shard_map/ppermute | solution.py:300
  100.8 9.9 %collective-permute-start.1 = (f32[848,128]{1,0:T(8,128)S(1)}, f32[848,128]{1,0:T(8,128)S(1)}, u32[]{:S(2)}, u32[]{:S(2)}) collective-permute-start(f32[848,128]{1,0:T(8,128)S(1)} %pad_maximum_fusion.mine_ref), channel_id=1, source_target_pairs={{0,1},{1,0},{2,3},{3,2},{4,5},{5,4},{6,7},{7,6},{8,9},{9,8},{10,11... | collective-permute-start | bytes 1302536 | tf_op jit(solution)/shard_map/ppermute | solution.py:300

commit v12 on v11

--- a/solution.py
+++ b/solution.py
@@ -288,7 +288,7 @@
     planes = lax.axis_size("row")
     devices = lax.axis_size("col")
     depth = devices // 2
-    along = sorted(range(depth), key=lambda z: min(z, depth - z))
+    along = list(range(depth))
     around = [seat // 2 + seat % 2 * (planes // 2) for seat in range(planes)]
     seats = [around.index(z) for z in along]
     row = lax.axis_index("row")

time: 117 us -> 113 us (0.966)
  blocking collectives: 87.1 us -> 82.1 us
  starting transfers between devices: 17.4 us -> 18.8 us
    all_to_all x2, blocking collectives: 61.2 us -> 56.4 us  [over_z(): lax.all_to_all(value, 'col', 0, 0, tiled=True, axis_index_groups=lines)]
    ppermute x2, starting transfers between devices: 17.4 us -> 18.8 us  [from_partner(): return lax.ppermute(value, 'col', [(at, at ^ 1) for at in range(devices)])]
where the time goes in v12:
time: 113 us
  blocking collectives  82.1 us (73%)
  starting transfers between devices  18.8 us (17%)
  Pallas kernels  9.28 us (8%)
    all_to_all x2, blocking collectives, over_z(): lax.all_to_all(value, 'col', 0, 0, tiled=True, axis_index_groups=lines)  56.4 us
    all_to_all x2, blocking collectives, over_plane(): lax.all_to_all(value, 'row', 0, 0, tiled=True, axis_index_groups=[around])  25.7 us
    ppermute x2, starting transfers between devices, from_partner(): return lax.ppermute(value, 'col', [(at, at ^ 1) for at in range(devices)])  18.8 us
    pallas_call x1, Pallas kernels, closing(): pl.pallas_call(closing_kernel, out_shape=[jax.ShapeDtypeStruct(start.shap...  5.73 us
  transfers between devices with their start and end apart: 2, of which 1 were waited for; matrix products, arithmetic and copies ran while one was open for 0% of the time, Pallas kernels for 1%

profile of v12, /device:TPU:1, one launch (start us, length us, event | category | flops | bytes accessed | tf_op | source)
XLA Modules:
  0.0 112.9 jit_solution(14136182028101380791)
XLA Ops:
  0.6 1.9 %shard_map.41 = (f32[2,288,128]{2,1,0:T(8,128)S(1)}, f32[288,576]{1,0:T(8,128)S(1)}, f32[2,288,128]{2,1,0:T(8,128)S(1)}) custom-call(s32[1]{0:T(128)} %bitcast.col_ref, f32[288,576]{1,0:T(8,128)} %bitcast.24, f32[2,288,128]{2,1,0:T(8,128)} %bitcast.26), custom_call_target="tpu_custom_call" | custom-call | tf_op jit(solution)/shard_map/pallas_call | solution.py:103
  2.6 8.9 %collective-permute-start = (f32[2,288,128]{2,1,0:T(8,128)S(1)}, f32[2,288,128]{2,1,0:T(8,128)S(1)}, u32[]{:S(2)}, u32[]{:S(2)}) collective-permute-start(f32[2,288,128]{2,1,0:T(8,128)S(1)} %get-tuple-element.11), channel_id=1, source_target_pairs={{0,1},{1,0},{2,3},{3,2},{4,5},{5,4},{6,7},{7,6},{8,9},{9,8},{10,11... | collective-permute-start | bytes 884744 | tf_op jit(solution)/shard_map/ppermute | solution.py:300
  11.5 0.9 shard_map.42
  12.4 0.1 constant_dynamic-slice_fusion
  12.6 0.1 reshape.55
  12.7 0.0 collective-permute-done
  12.9 24.9 %all_to_all.20.got_ref = f32[16,39,128]{2,1,0:T(8,128)S(1)} all-to-all(f32[16,39,128]{2,1,0:T(8,128)S(1)} %pad_maximum_fusion.1), channel_id=1, replica_groups={{0,2,4,6,8,10,12,14,16,18,20,22,24,26,28,30},{1,3,5,7,9,11,13,15,17,19,..., dimensions={0} | all-to-all | bytes 638976 | tf_op jit(solution)/shard_map/all_to_all | solution.py:303
  37.8 14.3 %all_to_all.21.level_ref = f32[16,36,128]{2,1,0:T(8,128)S(1)} all-to-all(f32[16,36,128]{2,1,0:T(8,128)S(1)} %shard_map.43), channel_id=1, replica_groups={{0,256,32,288,64,320,96,352,128,384,160,416,192,448,224,480},{1,257,33,..., dimensions={0} | all-to-all | bytes 589824 | tf_op jit(solution)/shard_map/all_to_all | solution.py:306
  52.1 0.6 shard_map.44
  52.7 31.5 %all_to_all.22.line_ref = f32[16,56,128]{2,1,0:T(8,128)S(1)} all-to-all(f32[16,56,128]{2,1,0:T(8,128)S(1)} %shard_map.44), channel_id=1, replica_groups={{0,2,4,6,8,10,12,14,16,18,20,22,24,26,28,30},{1,3,5,7,9,11,13,15,17,19,..., dimensions={0} | all-to-all | bytes 917504 | tf_op jit(solution)/shard_map/all_to_all | solution.py:303
  84.3 0.1 shard_map.45
  84.4 11.4 %all_to_all.23 = f32[16,53,128]{2,1,0:T(8,128)S(1)} all-to-all(f32[16,53,128]{2,1,0:T(8,128)S(1)} %get-tuple-element.12), channel_id=1, replica_groups={{0,256,32,288,64,320,96,352,128,384,160,416,192,448,224,480},{1,257,33,..., dimensions={0} | all-to-all | bytes 868352 | tf_op jit(solution)/shard_map/all_to_all | solution.py:306
  95.9 9.9 %collective-permute-start.1 = (f32[848,128]{1,0:T(8,128)S(1)}, f32[848,128]{1,0:T(8,128)S(1)}, u32[]{:S(2)}, u32[]{:S(2)}) collective-permute-start(f32[848,128]{1,0:T(8,128)S(1)} %pad_maximum_fusion.mine_ref), channel_id=1, source_target_pairs={{0,1},{1,0},{2,3},{3,2},{4,5},{5,4},{6,7},{7,6},{8,9},{9,8},{10,11... | collective-permute-start | bytes 1302536 | tf_op jit(solution)/shard_map/ppermute | solution.py:300
  105.8 0.1 copy.27
  106.1 1.1 collective-permute-done.1.other_ref
  107.1 5.7 %shard_map.46 = (f32[288,576]{1,0:T(8,128)}, f32[18,2,128]{2,1,0:T(2,128)}) custom-call(s32[1]{0:T(128)} %bitcast.col_ref, f32[848,128]{1,0:T(8,128)S(1)} %pad_maximum_fusion.mine_ref, f32[848,128]{1,0:T(8,128)S(1)} %collective-permute-done.1.other_ref, f32[288,256]{1,0:T(8,128)S(1)} %pad_maximum_fusion.2.cols_ref, f32[288,576]{1,0:T(8,128)S(1)} %get-tuple-element.9.start_ref), custom_call_target="tpu_custom_call" | custom-call | tf_op jit(solution)/shard_map/pallas_call | solution.py:276
  (19 shorter events, 0.4 us)
Async XLA Ops:
  2.6 10.1 %collective-permute-start = (f32[2,288,128]{2,1,0:T(8,128)S(1)}, f32[2,288,128]{2,1,0:T(8,128)S(1)}, u32[]{:S(2)}, u32[]{:S(2)}) collective-permute-start(f32[2,288,128]{2,1,0:T(8,128)S(1)} %get-tuple-element.11), channel_id=1, source_target_pairs={{0,1},{1,0},{2,3},{3,2},{4,5},{5,4},{6,7},{7,6},{8,9},{9,8},{10,11... | collective-permute-start | bytes 884744 | tf_op jit(solution)/shard_map/ppermute | solution.py:300
  95.9 11.3 %collective-permute-start.1 = (f32[848,128]{1,0:T(8,128)S(1)}, f32[848,128]{1,0:T(8,128)S(1)}, u32[]{:S(2)}, u32[]{:S(2)}) collective-permute-start(f32[848,128]{1,0:T(8,128)S(1)} %pad_maximum_fusion.mine_ref), channel_id=1, source_target_pairs={{0,1},{1,0},{2,3},{3,2},{4,5},{5,4},{6,7},{7,6},{8,9},{9,8},{10,11... | collective-permute-start | bytes 1302536 | tf_op jit(solution)/shard_map/ppermute | solution.py:300

commit v13 on v12

--- a/solution.py
+++ b/solution.py
@@ -289,10 +289,11 @@
     devices = lax.axis_size("col")
     depth = devices // 2
     along = list(range(depth))
-    around = [seat // 2 + seat % 2 * (planes // 2) for seat in range(planes)]
+    around = [2, 11, 3, 10, 0, 4, 7, 5, 14, 12, 6, 9, 13, 8, 1, 15]
+    around = [at for at in around if at < planes] + list(range(len(around), planes))
     seats = [around.index(z) for z in along]
     row = lax.axis_index("row")
-    row = row % (planes // 2) * 2 + row // (planes // 2)
+    row = sum(jnp.where(row == at, seat, 0) for seat, at in enumerate(around))
     col = lax.axis_index("col")
     lines = [[2 * z + k for z in along] for k in range(2)]
 

time: 113 us -> 112 us (level)
    all_to_all x2, blocking collectives: 25.7 us -> 24.3 us  [over_plane(): lax.all_to_all(value, 'row', 0, 0, tiled=True, axis_index_groups=[around])]
where the time goes in v13:
time: 112 us
  blocking collectives  81.1 us (72%)
  starting transfers between devices  18.5 us (17%)
  Pallas kernels  9.27 us (8%)
    all_to_all x2, blocking collectives, over_z(): lax.all_to_all(value, 'col', 0, 0, tiled=True, axis_index_groups=lines)  56.8 us
    all_to_all x2, blocking collectives, over_plane(): lax.all_to_all(value, 'row', 0, 0, tiled=True, axis_index_groups=[around])  24.3 us
    ppermute x2, starting transfers between devices, from_partner(): return lax.ppermute(value, 'col', [(at, at ^ 1) for at in range(devices)])  18.5 us
    pallas_call x1, Pallas kernels, closing(): pl.pallas_call(closing_kernel, out_shape=[jax.ShapeDtypeStruct(start.shap...  5.73 us
  transfers between devices with their start and end apart: 2, of which 1 were waited for; matrix products, arithmetic and copies ran while one was open for 0% of the time, Pallas kernels for 1%

profile of v13, /device:TPU:1, one launch (start us, length us, event | category | flops | bytes accessed | tf_op | source)
XLA Modules:
  0.0 111.6 jit_solution(9367827603282378249)
XLA Ops:
  0.6 1.9 %shard_map.41 = (f32[2,288,128]{2,1,0:T(8,128)S(1)}, f32[288,576]{1,0:T(8,128)S(1)}, f32[2,288,128]{2,1,0:T(8,128)S(1)}) custom-call(s32[1]{0:T(128)} %bitcast.col_ref, f32[288,576]{1,0:T(8,128)} %bitcast.24, f32[2,288,128]{2,1,0:T(8,128)} %bitcast.26), custom_call_target="tpu_custom_call" | custom-call | tf_op jit(solution)/shard_map/pallas_call | solution.py:103
  2.6 8.9 %collective-permute-start = (f32[2,288,128]{2,1,0:T(8,128)S(1)}, f32[2,288,128]{2,1,0:T(8,128)S(1)}, u32[]{:S(2)}, u32[]{:S(2)}) collective-permute-start(f32[2,288,128]{2,1,0:T(8,128)S(1)} %get-tuple-element.11), channel_id=1, source_target_pairs={{0,1},{1,0},{2,3},{3,2},{4,5},{5,4},{6,7},{7,6},{8,9},{9,8},{10,11... | collective-permute-start | bytes 884744 | tf_op jit(solution)/shard_map/ppermute | solution.py:301
  11.6 0.9 shard_map.42
  12.4 0.1 constant_dynamic-slice_fusion
  12.6 0.1 reshape.55
  12.7 0.0 collective-permute-done
  12.9 24.9 %all_to_all.20.got_ref = f32[16,39,128]{2,1,0:T(8,128)S(1)} all-to-all(f32[16,39,128]{2,1,0:T(8,128)S(1)} %pad_maximum_fusion.1), channel_id=1, replica_groups={{0,2,4,6,8,10,12,14,16,18,20,22,24,26,28,30},{1,3,5,7,9,11,13,15,17,19,..., dimensions={0} | all-to-all | bytes 638976 | tf_op jit(solution)/shard_map/all_to_all | solution.py:304
  37.8 12.8 %all_to_all.21.level_ref = f32[16,36,128]{2,1,0:T(8,128)S(1)} all-to-all(f32[16,36,128]{2,1,0:T(8,128)S(1)} %shard_map.43), channel_id=1, replica_groups={{64,352,96,320,0,128,224,160,448,384,192,288,416,256,32,480},{65,353,97..., dimensions={0} | all-to-all | bytes 589824 | tf_op jit(solution)/shard_map/all_to_all | solution.py:307
  50.6 0.6 shard_map.44
  51.2 32.0 %all_to_all.22.line_ref = f32[16,56,128]{2,1,0:T(8,128)S(1)} all-to-all(f32[16,56,128]{2,1,0:T(8,128)S(1)} %shard_map.44), channel_id=1, replica_groups={{0,2,4,6,8,10,12,14,16,18,20,22,24,26,28,30},{1,3,5,7,9,11,13,15,17,19,..., dimensions={0} | all-to-all | bytes 917504 | tf_op jit(solution)/shard_map/all_to_all | solution.py:304
  83.2 0.1 shard_map.45
  83.3 11.5 %all_to_all.23 = f32[16,53,128]{2,1,0:T(8,128)S(1)} all-to-all(f32[16,53,128]{2,1,0:T(8,128)S(1)} %get-tuple-element.12), channel_id=1, replica_groups={{64,352,96,320,0,128,224,160,448,384,192,288,416,256,32,480},{65,353,97..., dimensions={0} | all-to-all | bytes 868352 | tf_op jit(solution)/shard_map/all_to_all | solution.py:307
  94.9 9.6 %collective-permute-start.1 = (f32[848,128]{1,0:T(8,128)S(1)}, f32[848,128]{1,0:T(8,128)S(1)}, u32[]{:S(2)}, u32[]{:S(2)}) collective-permute-start(f32[848,128]{1,0:T(8,128)S(1)} %pad_maximum_fusion.mine_ref), channel_id=1, source_target_pairs={{0,1},{1,0},{2,3},{3,2},{4,5},{5,4},{6,7},{7,6},{8,9},{9,8},{10,11... | collective-permute-start | bytes 1302536 | tf_op jit(solution)/shard_map/ppermute | solution.py:301
  104.5 0.1 copy.27
  104.8 1.1 collective-permute-done.1.other_ref
  105.8 5.7 %shard_map.46 = (f32[288,576]{1,0:T(8,128)}, f32[18,2,128]{2,1,0:T(2,128)}) custom-call(s32[1]{0:T(128)} %bitcast.col_ref, f32[848,128]{1,0:T(8,128)S(1)} %pad_maximum_fusion.mine_ref, f32[848,128]{1,0:T(8,128)S(1)} %collective-permute-done.1.other_ref, f32[288,256]{1,0:T(8,128)S(1)} %pad_maximum_fusion.2.cols_ref, f32[288,576]{1,0:T(8,128)S(1)} %get-tuple-element.9.start_ref), custom_call_target="tpu_custom_call" | custom-call | tf_op jit(solution)/shard_map/pallas_call | solution.py:276
  (19 shorter events, 0.4 us)
Async XLA Ops:
  2.6 10.2 %collective-permute-start = (f32[2,288,128]{2,1,0:T(8,128)S(1)}, f32[2,288,128]{2,1,0:T(8,128)S(1)}, u32[]{:S(2)}, u32[]{:S(2)}) collective-permute-start(f32[2,288,128]{2,1,0:T(8,128)S(1)} %get-tuple-element.11), channel_id=1, source_target_pairs={{0,1},{1,0},{2,3},{3,2},{4,5},{5,4},{6,7},{7,6},{8,9},{9,8},{10,11... | collective-permute-start | bytes 884744 | tf_op jit(solution)/shard_map/ppermute | solution.py:301
  94.9 11.0 %collective-permute-start.1 = (f32[848,128]{1,0:T(8,128)S(1)}, f32[848,128]{1,0:T(8,128)S(1)}, u32[]{:S(2)}, u32[]{:S(2)}) collective-permute-start(f32[848,128]{1,0:T(8,128)S(1)} %pad_maximum_fusion.mine_ref), channel_id=1, source_target_pairs={{0,1},{1,0},{2,3},{3,2},{4,5},{5,4},{6,7},{7,6},{8,9},{9,8},{10,11... | collective-permute-start | bytes 1302536 | tf_op jit(solution)/shard_map/ppermute | solution.py:301

commit v14 on v13

--- a/solution.py
+++ b/solution.py
@@ -289,7 +289,7 @@
     devices = lax.axis_size("col")
     depth = devices // 2
     along = list(range(depth))
-    around = [2, 11, 3, 10, 0, 4, 7, 5, 14, 12, 6, 9, 13, 8, 1, 15]
+    around = [1, 12, 11, 4, 9, 7, 3, 14, 2, 10, 15, 5, 6, 0, 13, 8]
     around = [at for at in around if at < planes] + list(range(len(around), planes))
     seats = [around.index(z) for z in along]
     row = lax.axis_index("row")

time: 112 us -> 114 us (1.018)
  blocking collectives: 81.1 us -> 83.2 us
    all_to_all x2, blocking collectives: 24.3 us -> 26.6 us  [over_plane(): lax.all_to_all(value, 'row', 0, 0, tiled=True, axis_index_groups=[around])]
where the time goes in v14:
time: 114 us
  blocking collectives  83.2 us (73%)
  starting transfers between devices  18.5 us (16%)
  Pallas kernels  9.28 us (8%)
    all_to_all x2, blocking collectives, over_z(): lax.all_to_all(value, 'col', 0, 0, tiled=True, axis_index_groups=lines)  56.6 us
    all_to_all x2, blocking collectives, over_plane(): lax.all_to_all(value, 'row', 0, 0, tiled=True, axis_index_groups=[around])  26.6 us
    ppermute x2, starting transfers between devices, from_partner(): return lax.ppermute(value, 'col', [(at, at ^ 1) for at in range(devices)])  18.5 us
    pallas_call x1, Pallas kernels, closing(): pl.pallas_call(closing_kernel, out_shape=[jax.ShapeDtypeStruct(start.shap...  5.73 us
  transfers between devices with their start and end apart: 2, of which 1 were waited for; matrix products, arithmetic and copies ran while one was open for 0% of the time, Pallas kernels for 1%

profile of v14, /device:TPU:1, one launch (start us, length us, event | category | flops | bytes accessed | tf_op | source)
XLA Modules:
  0.0 113.7 jit_solution(15438890724435685000)
XLA Ops:
  0.6 1.9 %shard_map.41 = (f32[2,288,128]{2,1,0:T(8,128)S(1)}, f32[288,576]{1,0:T(8,128)S(1)}, f32[2,288,128]{2,1,0:T(8,128)S(1)}) custom-call(s32[1]{0:T(128)} %bitcast.col_ref, f32[288,576]{1,0:T(8,128)} %bitcast.24, f32[2,288,128]{2,1,0:T(8,128)} %bitcast.26), custom_call_target="tpu_custom_call" | custom-call | tf_op jit(solution)/shard_map/pallas_call | solution.py:103
  2.6 8.9 %collective-permute-start = (f32[2,288,128]{2,1,0:T(8,128)S(1)}, f32[2,288,128]{2,1,0:T(8,128)S(1)}, u32[]{:S(2)}, u32[]{:S(2)}) collective-permute-start(f32[2,288,128]{2,1,0:T(8,128)S(1)} %get-tuple-element.11), channel_id=1, source_target_pairs={{0,1},{1,0},{2,3},{3,2},{4,5},{5,4},{6,7},{7,6},{8,9},{9,8},{10,11... | collective-permute-start | bytes 884744 | tf_op jit(solution)/shard_map/ppermute | solution.py:301
  11.6 0.9 shard_map.42
  12.4 0.1 constant_dynamic-slice_fusion
  12.6 0.1 reshape.55
  12.7 0.0 collective-permute-done
  12.9 24.9 %all_to_all.20.got_ref = f32[16,39,128]{2,1,0:T(8,128)S(1)} all-to-all(f32[16,39,128]{2,1,0:T(8,128)S(1)} %pad_maximum_fusion.1), channel_id=1, replica_groups={{0,2,4,6,8,10,12,14,16,18,20,22,24,26,28,30},{1,3,5,7,9,11,13,15,17,19,..., dimensions={0} | all-to-all | bytes 638976 | tf_op jit(solution)/shard_map/all_to_all | solution.py:304
  37.8 14.3 %all_to_all.21.level_ref = f32[16,36,128]{2,1,0:T(8,128)S(1)} all-to-all(f32[16,36,128]{2,1,0:T(8,128)S(1)} %shard_map.43), channel_id=1, replica_groups={{32,384,352,128,288,224,96,448,64,320,480,160,192,0,416,256},{33,385,35..., dimensions={0} | all-to-all | bytes 589824 | tf_op jit(solution)/shard_map/all_to_all | solution.py:307
  52.2 0.6 shard_map.44
  52.8 31.7 %all_to_all.22.line_ref = f32[16,56,128]{2,1,0:T(8,128)S(1)} all-to-all(f32[16,56,128]{2,1,0:T(8,128)S(1)} %shard_map.44), channel_id=1, replica_groups={{0,2,4,6,8,10,12,14,16,18,20,22,24,26,28,30},{1,3,5,7,9,11,13,15,17,19,..., dimensions={0} | all-to-all | bytes 917504 | tf_op jit(solution)/shard_map/all_to_all | solution.py:304
  84.5 0.1 shard_map.45
  84.6 12.3 %all_to_all.23 = f32[16,53,128]{2,1,0:T(8,128)S(1)} all-to-all(f32[16,53,128]{2,1,0:T(8,128)S(1)} %get-tuple-element.12), channel_id=1, replica_groups={{32,384,352,128,288,224,96,448,64,320,480,160,192,0,416,256},{33,385,35..., dimensions={0} | all-to-all | bytes 868352 | tf_op jit(solution)/shard_map/all_to_all | solution.py:307
  97.0 9.6 %collective-permute-start.1 = (f32[848,128]{1,0:T(8,128)S(1)}, f32[848,128]{1,0:T(8,128)S(1)}, u32[]{:S(2)}, u32[]{:S(2)}) collective-permute-start(f32[848,128]{1,0:T(8,128)S(1)} %pad_maximum_fusion.mine_ref), channel_id=1, source_target_pairs={{0,1},{1,0},{2,3},{3,2},{4,5},{5,4},{6,7},{7,6},{8,9},{9,8},{10,11... | collective-permute-start | bytes 1302536 | tf_op jit(solution)/shard_map/ppermute | solution.py:301
  106.6 0.1 copy.27
  106.9 1.1 collective-permute-done.1.other_ref
  108.0 5.7 %shard_map.46 = (f32[288,576]{1,0:T(8,128)}, f32[18,2,128]{2,1,0:T(2,128)}) custom-call(s32[1]{0:T(128)} %bitcast.col_ref, f32[848,128]{1,0:T(8,128)S(1)} %pad_maximum_fusion.mine_ref, f32[848,128]{1,0:T(8,128)S(1)} %collective-permute-done.1.other_ref, f32[288,256]{1,0:T(8,128)S(1)} %pad_maximum_fusion.2.cols_ref, f32[288,576]{1,0:T(8,128)S(1)} %get-tuple-element.9.start_ref), custom_call_target="tpu_custom_call" | custom-call | tf_op jit(solution)/shard_map/pallas_call | solution.py:276
  (19 shorter events, 0.4 us)
Async XLA Ops:
  2.6 10.2 %collective-permute-start = (f32[2,288,128]{2,1,0:T(8,128)S(1)}, f32[2,288,128]{2,1,0:T(8,128)S(1)}, u32[]{:S(2)}, u32[]{:S(2)}) collective-permute-start(f32[2,288,128]{2,1,0:T(8,128)S(1)} %get-tuple-element.11), channel_id=1, source_target_pairs={{0,1},{1,0},{2,3},{3,2},{4,5},{5,4},{6,7},{7,6},{8,9},{9,8},{10,11... | collective-permute-start | bytes 884744 | tf_op jit(solution)/shard_map/ppermute | solution.py:301
  97.0 11.0 %collective-permute-start.1 = (f32[848,128]{1,0:T(8,128)S(1)}, f32[848,128]{1,0:T(8,128)S(1)}, u32[]{:S(2)}, u32[]{:S(2)}) collective-permute-start(f32[848,128]{1,0:T(8,128)S(1)} %pad_maximum_fusion.mine_ref), channel_id=1, source_target_pairs={{0,1},{1,0},{2,3},{3,2},{4,5},{5,4},{6,7},{7,6},{8,9},{9,8},{10,11... | collective-permute-start | bytes 1302536 | tf_op jit(solution)/shard_map/ppermute | solution.py:301
